TPU v7x, 32 devices: a whole 2x2x4 slice. The times are simulated.
32 devices in a mesh: dp: 4 (over x, core), ctx: 8 (over z, y).
Axes of the slice: x: 2, y: 2, z: 4, core: 2. Of those that a mesh axis runs over, the one named last changes fastest.
Arguments:
- tokens: bfloat16 [16384, 1152], P(('dp', 'ctx')), may hold values from -6 to 6
- attention_gain: bfloat16 [1152], P(('dp', 'ctx')), may hold values from 0.099609375 to 1.8984375
- query_weight: bfloat16 [1152, 1024], P(('dp', 'ctx')), may hold values from -0.1875 to 0.1875
- key_weight: bfloat16 [1152, 256], P(('dp', 'ctx')), may hold values from -0.1875 to 0.1875
- value_weight: bfloat16 [1152, 256], P(('dp', 'ctx')), may hold values from -0.1875 to 0.1875
- query_gain: bfloat16 [256], P(('dp', 'ctx')), may hold values from 1 to 2
- key_gain: bfloat16 [256], P(('dp', 'ctx')), may hold values from 1 to 2
- output_weight: bfloat16 [1024, 1152], P(('dp', 'ctx')), may hold values from -0.1875 to 0.1875
- mixed_gain: bfloat16 [1152], P(('dp', 'ctx')), may hold values from 0.099609375 to 1.8984375
- feed_gain: bfloat16 [1152], P(('dp', 'ctx')), may hold values from 0.099609375 to 1.8984375
- gate_weight: bfloat16 [1152, 6912], P(('dp', 'ctx')), may hold values from -0.1875 to 0.1875
- up_weight: bfloat16 [1152, 6912], P(('dp', 'ctx')), may hold values from -0.1875 to 0.1875
- down_weight: bfloat16 [6912, 1152], P(('dp', 'ctx')), may hold values from -0.078125 to 0.078125
- final_gain: bfloat16 [1152], P(('dp', 'ctx')), may hold values from 0.099609375 to 1.8984375
- segment_ids: int32 [16384], P('dp'), may hold values from 0 to 4, as said below
- positions: int32 [16384], P('dp'), may hold values from 0 to 2559, as said below
- cotangent: bfloat16 [16384, 1152], P(('dp', 'ctx')), may hold values from -6 to 6
Outputs:
- layer_out: bfloat16 [16384, 1152], P(('dp', 'ctx'))
- tokens_grad: bfloat16 [16384, 1152], P(('dp', 'ctx'))
- attention_gain_grad: float32 [1152], P(('dp', 'ctx'))
- query_weight_grad: float32 [1152, 1024], P(('dp', 'ctx'))
- key_weight_grad: float32 [1152, 256], P(('dp', 'ctx'))
- value_weight_grad: float32 [1152, 256], P(('dp', 'ctx'))
- query_gain_grad: float32 [256], P(('dp', 'ctx'))
- key_gain_grad: float32 [256], P(('dp', 'ctx'))
- output_weight_grad: float32 [1024, 1152], P(('dp', 'ctx'))
- mixed_gain_grad: float32 [1152], P(('dp', 'ctx'))
- feed_gain_grad: float32 [1152], P(('dp', 'ctx'))
- gate_weight_grad: float32 [1152, 6912], P(('dp', 'ctx'))
- up_weight_grad: float32 [1152, 6912], P(('dp', 'ctx'))
- down_weight_grad: float32 [6912, 1152], P(('dp', 'ctx'))
- final_gain_grad: float32 [1152], P(('dp', 'ctx'))
Inputs may be any that keep to these rules, and one draw needn't show every extreme that they name: `segment_ids`: each group's tokens form aligned blocks of 512. 2048 / 512 blocks, at places drawn from the seed, hold the prompt, segment id 0; each other block is one whole continuation, with its own id, and each id of 1 to 4 occurs in every group. `positions`: A prompt token's position is its place in the prompt, each of 0 to 2047 once a group; a continuation's token has 2048 plus its place in the continuation.
All inputs are finite; a program needn't handle non-finite values.
Results may differ from a plain program's by a relative error of at most 0.035.
Values may be sent and summed in bfloat16 or wider, within the bound.
A program may use at most 384 MiB of HBM per device.

v0:
```python
import jax
import jax.numpy as jnp
from jax import lax
from jax.sharding import PartitionSpec as P

FF = 6912
HQ = 4
HD = 256


EPSILON = 1e-06
THETA = 1000000.0


def block_width():
    return 1024


def rms_factor(values):
    return lax.rsqrt(jnp.mean(values * values, axis=-1, keepdims=True) + EPSILON)


def norm_back(incoming, values, factor, gain):
    scaled = incoming * gain
    gain_term = jnp.sum((incoming * values * factor).reshape(-1, values.shape[-1]), axis=0)
    inner = jnp.mean(scaled * values, axis=-1, keepdims=True)
    return (factor * scaled - values * (factor * factor * factor) * inner, gain_term)


def angles_of(position_ids):
    half_width = HD // 2
    inverse = THETA ** (-(jnp.arange(half_width, dtype=jnp.float32) * 2.0) / HD)
    angle = position_ids.astype(jnp.float32)[:, None] * inverse[None, :]
    return (jnp.cos(angle), jnp.sin(angle))


def rotate(values, cosine, sine):
    half_width = values.shape[-1] // 2
    first_half = values[..., :half_width]
    second_half = values[..., half_width:]
    return jnp.concatenate(
        [first_half * cosine - second_half * sine, second_half * cosine + first_half * sine],
        axis=-1,
    )


def visible(query_pos, query_seg, key_pos, key_seg):
    return (key_pos[None, :] <= query_pos[:, None]) & (
        (key_seg[None, :] == 0) | (key_seg[None, :] == query_seg[:, None])
    )


def body(
    tokens,
    attention_gain,
    query_weight,
    key_weight,
    value_weight,
    query_gain,
    key_gain,
    output_weight,
    mixed_gain,
    feed_gain,
    gate_weight,
    up_weight,
    down_weight,
    final_gain,
    segment_ids,
    positions,
    cotangent,
):
    local = tokens.shape[0]
    heads_rows = HQ * local
    scale = HD ** (-0.5)
    offset = lax.axis_index("ctx") * local
    query_pos = lax.dynamic_slice_in_dim(positions, offset, local)
    query_seg = lax.dynamic_slice_in_dim(segment_ids, offset, local)
    gain_one, query_full, key_full, value_full, query_scale, key_scale, output_full, mixed_scale = (
        lax.all_gather(attention_gain, ("dp", "ctx"), axis=0, tiled=True),
        lax.all_gather(query_weight, ("dp", "ctx"), axis=0, tiled=True),
        lax.all_gather(key_weight, ("dp", "ctx"), axis=0, tiled=True),
        lax.all_gather(value_weight, ("dp", "ctx"), axis=0, tiled=True),
        lax.all_gather(query_gain, ("dp", "ctx"), axis=0, tiled=True),
        lax.all_gather(key_gain, ("dp", "ctx"), axis=0, tiled=True),
        lax.all_gather(output_weight, ("dp", "ctx"), axis=0, tiled=True),
        lax.all_gather(mixed_gain, ("dp", "ctx"), axis=0, tiled=True),
    )
    feed_scale, gate_full, up_full, down_full, final_scale = (
        lax.all_gather(feed_gain, ("dp", "ctx"), axis=0, tiled=True),
        lax.all_gather(gate_weight, ("dp", "ctx"), axis=0, tiled=True),
        lax.all_gather(up_weight, ("dp", "ctx"), axis=0, tiled=True),
        lax.all_gather(down_weight, ("dp", "ctx"), axis=0, tiled=True),
        lax.all_gather(final_gain, ("dp", "ctx"), axis=0, tiled=True),
    )
    gain_one = gain_one.astype(jnp.float32)
    query_scale = query_scale.astype(jnp.float32)
    key_scale = key_scale.astype(jnp.float32)
    mixed_scale = mixed_scale.astype(jnp.float32)
    feed_scale = feed_scale.astype(jnp.float32)
    final_scale = final_scale.astype(jnp.float32)
    tokens_in = tokens.astype(jnp.float32)
    factor_one = rms_factor(tokens_in)
    normed = (tokens_in * factor_one * gain_one).astype(jnp.bfloat16)
    query_raw = jnp.dot(normed, query_full, preferred_element_type=jnp.float32)
    key_raw = jnp.dot(normed, key_full, preferred_element_type=jnp.float32)
    value_rows = jnp.dot(normed, value_full, preferred_element_type=jnp.float32).astype(
        jnp.bfloat16
    )
    cosine, sine = angles_of(query_pos)
    query_heads = query_raw.reshape(local, HQ, HD)
    query_factor = rms_factor(query_heads)
    query_rot = rotate(
        query_heads * query_factor * query_scale, cosine[:, None, :], sine[:, None, :]
    ).astype(jnp.bfloat16)
    query_rows = jnp.transpose(query_rot, (1, 0, 2)).reshape(heads_rows, HD)
    key_factor = rms_factor(key_raw)
    key_rows = rotate(key_raw * key_factor * key_scale, cosine, sine).astype(jnp.bfloat16)

    def attend_block(carry, key_block, value_block, start):
        count = key_block.shape[0]
        key_pos = lax.dynamic_slice_in_dim(positions, start, count)
        key_seg = lax.dynamic_slice_in_dim(segment_ids, start, count)
        allowed = visible(query_pos, query_seg, key_pos, key_seg)

        def update(running):
            running_max, running_sum, running_acc = running
            scores = (
                jnp.einsum("qd,kd->qk", query_rows, key_block, preferred_element_type=jnp.float32)
                * scale
            )
            scores = jnp.where(allowed[None], scores.reshape(HQ, local, count), -1e30).reshape(
                heads_rows, count
            )
            new_max = jnp.maximum(running_max, jnp.max(scores, axis=-1))
            decay = jnp.exp(running_max - new_max)
            weights = jnp.exp(scores - new_max[:, None])
            new_sum = running_sum * decay + jnp.sum(weights, axis=-1)
            new_acc = running_acc * decay[:, None] + jnp.dot(
                weights.astype(jnp.bfloat16), value_block, preferred_element_type=jnp.float32
            )
            return (new_max, new_sum, new_acc)

        return lax.cond(jnp.any(allowed), update, lambda running: running, carry)

    initial = (
        jnp.full((heads_rows,), -1e30, jnp.float32),
        jnp.zeros((heads_rows,), jnp.float32),
        jnp.zeros((heads_rows, HD), jnp.float32),
    )
    key_piece = lax.all_gather(key_rows, "ctx", axis=0, tiled=True)
    value_piece = lax.all_gather(value_rows, "ctx", axis=0, tiled=True)
    count = key_piece.shape[0]
    fold_width = block_width()

    def step_block(running, number):
        first = number * fold_width
        return (
            attend_block(
                running,
                lax.dynamic_slice_in_dim(key_piece, first, fold_width),
                lax.dynamic_slice_in_dim(value_piece, first, fold_width),
                first,
            ),
            None,
        )

    running_max, running_sum, running_acc = lax.scan(
        step_block, initial, jnp.arange(count // fold_width, dtype=jnp.int32)
    )[0]
    log_total = running_max + jnp.log(running_sum)
    out_heads = running_acc / running_sum[:, None]
    attended = (
        jnp.transpose(out_heads.reshape(HQ, local, HD), (1, 0, 2))
        .reshape(local, HQ * HD)
        .astype(jnp.bfloat16)
    )
    projected = jnp.dot(attended, output_full, preferred_element_type=jnp.float32)
    factor_three = rms_factor(projected)
    mixed = tokens_in + projected * factor_three * mixed_scale
    factor_two = rms_factor(mixed)
    normed_two = (mixed * factor_two * feed_scale).astype(jnp.bfloat16)
    gate_pre = jnp.dot(normed_two, gate_full, preferred_element_type=jnp.float32)
    up_pre = jnp.dot(normed_two, up_full, preferred_element_type=jnp.float32)
    hidden = (jax.nn.gelu(gate_pre, approximate=True) * up_pre).astype(jnp.bfloat16)
    branch = jnp.dot(hidden, down_full, preferred_element_type=jnp.float32)
    factor_four = rms_factor(branch)
    layer_out = (mixed + branch * factor_four * final_scale).astype(jnp.bfloat16)
    (
        attention_gain,
        query_weight,
        key_weight,
        value_weight,
        query_gain,
        key_gain,
        output_weight,
        mixed_gain,
        feed_gain,
        gate_weight,
        up_weight,
        down_weight,
        final_gain,
        branch,
    ) = lax.optimization_barrier(
        (
            attention_gain,
            query_weight,
            key_weight,
            value_weight,
            query_gain,
            key_gain,
            output_weight,
            mixed_gain,
            feed_gain,
            gate_weight,
            up_weight,
            down_weight,
            final_gain,
            branch,
        )
    )
    (
        unused_one,
        query_full,
        key_full,
        value_full,
        unused_two,
        unused_three,
        output_full,
        unused_four,
    ) = (
        lax.all_gather(attention_gain, ("dp", "ctx"), axis=0, tiled=True),
        lax.all_gather(query_weight, ("dp", "ctx"), axis=0, tiled=True),
        lax.all_gather(key_weight, ("dp", "ctx"), axis=0, tiled=True),
        lax.all_gather(value_weight, ("dp", "ctx"), axis=0, tiled=True),
        lax.all_gather(query_gain, ("dp", "ctx"), axis=0, tiled=True),
        lax.all_gather(key_gain, ("dp", "ctx"), axis=0, tiled=True),
        lax.all_gather(output_weight, ("dp", "ctx"), axis=0, tiled=True),
        lax.all_gather(mixed_gain, ("dp", "ctx"), axis=0, tiled=True),
    )
    unused_five, gate_full, up_full, down_full, unused_six = (
        lax.all_gather(feed_gain, ("dp", "ctx"), axis=0, tiled=True),
        lax.all_gather(gate_weight, ("dp", "ctx"), axis=0, tiled=True),
        lax.all_gather(up_weight, ("dp", "ctx"), axis=0, tiled=True),
        lax.all_gather(down_weight, ("dp", "ctx"), axis=0, tiled=True),
        lax.all_gather(final_gain, ("dp", "ctx"), axis=0, tiled=True),
    )
    out_grad = cotangent.astype(jnp.float32)
    branch_grad, final_term = norm_back(out_grad, branch, factor_four, final_scale)
    branch_grad = branch_grad.astype(jnp.bfloat16)
    down_weight_grad = lax.psum_scatter(
        jnp.einsum("tf,td->fd", hidden, branch_grad, preferred_element_type=jnp.float32),
        ("dp", "ctx"),
        scatter_dimension=0,
        tiled=True,
    )
    hidden_grad = jnp.einsum(
        "td,fd->tf", branch_grad, down_full, preferred_element_type=jnp.float32
    )
    unused_seven, geglu_back = jax.vjp(
        lambda gate_in, up_in: jax.nn.gelu(gate_in, approximate=True) * up_in, gate_pre, up_pre
    )
    gate_grad, up_grad = geglu_back(hidden_grad)
    gate_grad = gate_grad.astype(jnp.bfloat16)
    up_grad = up_grad.astype(jnp.bfloat16)
    gate_up_grad = jnp.concatenate([gate_grad, up_grad], axis=1)
    normed_cols = normed_two
    gate_up_rows = lax.psum_scatter(
        jnp.einsum("td,tf->df", normed_cols, gate_up_grad, preferred_element_type=jnp.float32),
        ("dp", "ctx"),
        scatter_dimension=0,
        tiled=True,
    )
    gate_weight_grad = gate_up_rows[:, :FF]
    up_weight_grad = gate_up_rows[:, FF:]
    normed_two_grad = jnp.einsum(
        "tf,df->td", gate_grad, gate_full, preferred_element_type=jnp.float32
    ) + jnp.einsum("tf,df->td", up_grad, up_full, preferred_element_type=jnp.float32)
    mixed_part, feed_term = norm_back(normed_two_grad, mixed, factor_two, feed_scale)
    mixed_grad = out_grad + mixed_part
    projected_grad, mixed_term = norm_back(mixed_grad, projected, factor_three, mixed_scale)
    projected_grad = projected_grad.astype(jnp.bfloat16)
    output_weight_grad = lax.psum_scatter(
        jnp.einsum("ta,td->ad", attended, projected_grad, preferred_element_type=jnp.float32),
        ("dp", "ctx"),
        scatter_dimension=0,
        tiled=True,
    )
    attended_grad = jnp.einsum(
        "td,ad->ta", projected_grad, output_full, preferred_element_type=jnp.float32
    ).astype(jnp.bfloat16)
    grad_rows = jnp.transpose(attended_grad.reshape(local, HQ, HD), (1, 0, 2)).reshape(
        heads_rows, HD
    )
    all_keys, all_values = (
        lax.all_gather(key_rows, "ctx", axis=0, tiled=True),
        lax.all_gather(value_rows, "ctx", axis=0, tiled=True),
    )
    group_count = all_keys.shape[0]
    width = block_width()
    number_blocks = group_count // width

    def block_parts(number):
        first = number * width
        key_block = lax.dynamic_slice_in_dim(all_keys, first, width)
        value_block = lax.dynamic_slice_in_dim(all_values, first, width)
        key_pos = lax.dynamic_slice_in_dim(positions, first, width)
        key_seg = lax.dynamic_slice_in_dim(segment_ids, first, width)
        return (key_block, value_block, visible(query_pos, query_seg, key_pos, key_seg))

    def probs_of(key_block, value_block, allowed):
        scores = (
            jnp.einsum("qd,kd->qk", query_rows, key_block, preferred_element_type=jnp.float32)
            * scale
        )
        scores = jnp.where(allowed[None], scores.reshape(HQ, local, width), -1e30).reshape(
            heads_rows, width
        )
        probs = jnp.exp(scores - log_total[:, None])
        prob_grad = jnp.einsum(
            "qd,kd->qk", grad_rows, value_block, preferred_element_type=jnp.float32
        )
        return (probs, prob_grad)

    def first_pass(delta, number):
        key_block, value_block, allowed = block_parts(number)

        def first_compute(running):
            probs, prob_grad = probs_of(key_block, value_block, allowed)
            return running + jnp.sum(probs * prob_grad, axis=-1)

        return (lax.cond(jnp.any(allowed), first_compute, lambda running: running, delta), None)

    delta = lax.scan(
        first_pass,
        jnp.zeros((heads_rows,), jnp.float32),
        jnp.arange(number_blocks, dtype=jnp.int32),
    )[0]

    def second_pass(query_total, number):
        key_block, value_block, allowed = block_parts(number)

        def second_compute(running):
            probs, prob_grad = probs_of(key_block, value_block, allowed)
            score_grad = (probs * (prob_grad - delta[:, None]) * scale).astype(jnp.bfloat16)
            new_total = running + jnp.dot(score_grad, key_block, preferred_element_type=jnp.float32)
            key_part = jnp.einsum(
                "qk,qd->kd", score_grad, query_rows, preferred_element_type=jnp.float32
            )
            value_part = jnp.einsum(
                "qk,qd->kd",
                probs.astype(jnp.bfloat16),
                grad_rows,
                preferred_element_type=jnp.float32,
            )
            return (new_total, key_part, value_part)

        def skipped(running):
            return (
                running,
                jnp.zeros((width, HD), jnp.float32),
                jnp.zeros((width, HD), jnp.float32),
            )

        new_total, key_part, value_part = lax.cond(
            jnp.any(allowed), second_compute, skipped, query_total
        )
        return (new_total, (key_part, value_part))

    query_total, (key_parts, value_parts) = lax.scan(
        second_pass,
        jnp.zeros((heads_rows, HD), jnp.float32),
        jnp.arange(number_blocks, dtype=jnp.int32),
    )
    key_terms = key_parts.reshape(group_count, HD)
    value_terms = value_parts.reshape(group_count, HD)
    key_grad_rows, value_grad_rows = (
        lax.psum_scatter(
            key_terms.astype(jnp.bfloat16), "ctx", scatter_dimension=0, tiled=True
        ).astype(jnp.float32),
        lax.psum_scatter(
            value_terms.astype(jnp.bfloat16), "ctx", scatter_dimension=0, tiled=True
        ).astype(jnp.float32),
    )
    values_grad = value_grad_rows.astype(jnp.bfloat16)
    key_back = rotate(key_grad_rows, cosine, -sine)
    key_in_grad, key_term = norm_back(key_back, key_raw, key_factor, key_scale)
    key_in_grad = key_in_grad.astype(jnp.bfloat16)
    query_back = rotate(
        jnp.transpose(query_total.reshape(HQ, local, HD), (1, 0, 2)),
        cosine[:, None, :],
        -sine[:, None, :],
    )
    query_in_grad, query_term = norm_back(query_back, query_heads, query_factor, query_scale)
    query_in_grad = query_in_grad.reshape(local, HQ * HD).astype(jnp.bfloat16)
    projection_grad = jnp.concatenate([query_in_grad, key_in_grad, values_grad], axis=1)
    normed_cols = normed
    projection_rows = lax.psum_scatter(
        jnp.einsum("td,ta->da", normed_cols, projection_grad, preferred_element_type=jnp.float32),
        ("dp", "ctx"),
        scatter_dimension=0,
        tiled=True,
    )
    query_weight_grad = projection_rows[:, : HQ * HD]
    key_weight_grad = projection_rows[:, HQ * HD : HQ * HD + HD]
    value_weight_grad = projection_rows[:, HQ * HD + HD :]
    normed_grad = jnp.einsum(
        "ta,da->td", query_in_grad, query_full, preferred_element_type=jnp.float32
    )
    normed_grad = normed_grad + jnp.einsum(
        "ta,da->td", key_in_grad, key_full, preferred_element_type=jnp.float32
    )
    normed_grad = normed_grad + jnp.einsum(
        "ta,da->td", values_grad, value_full, preferred_element_type=jnp.float32
    )
    tokens_part, gain_one_term = norm_back(normed_grad, tokens_in, factor_one, gain_one)
    tokens_grad = (mixed_grad + tokens_part).astype(jnp.bfloat16)
    (
        attention_gain_grad,
        query_gain_grad,
        key_gain_grad,
        mixed_gain_grad,
        feed_gain_grad,
        final_gain_grad,
    ) = (
        lax.psum_scatter(gain_one_term, ("dp", "ctx"), scatter_dimension=0, tiled=True),
        lax.psum_scatter(query_term, ("dp", "ctx"), scatter_dimension=0, tiled=True),
        lax.psum_scatter(key_term, ("dp", "ctx"), scatter_dimension=0, tiled=True),
        lax.psum_scatter(mixed_term, ("dp", "ctx"), scatter_dimension=0, tiled=True),
        lax.psum_scatter(feed_term, ("dp", "ctx"), scatter_dimension=0, tiled=True),
        lax.psum_scatter(final_term, ("dp", "ctx"), scatter_dimension=0, tiled=True),
    )
    return (
        layer_out,
        tokens_grad,
        attention_gain_grad,
        query_weight_grad,
        key_weight_grad,
        value_weight_grad,
        query_gain_grad,
        key_gain_grad,
        output_weight_grad,
        mixed_gain_grad,
        feed_gain_grad,
        gate_weight_grad,
        up_weight_grad,
        down_weight_grad,
        final_gain_grad,
    )


def solution(mesh):
    return jax.shard_map(
        body,
        mesh=mesh,
        in_specs=(
            P(("dp", "ctx"), None),
            P(("dp", "ctx")),
            P(("dp", "ctx"), None),
            P(("dp", "ctx"), None),
            P(("dp", "ctx"), None),
            P(("dp", "ctx")),
            P(("dp", "ctx")),
            P(("dp", "ctx"), None),
            P(("dp", "ctx")),
            P(("dp", "ctx")),
            P(("dp", "ctx"), None),
            P(("dp", "ctx"), None),
            P(("dp", "ctx"), None),
            P(("dp", "ctx")),
            P("dp"),
            P("dp"),
            P(("dp", "ctx"), None),
        ),
        out_specs=(
            P(("dp", "ctx"), None),
            P(("dp", "ctx"), None),
            P(("dp", "ctx")),
            P(("dp", "ctx"), None),
            P(("dp", "ctx"), None),
            P(("dp", "ctx"), None),
            P(("dp", "ctx")),
            P(("dp", "ctx")),
            P(("dp", "ctx"), None),
            P(("dp", "ctx")),
            P(("dp", "ctx")),
            P(("dp", "ctx"), None),
            P(("dp", "ctx"), None),
            P(("dp", "ctx"), None),
            P(("dp", "ctx")),
        ),
        check_vma=False,
    )
```

profile of v0, /device:TPU:0, one launch (start us, length us, event | category | flops | bytes accessed | tf_op | source)
XLA Modules:
  0.0 2947.1 jit_solution(18052374977449460637)
XLA Ops:
  14.6 42.3 %all-reduce.17 = (bf16[1152]{0:T(1024)(128)(2,1)S(1)}, bf16[256]{0:T(256)(128)(2,1)S(1)}, bf16[256]{0:T(256)(128)(2,1)S(1)}, bf16[1152]{0:T(1024)(128)(2,1)S(1)}...) all-reduce(bf16[1152]{0:T(1024)(128)(2,1)S(1)} %dynamic-update-slic, ...), channel_id=1, replica_groups=mesh['dp'=4,'ctx'=8] {'dp','ctx'}, use_global_device_ids=true, to_apply=%add | all-reduce | flops 5120 | bytes 20480
  57.0 70.6 %all-gather = bf16[32,36,256]{2,1,0:T(8,128)(2,1)S(1)} all-gather(bf16[1,36,256]{2,1,0:T(8,128)(2,1)} %bitcast.166), channel_id=1, replica_groups=mesh['dp'=4,'ctx'=8] {'dp','ctx'}, dimensions={0}, use_global_device_ids=true | all-gather | bytes 608256 | tf_op jit(solution)/shard_map/all_gather | solution.py:81
  132.6 69.7 %all-gather.2 = bf16[32,36,256]{2,1,0:T(8,128)(2,1)S(1)} all-gather(bf16[1,36,256]{2,1,0:T(8,128)(2,1)S(1)} %bitcast.168), channel_id=1, replica_groups=mesh['dp'=4,'ctx'=8] {'dp','ctx'}, dimensions={0}, use_global_device_ids=true | all-gather | bytes 608256 | tf_op jit(solution)/shard_map/all_gather | solution.py:82
  211.6 31.1 %all-gather.35.cloned.1.call-done = bf16[32,36,1024]{2,1,0:T(8,128)(2,1)} async-done(((bf16[1,36,1024]{2,1,0:T(8,128)(2,1)}), bf16[32,36,1024]{2,1,0:T(8,128)(2,1)}) %all-gather.35.cloned.1.call-update) | async-done | bytes 2359312 | tf_op jit(solution)/shard_map/all_gather | solution.py:80
  257.8 35.8 %all-gather.25.cloned.1.call-done = bf16[4096,256]{1,0:T(8,128)(2,1)} async-done(((bf16[512,256]{1,0:T(8,128)(2,1)}), bf16[4096,256]{1,0:T(8,128)(2,1)}) %all-gather.25.cloned.1.call-update) | async-done | bytes 2097168 | tf_op jit(solution)/shard_map/all_gather | solution.py:151
  293.8 56.8 %while.44 = (s32[]{:T(128)}, f32[2048]{0:T(1024)S(1)}, f32[2048]{0:T(1024)S(1)}, f32[2048,256]{1,0:T(8,128)S(1)}, s32[4]{0:T(128)S(1)}, /*index=5*/s32[4096]{0:T...) while((s32[]{:T(128)}, f32[2048]{0:T(1024)S(1)}, ...), condition=%wide.region_9.10_spmd, body=%wide.region_3.9_spmd.sunk | while | flops 2165838848 | bytes 41057628 | solution.py:167
  360.4 112.8 %all-gather.39.cloned.1.call-done = bf16[32,36,6912]{2,1,0:T(8,128)(2,1)} async-done(((bf16[1,36,6912]{2,1,0:T(8,128)(2,1)}), bf16[32,36,6912]{2,1,0:T(8,128)(2,1)}) %all-gather.39.cloned.1.call-update) | async-done | bytes 15925264 | tf_op jit(solution)/shard_map/all_gather | solution.py:91
  473.2 18.9 reshape.335
  492.1 101.3 %all-gather.37.cloned.1.call-done = bf16[32,36,6912]{2,1,0:T(8,128)(2,1)} async-done(((bf16[1,36,6912]{2,1,0:T(8,128)(2,1)}), bf16[32,36,6912]{2,1,0:T(8,128)(2,1)}) %all-gather.37.cloned.1.call-update) | async-done | bytes 15925264 | tf_op jit(solution)/shard_map/all_gather | solution.py:90
  593.4 18.5 reshape.333
  627.9 21.3 multiply_convert_fusion.1
  649.2 56.4 %all-gather.29.cloned.1.call-done = bf16[6912,1152]{1,0:T(8,128)(2,1)} async-done(((bf16[216,1152]{1,0:T(8,128)(2,1)}), bf16[6912,1152]{1,0:T(8,128)(2,1)}) %all-gather.29.cloned.1.call-update) | async-done | bytes 15925264 | tf_op jit(solution)/shard_map/all_gather | solution.py:92
  725.9 112.1 %all-gather.41.cloned.1.call-done = bf16[32,36,6912]{2,1,0:T(8,128)(2,1)} async-done(((bf16[1,36,6912]{2,1,0:T(8,128)(2,1)}), bf16[32,36,6912]{2,1,0:T(8,128)(2,1)}) %all-gather.41.cloned.1.call-update) | async-done | bytes 15925264 | tf_op jit(solution)/shard_map/all_gather | solution.py:242
  838.1 18.5 reshape.337
  856.6 93.6 %all-gather.31.cloned.1.call-done = bf16[6912,1152]{1,0:T(8,128)(2,1)} async-done(((bf16[216,1152]{1,0:T(8,128)(2,1)}), bf16[6912,1152]{1,0:T(8,128)(2,1)}) %all-gather.31.cloned.1.call-update) | async-done | bytes 15925264 | tf_op jit(solution)/shard_map/all_gather | solution.py:244
  950.2 29.0 multiply_convert_fusion
  995.2 75.2 %all-gather.43.cloned.1.call-done = bf16[32,36,6912]{2,1,0:T(8,128)(2,1)} async-done(((bf16[1,36,6912]{2,1,0:T(8,128)(2,1)}), bf16[32,36,6912]{2,1,0:T(8,128)(2,1)}) %all-gather.43.cloned.1.call-update) | async-done | bytes 15925264 | tf_op jit(solution)/shard_map/all_gather | solution.py:243
  1070.4 18.4 reshape.339
  1111.2 17.7 all-gather.33.cloned.1.call-done
  1133.4 43.0 %while.45 = (s32[]{:T(128)}, f32[2048]{0:T(1024)S(1)}, s32[4]{0:T(128)S(1)}, s32[4096]{0:T(1024)S(1)}, s32[512]{0:T(512)S(1)}, /*index=5*/s32[4096]{0:T(1024)S(1...) while((s32[]{:T(128)}, f32[2048]{0:T(1024)S(1)}, ...), condition=%wide.region_21.22_spmd, body=%wide.region_16.21_spmd.sunk | while | flops 2160591872 | bytes 29433132 | solution.py:333
  1177.8 67.7 %while.46 = (s32[]{:T(128)}, f32[2048,256]{1,0:T(8,128)}, bf16[4,1024,256]{2,1,0:T(8,128)(2,1)}, bf16[4,1024,256]{2,1,0:T(8,128)(2,1)}, s32[4]{0:T(128)S(1)}, /*...) while((s32[]{:T(128)}, f32[2048,256]{1,0:T(8,128)}, ...), condition=%wide.region_26.0_spmd, body=%wide.region_22.26_spmd.sunk | while | flops 5394924544 | bytes 87612352 | solution.py:369
  1207.2 16.5 conditional.8
  1255.7 32.5 %fusion.46 = f32[1152,13824]{1,0:T(8,128)} fusion(bf16[512,1152]{1,0:T(8,128)(2,1)S(1)} %copy-done.17, bf16[512,6912]{1,0:T(8,128)(2,1)} %get-tuple-element.747, bf16[512,6912]{1,0:T(8,128)(2,1)} %get-tuple-element.748), kind=kOutput, calls=%fused_computation.60 | convolution fusion | flops 16335765504 | bytes 79036416 | tf_op jit(solution)/shard_map/td,tf->df/dot_general | solution.py:268
  1291.1 51.9 %reduce-scatter.7.cloned.1.call-done = bf16[512,256]{0,1:T(8,128)(2,1)} async-done(((bf16[4096,256]{0,1:T(8,128)(2,1)}), bf16[512,256]{0,1:T(8,128)(2,1)}) %reduce-scatter.7.cloned.1.call-update) | async-done | bytes 262160 | tf_op jit(solution)/shard_map/reduce_scatter | solution.py:377
  1359.9 53.7 %reduce-scatter.9.cloned.1.call-done = bf16[512,256]{1,0:T(8,128)(2,1)} async-done(((bf16[4096,256]{1,0:T(8,128)(2,1)}), bf16[512,256]{1,0:T(8,128)(2,1)}) %reduce-scatter.9.cloned.1.call-update) | async-done | bytes 262160 | tf_op jit(solution)/shard_map/reduce_scatter | solution.py:380
  1426.0 18.9 fusion.96
  1446.7 73.3 %all-gather.8 = bf16[32,36,256]{2,1,0:T(8,128)(2,1)S(1)} all-gather(bf16[1,36,256]{2,1,0:T(8,128)(2,1)S(1)} %bitcast.167), channel_id=1, replica_groups=mesh['dp'=4,'ctx'=8] {'dp','ctx'}, dimensions={0}, use_global_device_ids=true | all-gather | bytes 608256 | tf_op jit(solution)/shard_map/all_gather | solution.py:233
  1521.0 76.6 %all-gather.9 = bf16[32,36,256]{2,1,0:T(8,128)(2,1)S(1)} all-gather(bf16[1,36,256]{2,1,0:T(8,128)(2,1)S(1)} %bitcast.169), channel_id=1, replica_groups=mesh['dp'=4,'ctx'=8] {'dp','ctx'}, dimensions={0}, use_global_device_ids=true | all-gather | bytes 608256 | tf_op jit(solution)/shard_map/all_gather | solution.py:234
  1611.3 39.9 %all-reduce.15 = (f32[1152]{0:T(1024)}, f32[256]{0:T(256)}, f32[256]{0:T(256)}, f32[1152]{0:T(1024)}, f32[1152]{0:T(1024)}, /*index=5*/f32[1152]{0:T(1024)}) all-reduce(f32[1152]{0:T(1024)} %get-tuple-element.626, f32[256]{0:T(256)} %fusion.68, f32[256]{0:T(256)} %get-tuple-element.628, ...), channel_id=4, replica_groups=mesh['dp'=4,'ctx'=8] {'dp','ctx'}, use_global_device_ids=true, to_apply=%region_33.34.clone | all-reduce | flops 5120 | bytes 40960
  1662.9 844.8 %all-reduce.20.cloned.1.call-done = (f32[1152,1536]{1,0:T(8,128)}, f32[1152,13824]{1,0:T(8,128)}) async-done(((f32[1152,1536]{1,0:T(8,128)}, f32[1152,13824]{1,0:T(8,128)}), (f32[1152,1536]{1,0:T(8,128)}, f32[1152,13824]{1,0:T(8,128)})) %all-reduce.20.cloned.1.call-update) | async-done | bytes 70778896
  2514.4 106.0 %reduce-scatter.11.cloned.1.call-done = f32[32,1152]{1,0:T(8,128)} async-done(((f32[1024,1152]{1,0:T(8,128)}), f32[32,1152]{1,0:T(8,128)}) %reduce-scatter.11.cloned.1.call-update) | async-done | bytes 147472 | tf_op jit(solution)/shard_map/reduce_scatter | solution.py:282
  2620.5 319.7 %reduce-scatter.13.cloned.1.call-done = f32[216,1152]{1,0:T(8,128)} async-done(((f32[6912,1152]{1,0:T(8,128)}), f32[216,1152]{1,0:T(8,128)}) %reduce-scatter.13.cloned.1.call-update) | async-done | bytes 995344
  (467 shorter events, 450.7 us)
Async XLA Ops:
  7.2 120.5 %copy-start.11 = (bf16[512,1152]{1,0:T(8,128)(2,1)S(1)}, bf16[512,1152]{1,0:T(8,128)(2,1)}, u32[]{:S(2)}) copy-start(bf16[512,1152]{1,0:T(8,128)(2,1)} %param.29) | copy-start | bytes 3538948
  7.2 200.2 %all-gather.23.cloned.1.call-start = ((), (), s32[]{:S(2)}) async-start(), calls=%async_computation.4 | async-start | bytes 2359296 | tf_op jit(solution)/shard_map/all_gather | solution.py:150
  7.3 122.6 %copy-start.84 = (f32[128]{0:T(128)}, f32[128]{0:T(128)S(1)}, u32[]{:S(2)}) copy-start(f32[128]{0:T(128)S(1)} %multiply_power_fusion) | copy-start | bytes 1540
  9.5 237.3 %copy-start.67 = (f32[512]{0:T(512)}, f32[512]{0:T(512)S(1)}, u32[]{:S(2)}) copy-start(f32[512]{0:T(512)S(1)} %get-tuple-element.770) | copy-start | bytes 6148
  56.9 189.8 %copy-start.60 = (f32[1152]{0:T(1024)}, f32[1152]{0:T(1024)S(1)}, u32[]{:S(2)}) copy-start(f32[1152]{0:T(1024)S(1)} %convert_element_type.122) | copy-start | bytes 13828
  131.8 110.8 %all-gather.35.cloned.1.call-start = ((), (), s32[]{:S(2)}) async-start(), calls=%async_computation.13 | async-start | bytes 2703360 | tf_op jit(solution)/shard_map/all_gather | solution.py:80
  132.6 161.0 %all-gather.25.cloned.1.call-start = ((), (), s32[]{:S(2)}) async-start(), calls=%async_computation.5 | async-start | bytes 2359296 | tf_op jit(solution)/shard_map/all_gather | solution.py:151
  203.8 149.7 %all-gather.27.cloned.1.call-start = ((), (), s32[]{:S(2)}) async-start(), calls=%async_computation.6 | async-start | bytes 2433024 | tf_op jit(solution)/shard_map/all_gather | solution.py:85
  204.4 268.8 %all-gather.39.cloned.1.call-start = ((), (), s32[]{:S(2)}) async-start(), calls=%async_computation.15 | async-start | bytes 18247680 | tf_op jit(solution)/shard_map/all_gather | solution.py:91
  205.0 388.5 %all-gather.37.cloned.1.call-start = ((), (), s32[]{:S(2)}) async-start(), calls=%async_computation.14 | async-start | bytes 18247680 | tf_op jit(solution)/shard_map/all_gather | solution.py:90
  205.5 500.0 %all-gather.29.cloned.1.call-start = ((), (), s32[]{:S(2)}) async-start(), calls=%async_computation.7 | async-start | bytes 16422912 | tf_op jit(solution)/shard_map/all_gather | solution.py:92
  206.3 631.8 %all-gather.41.cloned.1.call-start = ((), (), s32[]{:S(2)}) async-start(), calls=%async_computation.16 | async-start | bytes 18247680 | tf_op jit(solution)/shard_map/all_gather | solution.py:242
  207.1 150.8 %copy-start.50 = (f32[1152]{0:T(1024)}, f32[1152]{0:T(1024)S(1)}, u32[]{:S(2)}) copy-start(f32[1152]{0:T(1024)S(1)} %convert_element_type.132) | copy-start | bytes 13828
  207.1 152.1 %copy-start.58 = (f32[1152]{0:T(1024)}, f32[1152]{0:T(1024)S(1)}, u32[]{:S(2)}) copy-start(f32[1152]{0:T(1024)S(1)} %convert_element_type.133) | copy-start | bytes 13828
  359.2 132.9 %copy-start.72 = (f32[512]{0:T(512)}, f32[512]{0:T(512)S(1)}, u32[]{:S(2)}) copy-start(f32[512]{0:T(512)S(1)} %get-tuple-element.776) | copy-start | bytes 6148
  360.4 267.5 %copy-start.16 = (bf16[512,1152]{1,0:T(8,128)(2,1)}, bf16[512,1152]{1,0:T(8,128)(2,1)S(1)}, u32[]{:S(2)}) copy-start(bf16[512,1152]{1,0:T(8,128)(2,1)S(1)} %multiply_convert_fusion.2) | copy-start | bytes 3538948
  720.4 229.7 %copy-start.18 = (f32[512,1152]{1,0:T(8,128)}, f32[512,1152]{1,0:T(8,128)S(1)}, u32[]{:S(2)}) copy-start(f32[512,1152]{1,0:T(8,128)S(1)} %get-tuple-element.451) | copy-start | bytes 7077892
  720.5 229.7 %all-gather.31.cloned.1.call-start = ((), (), s32[]{:S(2)}) async-start(), calls=%async_computation.8 | async-start | bytes 16422912 | tf_op jit(solution)/shard_map/all_gather | solution.py:244
  721.2 349.2 %all-gather.43.cloned.1.call-start = ((), (), s32[]{:S(2)}) async-start(), calls=%async_computation.17 | async-start | bytes 18247680 | tf_op jit(solution)/shard_map/all_gather | solution.py:243
  721.8 407.1 %all-gather.33.cloned.1.call-start = ((), (), s32[]{:S(2)}) async-start(), calls=%async_computation.9 | async-start | bytes 2433024 | tf_op jit(solution)/shard_map/all_gather | solution.py:237
  723.8 226.3 %copy-start.70 = (f32[512]{0:T(512)}, f32[512]{0:T(512)S(1)}, u32[]{:S(2)}) copy-start(f32[512]{0:T(512)S(1)} %get-tuple-element.778) | copy-start | bytes 6148
  723.8 226.3 %copy-start.86 = (f32[512]{0:T(512)}, f32[512]{0:T(512)S(1)}, u32[]{:S(2)}) copy-start(f32[512]{0:T(512)S(1)} %get-tuple-element.777) | copy-start | bytes 6148
  725.7 224.5 %copy-start.56 = (f32[1152]{0:T(1024)S(1)}, f32[1152]{0:T(1024)}, u32[]{:S(2)}) copy-start(f32[1152]{0:T(1024)} %copy-done.55) | copy-start | bytes 13828
  725.7 617.3 %reduce-scatter.7.cloned.1.call-start = ((), (), s32[]{:S(2)}) async-start(), calls=%async_computation.10 | async-start | bytes 2359296 | tf_op jit(solution)/shard_map/reduce_scatter | solution.py:377
  995.2 93.6 %copy-start.8 = (f32[512,1152]{1,0:T(8,128)S(1)}, f32[512,1152]{1,0:T(8,128)}, u32[]{:S(2)}) copy-start(f32[512,1152]{1,0:T(8,128)} %copy-done.7) | copy-start | bytes 7077892
  995.2 93.6 %copy-start.59 = (f32[1152]{0:T(1024)S(1)}, f32[1152]{0:T(1024)}, u32[]{:S(2)}) copy-start(f32[1152]{0:T(1024)} %copy-done.58) | copy-start | bytes 13828
  1249.8 163.7 %reduce-scatter.9.cloned.1.call-start = ((), (), s32[]{:S(2)}) async-start(), calls=%async_computation.11 | async-start | bytes 2359296 | tf_op jit(solution)/shard_map/reduce_scatter | solution.py:380
  1250.6 347.9 %all-gather.45.cloned.1.call-start = ((), (), s32[]{:S(2)}) async-start(), calls=%async_computation.18 | async-start | bytes 2703360 | tf_op jit(solution)/shard_map/all_gather | solution.py:232
  1255.6 1252.1 %all-reduce.20.cloned.1.call-start = ((), (), s32[]{:S(2)}) async-start(), calls=%async_computation.20 | async-start | bytes 141557760
  1420.0 1200.5 %reduce-scatter.11.cloned.1.call-start = ((), (), s32[]{:S(2)}) async-start(), calls=%async_computation.12 | async-start | bytes 4866048 | tf_op jit(solution)/shard_map/reduce_scatter | solution.py:282
  1425.3 1514.8 %reduce-scatter.13.cloned.1.call-start = ((), (), s32[]{:S(2)}) async-start(), calls=%async_computation.19 | async-start | bytes 32845824
  1445.1 75.9 %copy-start.54 = (bf16[36,256]{1,0:T(8,128)(2,1)S(1)}, bf16[36,256]{1,0:T(8,128)(2,1)}, u32[]{:S(2)}) copy-start(bf16[36,256]{1,0:T(8,128)(2,1)} %param.33) | copy-start | bytes 55300
  (78 other events, 1025.6 us)
Sparse Core Ops, SparseCore 0:
  132.0 51.0 all-gather.22
  186.0 56.6 all-gather.34
  245.4 48.1 all-gather.24
  296.4 55.7 all-gather.26
  355.0 118.1 all-gather.38
  475.9 117.4 all-gather.36
  596.3 109.1 all-gather.28
  720.6 117.4 all-gather.40
  840.9 109.1 all-gather.30
  952.9 117.4 all-gather.42
  1073.3 55.4 all-gather.32
  1250.0 93.0 reduce-scatter.6
  1346.6 66.8 reduce-scatter.8
  1416.3 57.5 all-gather.44
  1480.1 1027.5 all-reduce.19
  2513.6 106.8 reduce-scatter.10
  2628.5 311.6 reduce-scatter.12
where the time goes:
time: 2960 us; the launch traced here: 2950 us
  waiting for transfers between devices  2020 us (68%)
  blocking collectives  373 us (13%)
  matrix products  267 us (9%)
  local copies, waits for them, and re-layouts  193 us (7%)
  other arithmetic  64.3 us (2%)
    unnamed x19, waiting for transfers between devices  1170 us
    all_gather x2, waiting for transfers between devices, body(): lax.all_gather(gate_weight, ('dp', 'ctx'), axis=0, tiled=True)  213 us
    all_gather x2, waiting for transfers between devices, body(): lax.all_gather(up_weight, ('dp', 'ctx'), axis=0, tiled=True)  188 us
    all_gather x2, waiting for transfers between devices, body(): lax.all_gather(down_weight, ('dp', 'ctx'), axis=0, tiled=True)  150 us
    all_gather x2, blocking collectives, body(): lax.all_gather(value_weight, ('dp', 'ctx'), axis=0, tiled=True)  146 us
    all_gather x2, blocking collectives, body(): lax.all_gather(key_weight, ('dp', 'ctx'), axis=0, tiled=True)  144 us
    unnamed x202, local copies, waits for them, and re-layouts  110 us
    reduce_scatter x1, waiting for transfers between devices, body(): lax.psum_scatter(jnp.einsum('ta,td->ad', attended, projected_grad, prefer...  106 us
  transfers between devices with their start and end apart: 17, of which 14 were waited for; matrix products, arithmetic and copies ran while one was open for 13% of the time, Pallas kernels for 0%

commit v1 on v0

v1 whole, which is shorter than its diff:
```python
import jax
import jax.numpy as jnp
import numpy as np
from jax import lax
from jax.experimental import pallas as pl
from jax.experimental.pallas import tpu as pltpu
from jax.sharding import Mesh, PartitionSpec as P

FF = 6912
HQ = 4
HD = 256
EPSILON = 1e-06
THETA = 1000000.0
BF = jnp.bfloat16
F32 = jnp.float32

AXES = ("x", "core", "w", "z", "y")
CTX_GRID = {8: (1, 4, 2), 32: (2, 4, 4)}


def grid_of(mesh):
    dp, ctx = mesh.shape["dp"], mesh.shape["ctx"]
    w, z, y = CTX_GRID.get(ctx, (1, ctx, 1))
    return (dp // 2, 2, w, z, y)


class Place:
    def __init__(self, sizes):
        self.size = dict(zip(AXES, sizes))
        self.at = {a: lax.axis_index(a) for a in AXES}

    def shift(self, value, axis, by):
        n = self.size[axis]
        return lax.ppermute(value, axis, [(i, (i + by) % n) for i in range(n)])

    def shift_wz(self, value, kw, kz):
        nw, nz = self.size["w"], self.size["z"]
        pairs = [
            (w * nz + z, ((w + kw) % nw) * nz + (z + kz) % nz) for w in range(nw) for z in range(nz)
        ]
        return lax.ppermute(value, ("w", "z"), pairs)

    def swap_core(self, value):
        return lax.ppermute(value, "core", [(0, 1), (1, 0)])

    def wz_steps(self):
        return [(kw, kz) for kw in range(self.size["w"]) for kz in range(self.size["z"])]

    def chip(self, spot):
        size = self.size
        return ((spot["x"] * size["w"] + spot["w"]) * size["z"] + spot["z"]) * size["y"] + spot["y"]

    def ctx_chip(self, spot):
        return (spot["w"] * self.size["z"] + spot["z"]) * self.size["y"] + spot["y"]

    def gather(self, own, orders, after=None):
        size, at = self.size, self.at
        rows = own.shape[0]
        chips = size["x"] * size["w"] * size["z"] * size["y"]
        full = jnp.zeros((chips * rows, own.shape[1]), own.dtype)
        came = []
        if after is not None:
            own, _ = lax.optimization_barrier((own, after))
        for number, (kw, kz) in enumerate(self.wz_steps()):
            block = own if kw == kz == 0 else self.shift_wz(own, kw, kz)
            if kw or kz:
                came.append(block)
            spot = {"w": (at["w"] - kw) % size["w"], "z": (at["z"] - kz) % size["z"]}
            first, second = orders[number % len(orders)]
            for ka in range(size[first]):
                block_a = block if ka == 0 else self.shift(block, first, ka)
                spot[first] = (at[first] - ka) % size[first]
                for kb in range(size[second]):
                    block_b = block_a if kb == 0 else self.shift(block_a, second, kb)
                    spot[second] = (at[second] - kb) % size[second]
                    full = lax.dynamic_update_slice(full, block_b, (self.chip(spot) * rows, 0))
        return full, came

    def gather_group(self, own):
        size, at = self.size, self.at
        rows = own.shape[0]
        full = jnp.zeros((size["w"] * size["z"] * size["y"] * rows, own.shape[1]), own.dtype)
        for kw, kz in self.wz_steps():
            block = own if kw == kz == 0 else self.shift_wz(own, kw, kz)
            spot = {"w": (at["w"] - kw) % size["w"], "z": (at["z"] - kz) % size["z"]}
            for ky in range(size["y"]):
                block_y = block if ky == 0 else self.shift(block, "y", ky)
                spot["y"] = (at["y"] - ky) % size["y"]
                full = lax.dynamic_update_slice(full, block_y, (self.ctx_chip(spot) * rows, 0))
        return full

    def scatter(self, full, orders):
        size, at = self.size, self.at
        lead = ("x", "w", "z", "y") if "x" in orders[0] else ("w", "z", "y")
        grid = tuple(size[a] for a in lead)
        full = full.reshape(grid + (-1, full.shape[-1]))
        total = None
        for number, (kw, kz) in reversed(list(enumerate(self.wz_steps()))):
            spot = {"w": (at["w"] + kw) % size["w"], "z": (at["z"] + kz) % size["z"]}
            names = [a for a in lead if a not in spot]
            part = lax.dynamic_slice(
                full,
                tuple(spot.get(a, 0) for a in lead) + (0, 0),
                tuple(1 if a in spot else size[a] for a in lead) + full.shape[-2:],
            ).reshape(tuple(size[a] for a in names) + full.shape[-2:])
            for axis in reversed(orders[number % len(orders)]):
                dim, n = names.index(axis), size[axis]
                names.remove(axis)

                def take(k):
                    return lax.dynamic_index_in_dim(part, (at[axis] + k) % n, dim, keepdims=False)

                acc = take(0).astype(F32)
                for k in range(1, n):
                    acc = acc + self.shift(take(k), axis, k).astype(F32)
                if names:
                    part = acc.astype(BF)
            if kw or kz:
                acc = self.shift_wz(acc.astype(BF), kw, kz).astype(F32)
            total = acc if total is None else total + acc
        return total


def rms_factor(values):
    return lax.rsqrt(jnp.mean(values * values, axis=-1, keepdims=True) + EPSILON)


def norm_back(incoming, values, factor, gain):
    scaled = incoming * gain
    gain_term = jnp.sum((incoming * values * factor).reshape(-1, values.shape[-1]), axis=0)
    inner = jnp.mean(scaled * values, axis=-1, keepdims=True)
    return (factor * scaled - values * (factor * factor * factor) * inner, gain_term)


def angles_of(position_ids):
    half_width = HD // 2
    inverse = THETA ** (-(jnp.arange(half_width, dtype=F32) * 2.0) / HD)
    angle = position_ids.astype(F32)[:, None] * inverse[None, :]
    return (jnp.cos(angle), jnp.sin(angle))


def rotate(values, cosine, sine):
    half_width = values.shape[-1] // 2
    first_half = values[..., :half_width]
    second_half = values[..., half_width:]
    return jnp.concatenate(
        [first_half * cosine - second_half * sine, second_half * cosine + first_half * sine],
        axis=-1,
    )


def matmul(left, right):
    return jnp.dot(left, right, preferred_element_type=F32)


def matmul_nt(left, right):
    return jnp.einsum("ij,kj->ik", left, right, preferred_element_type=F32)


def matmul_tn(left, right):
    return jnp.einsum("ji,jk->ik", left, right, preferred_element_type=F32)


def allowed_pairs(key_pos, key_seg, query_pos, query_seg):
    return (key_pos <= query_pos) & ((key_seg == 0) | (key_seg == query_seg))


def forward_kernel(
    live, q_ref, kv_ref, key_pos, key_seg, query_pos, query_seg, out_ref, log_ref, acc, total
):
    block = pl.program_id(0)
    local = q_ref.shape[0]

    @pl.when(block == 0)
    def _():
        acc[...] = jnp.zeros_like(acc)
        total[...] = jnp.zeros_like(total)

    @pl.when(live[block] != 0)
    def _():
        keys = kv_ref[:, :HD]
        values_t = kv_ref[:, HD:].T
        allowed = allowed_pairs(key_pos[...], key_seg[...], query_pos[...], query_seg[...])
        for head in range(HQ):
            mine = pl.ds(head * local, local)
            scores = matmul_nt(keys, q_ref[:, head * HD : (head + 1) * HD]) * HD ** (-0.5)
            weights = jnp.where(allowed, jnp.exp(scores), 0.0)
            total[:, mine] += jnp.sum(weights, axis=0, keepdims=True)
            acc[:, mine] += matmul(values_t, weights.astype(BF))

    @pl.when(block == pl.num_programs(0) - 1)
    def _():
        for head in range(HQ):
            mine = pl.ds(head * local, local)
            out_ref[:, head * HD : (head + 1) * HD] = (acc[:, mine] / total[:, mine]).T.astype(BF)
        log_ref[...] = jnp.log(total[...])


def backward_kernel(
    live,
    q_ref,
    grad_ref,
    log_ref,
    delta_ref,
    kv_ref,
    key_pos,
    key_seg,
    query_pos,
    query_seg,
    q_grad_ref,
    kv_grad_ref,
    acc,
):
    block = pl.program_id(0)
    local = q_ref.shape[0]

    @pl.when(block == 0)
    def _():
        acc[...] = jnp.zeros_like(acc)

    @pl.when(live[block] == 0)
    def _():
        kv_grad_ref[...] = jnp.zeros_like(kv_grad_ref)

    @pl.when(live[block] != 0)
    def _():
        keys = kv_ref[:, :HD]
        keys_t = keys.T
        values = kv_ref[:, HD:]
        allowed = allowed_pairs(key_pos[...], key_seg[...], query_pos[...], query_seg[...])
        key_grad = jnp.zeros(keys.shape, F32)
        value_grad = jnp.zeros(keys.shape, F32)
        for head in range(HQ):
            mine = pl.ds(head * local, local)
            queries = q_ref[:, head * HD : (head + 1) * HD]
            grads = grad_ref[:, head * HD : (head + 1) * HD]
            scores = matmul_nt(keys, queries) * HD ** (-0.5)
            probs = jnp.where(allowed, jnp.exp(scores - log_ref[:, mine]), 0.0)
            prob_grad = matmul_nt(values, grads)
            score_grad = (probs * (prob_grad - delta_ref[:, mine]) * HD ** (-0.5)).astype(BF)
            value_grad += matmul(probs.astype(BF), grads)
            key_grad += matmul(score_grad, queries)
            acc[:, mine] += matmul(keys_t, score_grad)
        kv_grad_ref[:, :HD] = key_grad.astype(BF)
        kv_grad_ref[:, HD:] = value_grad.astype(BF)

    @pl.when(block == pl.num_programs(0) - 1)
    def _():
        for head in range(HQ):
            mine = pl.ds(head * local, local)
            q_grad_ref[:, head * HD : (head + 1) * HD] = acc[:, mine].T


class Attention:
    def __init__(self, positions, segment_ids, query_pos, query_seg):
        local = query_pos.shape[0]
        self.local = local
        self.blocks = positions.shape[0] // local
        pos = positions.reshape(self.blocks, local)
        seg = segment_ids.reshape(self.blocks, local)
        seg_low, seg_high = jnp.min(seg, axis=1), jnp.max(seg, axis=1)
        late = jnp.min(pos, axis=1) > jnp.max(query_pos)
        foreign = (seg_low > 0) & (
            (seg_low > jnp.max(query_seg)) | (seg_high < jnp.min(query_seg))
        )
        self.live = jnp.where(late | foreign, 0, 1).astype(jnp.int32)
        self.marks = (
            positions.reshape(-1, 1),
            segment_ids.reshape(-1, 1),
            query_pos.reshape(1, -1),
            query_seg.reshape(1, -1),
        )

    def specs(self):
        local = self.local
        whole = lambda *shape: pl.BlockSpec(shape, lambda j, live: (0,) * len(shape))
        rows = lambda width: pl.BlockSpec((local, width), lambda j, live: (j, 0))
        marks = [rows(1), rows(1), whole(1, local), whole(1, local)]
        return whole, rows, marks

    def forward(self, queries, key_values):
        local, wide = queries.shape
        whole, rows, marks = self.specs()
        return pl.pallas_call(
            forward_kernel,
            out_shape=(
                jax.ShapeDtypeStruct((local, wide), BF),
                jax.ShapeDtypeStruct((1, HQ * local), F32),
            ),
            grid_spec=pltpu.PrefetchScalarGridSpec(
                num_scalar_prefetch=1,
                grid=(self.blocks,),
                in_specs=[whole(local, wide), rows(2 * HD)] + marks,
                out_specs=(whole(local, wide), whole(1, HQ * local)),
                scratch_shapes=[
                    pltpu.VMEM((HD, HQ * local), F32),
                    pltpu.VMEM((1, HQ * local), F32),
                ],
            ),
            cost_estimate=pl.CostEstimate(
                flops=20 * 4 * local * local * HD, bytes_accessed=8 << 20, transcendentals=0
            ),
        )(self.live, queries, key_values, *self.marks)

    def backward(self, queries, grads, logs, delta, key_values):
        local, wide = queries.shape
        whole, rows, marks = self.specs()
        return pl.pallas_call(
            backward_kernel,
            out_shape=(
                jax.ShapeDtypeStruct((local, wide), F32),
                jax.ShapeDtypeStruct(key_values.shape, BF),
            ),
            grid_spec=pltpu.PrefetchScalarGridSpec(
                num_scalar_prefetch=1,
                grid=(self.blocks,),
                in_specs=[
                    whole(local, wide),
                    whole(local, wide),
                    whole(1, HQ * local),
                    whole(1, HQ * local),
                    rows(2 * HD),
                ]
                + marks,
                out_specs=(whole(local, wide), rows(2 * HD)),
                scratch_shapes=[pltpu.VMEM((HD, HQ * local), F32)],
            ),
            cost_estimate=pl.CostEstimate(
                flops=20 * 10 * local * local * HD, bytes_accessed=16 << 20, transcendentals=0
            ),
        )(self.live, queries, grads, logs, delta, key_values, *self.marks)


def body(
    sizes,
    tokens,
    attention_gain,
    query_weight,
    key_weight,
    value_weight,
    query_gain,
    key_gain,
    output_weight,
    mixed_gain,
    feed_gain,
    gate_weight,
    up_weight,
    down_weight,
    final_gain,
    segment_ids,
    positions,
    cotangent,
):
    place = Place(sizes)
    nx, _, nw, nz, ny = sizes
    chips = nx * nw * nz * ny
    core = place.at["core"]
    local, model = tokens.shape
    rows = query_weight.shape[0]
    wide = HQ * HD
    half = FF // 2
    stretch = half // nx
    offset = place.ctx_chip(place.at) * local
    query_pos = lax.dynamic_slice_in_dim(positions, offset, local)
    query_seg = lax.dynamic_slice_in_dim(segment_ids, offset, local)
    both_ways = (("x", "y"), ("y", "x"))

    def pick(pair, which):
        return lax.dynamic_index_in_dim(pair, which, 0, keepdims=False)

    def cores_in_order(own, other):
        return jnp.where(core == 0, jnp.stack([own, other]), jnp.stack([other, own]))

    inside = np.arange(model).reshape(nx, 2, nw, nz, ny, rows).transpose(0, 2, 3, 4, 1, 5).reshape(-1)
    order = jnp.asarray(inside, jnp.int32)
    counting = lax.iota(jnp.int32, model)
    to_inside = (counting[:, None] == order[None, :]).astype(BF)
    to_outside = (order[:, None] == counting[None, :]).astype(BF)

    def reorder(values, matrix):
        if values.dtype == F32:
            return jnp.dot(values, matrix.astype(F32), precision=lax.Precision.HIGHEST)
        return matmul(values, matrix).astype(BF)

    def column_halves(query, key, value):
        cut = lambda m: m.reshape(m.shape[0], 2, -1)
        halves = jnp.concatenate([cut(query), cut(key), cut(value)], axis=2)
        return jnp.moveaxis(halves, 1, 0)

    head_width = wide // 2 + HD
    gains = jnp.concatenate(
        [attention_gain, mixed_gain, feed_gain, final_gain, query_gain, key_gain]
    )
    gain_count = gains.size
    projections = column_halves(query_weight, key_weight, value_weight)
    gain_rows = -(-gain_count // head_width) * 8
    gain_block = jnp.zeros((gain_rows * head_width,), BF).at[:gain_count].set(gains)
    small = jnp.concatenate(
        [gain_block.reshape(gain_rows, head_width), reorder(output_weight, to_inside).reshape(-1, head_width)]
    )
    first_own = jnp.concatenate(
        [
            cores_in_order(pick(projections, core), place.swap_core(pick(projections, 1 - core))).reshape(
                2 * rows, head_width
            ),
            small,
        ]
    )
    first_all, first_came = place.gather(first_own, both_ways)
    first_all = cores_in_order(first_all, place.swap_core(first_all)).reshape(
        2, chips, first_own.shape[0], head_width
    )
    projection_full = first_all[:, :, : 2 * rows].reshape(2, model, head_width)
    projection_full = jnp.concatenate([projection_full[0], projection_full[1]], axis=1)
    gains_all = first_all[:, :, 2 * rows].reshape(2, chips, head_width)[:, :, :gain_count]
    gains_all = jnp.moveaxis(gains_all.astype(F32), 0, 1)
    spans = np.cumsum([0, rows, rows, rows, rows, query_gain.size, key_gain.size])
    gain_one, mixed_scale, feed_scale, final_scale, query_scale, key_scale = (
        gains_all[:, :, a:b] for a, b in zip(spans[:-1], spans[1:])
    )
    gain_one, mixed_scale, feed_scale, final_scale = (
        g.reshape(model) for g in (gain_one, mixed_scale, feed_scale, final_scale)
    )

    def true_order(values):
        values = values.reshape(nx, nw, nz, ny, 2, -1)
        return jnp.transpose(values, (0, 4, 1, 2, 3, 5)).reshape(-1)

    query_scale, key_scale = true_order(query_scale), true_order(key_scale)
    output_full = first_all[:, :, 2 * rows + gain_rows :].reshape(2, nx, nw * nz * ny, -1, model)
    output_full = jnp.moveaxis(output_full, 0, 1).reshape(wide, model)

    gate_up = jnp.stack([gate_weight, up_weight], axis=1).reshape(rows, 2, nx, 2, stretch)

    def half_of(which):
        piece = lax.dynamic_index_in_dim(gate_up, which, 3, keepdims=False)
        return piece.reshape(rows, FF)

    gate_up_own = cores_in_order(half_of(core), place.swap_core(half_of(1 - core)))
    gate_up_full, gate_up_came = place.gather(
        gate_up_own.reshape(2 * rows, FF), both_ways, first_came
    )
    down_full, _ = place.gather(reorder(down_weight, to_inside), both_ways, gate_up_came)

    tokens_in = reorder(tokens, to_inside).astype(F32)
    out_grad = reorder(cotangent, to_inside).astype(F32)
    factor_one = rms_factor(tokens_in)
    normed = (tokens_in * factor_one * gain_one).astype(BF)
    raw = matmul(normed, projection_full)
    heads_half = wide // 2

    def both_halves(at, width):
        return [raw[:, at : at + width], raw[:, head_width + at : head_width + at + width]]

    query_raw = [
        piece[:, h * HD : (h + 1) * HD]
        for piece in both_halves(0, heads_half)
        for h in range(HQ // 2)
    ]
    key_raw = jnp.concatenate(both_halves(heads_half, HD // 2), axis=1)
    value_rows = jnp.concatenate(both_halves(heads_half + HD // 2, HD // 2), axis=1).astype(BF)
    cosine, sine = angles_of(query_pos)
    key_factor = rms_factor(key_raw)
    key_rows = rotate(key_raw * key_factor * key_scale, cosine, sine).astype(BF)
    key_values = place.gather_group(jnp.concatenate([key_rows, value_rows], axis=1))
    query_factor = [rms_factor(q) for q in query_raw]
    queries = jnp.concatenate(
        [
            rotate(q * f * query_scale, cosine, sine).astype(BF)
            for q, f in zip(query_raw, query_factor)
        ],
        axis=1,
    )
    attention = Attention(positions, segment_ids, query_pos, query_seg)
    attended, logs = attention.forward(queries, key_values)
    projected = matmul(attended, output_full)
    factor_three = rms_factor(projected)
    mixed = tokens_in + projected * factor_three * mixed_scale
    factor_two = rms_factor(mixed)
    normed_two = (mixed * factor_two * feed_scale).astype(BF)
    normed_both = jnp.concatenate([normed_two, place.swap_core(normed_two)])
    pre = matmul(normed_both, gate_up_full)
    gate_pre, up_pre = pre[:, :half], pre[:, half:]
    hidden = (jax.nn.gelu(gate_pre, approximate=True) * up_pre).astype(BF)
    branch_both = matmul(hidden, down_full)
    branch = branch_both[:local] + place.swap_core(branch_both[local:])
    factor_four = rms_factor(branch)
    layer_out = reorder((mixed + branch * factor_four * final_scale).astype(BF), to_outside)

    branch_grad, final_term = norm_back(out_grad, branch, factor_four, final_scale)
    branch_grad = branch_grad.astype(BF)
    branch_grad_both = jnp.concatenate([branch_grad, place.swap_core(branch_grad)])
    down_terms = matmul_tn(hidden, branch_grad_both).astype(BF)
    down_weight_grad = reorder(place.scatter(down_terms, both_ways), to_outside)
    hidden_grad = matmul_nt(branch_grad_both, down_full)
    _, geglu_back = jax.vjp(
        lambda gate_in, up_in: jax.nn.gelu(gate_in, approximate=True) * up_in, gate_pre, up_pre
    )
    gate_grad, up_grad = geglu_back(hidden_grad)
    gate_up_grad = jnp.concatenate([gate_grad.astype(BF), up_grad.astype(BF)], axis=1)
    gate_up_terms = matmul_tn(normed_both, gate_up_grad).astype(BF)
    gate_up_rows = place.scatter(gate_up_terms, both_ways).reshape(2, rows, FF)
    both = cores_in_order(pick(gate_up_rows, core), place.swap_core(pick(gate_up_rows, 1 - core)))
    both = both.reshape(2, rows, 2, nx, stretch)
    both = jnp.transpose(both, (2, 1, 3, 0, 4)).reshape(2, rows, FF)
    gate_weight_grad, up_weight_grad = both[0], both[1]

    normed_two_both = matmul_nt(gate_up_grad, gate_up_full)
    normed_two_grad = normed_two_both[:local] + place.swap_core(normed_two_both[local:])
    mixed_part, feed_term = norm_back(normed_two_grad, mixed, factor_two, feed_scale)
    mixed_grad = out_grad + mixed_part
    projected_grad, mixed_term = norm_back(mixed_grad, projected, factor_three, mixed_scale)
    projected_grad = projected_grad.astype(BF)
    output_terms = matmul_tn(attended, projected_grad).astype(BF)
    attended_grad = matmul_nt(projected_grad, output_full).astype(BF)
    delta = jnp.stack(
        [
            jnp.sum(
                attended_grad[:, h * HD : (h + 1) * HD].astype(F32)
                * attended[:, h * HD : (h + 1) * HD].astype(F32),
                axis=1,
            )
            for h in range(HQ)
        ]
    ).reshape(1, -1)
    queries_grad, key_value_terms = attention.backward(
        queries, attended_grad, logs, delta, key_values
    )
    key_value_grad = place.scatter(key_value_terms, (("y",),))
    key_grad_rows = key_value_grad[:, :HD]
    values_grad = key_value_grad[:, HD:].astype(BF)
    key_back = rotate(key_grad_rows, cosine, -sine)
    key_in_grad, key_term = norm_back(key_back, key_raw, key_factor, key_scale)
    key_in_grad = key_in_grad.astype(BF)
    query_in_grad, query_term = [], 0.0
    for h in range(HQ):
        query_back = rotate(queries_grad[:, h * HD : (h + 1) * HD], cosine, -sine)
        grad, term = norm_back(query_back, query_raw[h], query_factor[h], query_scale)
        query_in_grad.append(grad.astype(BF))
        query_term = query_term + term
    quarter = HD // 2
    raw_grad = []
    for c in range(2):
        raw_grad.append(
            jnp.concatenate(
                query_in_grad[c * HQ // 2 : (c + 1) * HQ // 2]
                + [
                    key_in_grad[:, c * quarter : (c + 1) * quarter],
                    values_grad[:, c * quarter : (c + 1) * quarter],
                ],
                axis=1,
            )
        )
    normed_grad = matmul_nt(jnp.concatenate(raw_grad, axis=1), projection_full)
    tokens_part, gain_one_term = norm_back(normed_grad, tokens_in, factor_one, gain_one)
    tokens_grad = reorder((mixed_grad + tokens_part).astype(BF), to_outside)

    def chip_order(values):
        values = values.reshape(nx, 2, nw, nz, ny, -1)
        return jnp.transpose(values, (0, 2, 3, 4, 1, 5)).reshape(chips, 2, -1)

    gain_terms = jnp.concatenate(
        [t.reshape(chips, 2, -1) for t in (gain_one_term, mixed_term, feed_term, final_term)]
        + [chip_order(query_term), chip_order(key_term)],
        axis=2,
    )
    gain_terms = jnp.moveaxis(gain_terms, 1, 0).astype(BF)
    gain_terms = jnp.pad(
        gain_terms, ((0, 0), (0, 0), (0, gain_rows * head_width - gain_count))
    ).reshape(2, chips, gain_rows, head_width)
    output_terms = output_terms.reshape(nx, 2, nw * nz * ny, -1, model)
    output_terms = jnp.moveaxis(output_terms, 1, 0).reshape(2, chips, -1, head_width)
    grads_pair = jnp.stack(raw_grad)

    def terms_of(which):
        return jnp.concatenate(
            [
                matmul_tn(normed, pick(grads_pair, which)).astype(BF).reshape(chips, 2 * rows, head_width),
                pick(gain_terms, which),
                pick(output_terms, which),
            ],
            axis=1,
        ).reshape(-1, head_width)

    first_terms = terms_of(core).astype(F32) + place.swap_core(terms_of(1 - core)).astype(F32)
    first_grad = place.scatter(first_terms.astype(BF), both_ways)
    projection_rows = first_grad[: 2 * rows].reshape(2, rows, head_width)
    projection_rows = cores_in_order(
        pick(projection_rows, core), place.swap_core(pick(projection_rows, 1 - core))
    )

    def whole_columns(a, b):
        return jnp.moveaxis(projection_rows[:, :, a:b], 0, 1).reshape(rows, -1)

    query_weight_grad = whole_columns(0, heads_half)
    key_weight_grad = whole_columns(heads_half, heads_half + quarter)
    value_weight_grad = whole_columns(heads_half + quarter, head_width)
    gain_grad = first_grad[2 * rows : 2 * rows + gain_rows].reshape(-1)
    (
        attention_gain_grad,
        mixed_gain_grad,
        feed_gain_grad,
        final_gain_grad,
        query_gain_grad,
        key_gain_grad,
    ) = (gain_grad[a:b] for a, b in zip(spans[:-1], spans[1:]))
    output_weight_grad = reorder(first_grad[2 * rows + gain_rows :].reshape(-1, model), to_outside)
    return (
        layer_out,
        tokens_grad,
        attention_gain_grad,
        query_weight_grad,
        key_weight_grad,
        value_weight_grad,
        query_gain_grad,
        key_gain_grad,
        output_weight_grad,
        mixed_gain_grad,
        feed_gain_grad,
        gate_weight_grad,
        up_weight_grad,
        down_weight_grad,
        final_gain_grad,
    )


def solution(mesh):
    sizes = grid_of(mesh)
    grid = Mesh(mesh.devices.reshape(sizes), AXES)
    matrix, vector, group = P(AXES, None), P(AXES), P(("x", "core"))
    return jax.shard_map(
        lambda *arrays: body(sizes, *arrays),
        mesh=grid,
        in_specs=(
            matrix,
            vector,
            matrix,
            matrix,
            matrix,
            vector,
            vector,
            matrix,
            vector,
            vector,
            matrix,
            matrix,
            matrix,
            vector,
            group,
            group,
            matrix,
        ),
        out_specs=(
            matrix,
            matrix,
            vector,
            matrix,
            matrix,
            matrix,
            vector,
            vector,
            matrix,
            vector,
            vector,
            matrix,
            matrix,
            matrix,
            vector,
        ),
        check_vma=False,
    )
```

time: 2960 us -> 1180 us (0.40)
  waiting for transfers between devices: 2020 us -> 436 us
  blocking collectives: 373 us -> 0 us
  starting transfers between devices: 0.85 us -> 225 us
  matrix products: 267 us -> 168 us
  other arithmetic: 64.3 us -> 125 us
    unnamed x19 -> x0, waiting for transfers between devices: 1170 us -> none
    all_gather x12 -> x0, waiting for transfers between devices: 636 us -> none  [the longest x2 213 us: body(): lax.all_gather(gate_weight, ('dp', 'ctx'), axis=0, tiled=True)]
    ppermute x0 -> x102, waiting for transfers between devices: none -> 436 us  [the longest x68 302 us: shift(): return lax.ppermute(value, axis, [(i, (i + by) % n) for i in range(n)])]
    all_gather x4 -> x0, blocking collectives: 290 us -> none  [the longest x2 146 us: body(): lax.all_gather(value_weight, ('dp', 'ctx'), axis=0, tiled=True)]
    ppermute x0 -> x102, starting transfers between devices: none -> 225 us  [the longest x24 122 us: shift_wz(): return lax.ppermute(value, ('w', 'z'), pairs)]
    reduce_scatter x3 -> x0, waiting for transfers between devices: 212 us -> none  [the longest x1 106 us: body(): lax.psum_scatter(jnp.einsum('ta,td->ad', attended, projected_grad, prefer...]
    dot_general x45 -> x21, matrix products: 267 us -> 168 us  [the longest x10 62.7 us: matmul(): return jnp.dot(left, right, preferred_element_type=F32)]
    unnamed x202 -> x304, local copies, waits for them, and re-layouts: 110 us -> 22.1 us
  transfers between devices with their start and end apart: 17 -> 102, of which waited for: 14 -> 36; matrix products, arithmetic and copies ran while one was open for 13% -> 32% of each run, Pallas kernels for 0% -> 2%
where the time goes in v1:
time: 1180 us; the launch traced here: 1170 us
  waiting for transfers between devices  436 us (37%)
  starting transfers between devices  225 us (19%)
  local copies, waits for them, and re-layouts  186 us (16%)
  matrix products  168 us (14%)
  other arithmetic  125 us (11%)
  Pallas kernels  24.2 us (2%)
    ppermute x68, waiting for transfers between devices, shift(): return lax.ppermute(value, axis, [(i, (i + by) % n) for i in range(n)])  302 us
    ppermute x24, waiting for transfers between devices, shift_wz(): return lax.ppermute(value, ('w', 'z'), pairs)  130 us
    ppermute x24, starting transfers between devices, shift_wz(): return lax.ppermute(value, ('w', 'z'), pairs)  122 us
    ppermute x68, starting transfers between devices, shift(): return lax.ppermute(value, axis, [(i, (i + by) % n) for i in range(n)])  101 us
    dot_general x10, matrix products, matmul(): return jnp.dot(left, right, preferred_element_type=F32)  62.7 us
    dot_general x4, matrix products, matmul_nt(): return jnp.einsum('ij,kj->ik', left, right, preferred_element_type=F32)  57.4 us
    dynamic_update_slice x48, local copies, waits for them, and re-layouts, gather(): full = lax.dynamic_update_slice(full, block_b, (self.chip(spot) * rows, 0))  44.9 us
    dot_general x5, matrix products, matmul_tn(): return jnp.einsum('ji,jk->ik', left, right, preferred_element_type=F32)  40.1 us
  transfers between devices with their start and end apart: 102, of which 36 were waited for; matrix products, arithmetic and copies ran while one was open for 32% of the time, Pallas kernels for 2%

profile of v1, /device:TPU:0, one launch (start us, length us, event | category | flops | bytes accessed | tf_op | source)
XLA Modules:
  0.0 1167.3 jit_solution(11532273196389604990)
XLA Ops:
  116.2 7.5 collective-permute-done.29
  123.8 40.1 %collective-permute-done.33 = bf16[72,6912]{1,0:T(8,128)(2,1)} collective-permute-done((bf16[72,6912]{1,0:T(8,128)(2,1)S(1)}, bf16[72,6912]{1,0:T(8,128)(2,1)}, u32[]{:S(2)}, u32[]{:S(2)}) %collective-permute-start.33) | collective-permute-done | bytes 995360 | tf_op jit(solution)/shard_map/ppermute | solution.py:41
  164.9 31.8 %collective-permute-start.44 = (bf16[216,1152]{1,0:T(8,128)(2,1)S(1)}, bf16[216,1152]{1,0:T(8,128)(2,1)}, u32[]{:S(2)}, u32[]{:S(2)}) collective-permute-start(bf16[216,1152]{1,0:T(8,128)(2,1)S(1)} %copy-done.72), channel_id=1, source_target_pairs={{0,2},{2,4},{4,6},{6,0},{1,3},{3,5},{5,7},{7,1},{8,10},{10,12},{12... | collective-permute-start | bytes 1493000 | tf_op jit(solution)/shard_map/ppermute | solution.py:41
  210.2 9.1 collective-permute-done.28
  230.4 13.9 %collective-permute-done.31 = bf16[72,6912]{1,0:T(8,128)(2,1)S(1)} collective-permute-done((bf16[72,6912]{1,0:T(8,128)(2,1)S(1)}, bf16[72,6912]{1,0:T(8,128)(2,1)S(1)}, u32[]{:S(2)}, u32[]{:S(2)}) %collective-permute-start.31) | collective-permute-done | bytes 995360 | tf_op jit(solution)/shard_map/ppermute | solution.py:34
  246.8 8.2 collective-permute-done.43
  269.5 8.9 collective-permute-done.50
  291.9 20.4 %collective-permute-done.54 = bf16[216,1152]{1,0:T(8,128)(2,1)S(1)} collective-permute-done((bf16[216,1152]{1,0:T(8,128)(2,1)S(1)}, bf16[216,1152]{1,0:T(8,128)(2,1)S(1)}, u32[]{:S(2)}, u32[]{:S(2)}) %collective-permute-start.54) | collective-permute-done | bytes 497696 | tf_op jit(solution)/shard_map/ppermute | solution.py:34
  323.3 20.6 %collective-permute-done.55 = bf16[216,1152]{1,0:T(8,128)(2,1)S(1)} collective-permute-done((bf16[216,1152]{1,0:T(8,128)(2,1)S(1)}, bf16[216,1152]{1,0:T(8,128)(2,1)S(1)}, u32[]{:S(2)}, u32[]{:S(2)}) %collective-permute-start.55) | collective-permute-done | bytes 497696 | tf_op jit(solution)/shard_map/ppermute | solution.py:34
  350.2 12.3 %collective-permute-done.34 = bf16[72,6912]{1,0:T(8,128)(2,1)S(1)} collective-permute-done((bf16[72,6912]{1,0:T(8,128)(2,1)}, bf16[72,6912]{1,0:T(8,128)(2,1)S(1)}, u32[]{:S(2)}, u32[]{:S(2)}) %collective-permute-start.34) | collective-permute-done | bytes 995360 | tf_op jit(solution)/shard_map/ppermute | solution.py:34
  362.7 10.5 collective-permute-done.36
  373.4 8.4 maximum_select_fusion
  398.6 15.0 %collective-permute-start.18 = (bf16[512,512]{1,0:T(8,128)(2,1)}, bf16[512,512]{1,0:T(8,128)(2,1)}, u32[]{:S(2)}, u32[]{:S(2)}) collective-permute-start(bf16[512,512]{1,0:T(8,128)(2,1)} %get-tuple-element.161), channel_id=1, source_target_pairs={{0,2},{2,4},{4,6},{6,0},{1,3},{3,5},{5,7},{7,1},{8,10},{10,12},{12... | collective-permute-start | bytes 1572872 | tf_op jit(solution)/shard_map/ppermute | solution.py:41
  459.5 10.1 shard_map.289
  488.1 25.9 %fusion.68 = f32[1024,6912]{1,0:T(8,128)} fusion(bf16[1152,6912]{1,0:T(8,128)(2,1)} %constant_dynamic-update-slice_fusion.30, bf16[512,1152]{0,1:T(8,128)(2,1)S(1)} %collective-permute-done.24, bf16[512,1152]{0,1:T(8,128)(2,1)S(1)} %multiply_convert_fusion.2), kind=kOutput, calls=%fused_computation.118 | convolution fusion | flops 16312172544 | bytes 46596096 | tf_op jit(solution)/shard_map/dot_general | solution.py:153
  514.1 13.3 %multiply_convert_fusion.1 = bf16[1024,3456]{1,0:T(8,128)(2,1)} fusion(f32[1024,6912]{1,0:T(8,128)} %fusion.68), kind=kLoop, calls=%fused_computation.13 | loop fusion | flops 35389440 | bytes 35389440 | tf_op jit(solution)/shard_map/convert_element_type | solution.py:484
  527.3 12.6 %fusion.213 = f32[1024,1152]{0,1:T(8,128)} fusion(bf16[1024,3456]{1,0:T(8,128)(2,1)} %multiply_convert_fusion.1, bf16[3456,1152]{1,0:T(8,128)(2,1)S(1)} %bitcast.317), kind=kOutput, calls=%fused_computation.467 | convolution fusion | flops 8153726976 | bytes 19759104 | tf_op jit(solution)/shard_map/dot_general | solution.py:153
  560.7 12.4 %convolution_convert_fusion.1 = bf16[3456,1152]{1,0:T(8,128)(2,1)S(1)} fusion(bf16[1024,3456]{1,0:T(8,128)(2,1)} %multiply_convert_fusion.1, bf16[512,1152]{0,1:T(8,128)(2,1)} %collective-permute-done.57, bf16[512,1152]{0,1:T(8,128)(2,1)S(1)} %subtract_convert_fusion.1), kind=kOutput, calls=%fused_computation.3 | convolution fusion | flops 8162426880 | bytes 17399808 | tf_op jit(solution)/shard_map/ji,jk->ik/dot_general | solution.py:161
  584.4 25.4 %fusion.6 = (bf16[1024,3456]{1,0:T(8,128)(2,1)}, bf16[1024,3456]{1,0:T(8,128)(2,1)}) fusion(f32[1024,6912]{1,0:T(8,128)} %fusion.68, bf16[3456,1152]{1,0:T(8,128)(2,1)} %constant_dynamic-update-slice_fusion.14, bf16[512,1152]{0,1:T(8,128)(2,1)} %collective-permute-done.57, bf16[512,1152]{0,1:T(8,128)(2,1)S(1)} %subtract_convert_fusion.1), kind=kOutput, calls=%fused_computation.10 | convolution fusion | flops 8243380224 | bytes 52789248 | tf_op jit(solution)/shard_map/ij,kj->ik/dot_general | solution.py:157
  609.8 26.7 %fusion.7 = f32[1024,1152]{0,1:T(8,128)S(1)} fusion(bf16[1152,6912]{1,0:T(8,128)(2,1)} %constant_dynamic-update-slice_fusion.30, bf16[1024,3456]{1,0:T(8,128)(2,1)} %get-tuple-element.92, bf16[1024,3456]{1,0:T(8,128)(2,1)} %get-tuple-element.91), kind=kOutput, calls=%fused_computation.15 | convolution fusion | flops 16335765504 | bytes 34799616 | tf_op jit(solution)/shard_map/ij,kj->ik/dot_general | solution.py:157
  636.5 22.6 %convolution_convert_fusion = bf16[1152,6912]{1,0:T(8,128)(2,1)} fusion(bf16[1024,3456]{1,0:T(8,128)(2,1)} %get-tuple-element.92, bf16[1024,3456]{1,0:T(8,128)(2,1)} %get-tuple-element.91, bf16[512,1152]{0,1:T(8,128)(2,1)} %copy-done.127, bf16[512,1152]{0,1:T(8,128)(2,1)S(1)} %copy-done.64), kind=kOutput, calls=%fused_computation | convolution fusion | flops 16348446720 | bytes 32440320 | tf_op jit(solution)/shard_map/ji,jk->ik/dot_general | solution.py:161
  684.6 76.8 %collective-permute-done.95 = bf16[216,1152]{1,0:T(8,128)(2,1)S(1)} collective-permute-done((bf16[216,1152]{1,0:T(8,128)(2,1)S(1)}, bf16[216,1152]{1,0:T(8,128)(2,1)S(1)}, u32[]{:S(2)}, u32[]{:S(2)}) %collective-permute-start.95) | collective-permute-done | bytes 497696 | tf_op jit(solution)/shard_map/ppermute | solution.py:34
  761.4 14.6 %collective-permute-start.93 = (bf16[216,1152]{1,0:T(8,128)(2,1)S(1)}, bf16[216,1152]{1,0:T(8,128)(2,1)S(1)}, u32[]{:S(2)}, u32[]{:S(2)}) collective-permute-start(bf16[216,1152]{1,0:T(8,128)(2,1)S(1)} %fusion.83), channel_id=1, source_target_pairs={{0,6},{2,0},{4,2},{6,4},{1,7},{3,1},{5,3},{7,5},{8,14},{10,8},{12,... | collective-permute-start | bytes 1493000 | tf_op jit(solution)/shard_map/ppermute | solution.py:41
  789.8 26.8 %collective-permute-done.96 = bf16[216,1152]{1,0:T(8,128)(2,1)S(1)} collective-permute-done((bf16[216,1152]{1,0:T(8,128)(2,1)S(1)}, bf16[216,1152]{1,0:T(8,128)(2,1)S(1)}, u32[]{:S(2)}, u32[]{:S(2)}) %collective-permute-start.96) | collective-permute-done | bytes 497696 | tf_op jit(solution)/shard_map/ppermute | solution.py:41
  834.4 42.7 %collective-permute-done.88 = bf16[2,72,6912]{2,1,0:T(8,128)(2,1)} collective-permute-done((bf16[2,72,6912]{2,1,0:T(8,128)(2,1)}, bf16[2,72,6912]{2,1,0:T(8,128)(2,1)}, u32[]{:S(2)}, u32[]{:S(2)}) %collective-permute-start.88) | collective-permute-done | bytes 1990688 | tf_op jit(solution)/shard_map/ppermute | solution.py:34
  899.6 14.0 %shard_map.290 = (f32[512,1024]{1,0:T(8,128)}, bf16[4096,512]{1,0:T(8,128)(2,1)}) custom-call(s32[8]{0:T(128)} %or_select_fusion.live, bf16[512,1024]{1,0:T(8,128)(2,1)} %fusion.177.q_ref, bf16[512,1024]{1,0:T(8,128)(2,1)} %copy-done.66, f32[1,2048]{1,0:T(1,128)} %get-tuple-element.36.log_ref, f32[1,2048]{1,0:T(1,128)} %bitcast.356, ...), custom_call_target="tpu_custom_call" | custom-call | flops 13421772800 | bytes 16777216 | tf_op jit(solution)/shard_map/pallas_call | solution.py:308
  920.8 11.7 %collective-permute-start.59 = (bf16[512,512]{1,0:T(8,128)(2,1)}, bf16[512,512]{1,0:T(8,128)(2,1)}, u32[]{:S(2)}, u32[]{:S(2)}) collective-permute-start(bf16[512,512]{1,0:T(8,128)(2,1)} %get-tuple-element.114), channel_id=1, source_target_pairs={{0,1},{1,0},{2,3},{3,2},{4,5},{5,4},{6,7},{7,6},{8,9},{9,8},{10,11... | collective-permute-start | bytes 1572872 | tf_op jit(solution)/shard_map/ppermute | solution.py:34
  960.3 7.8 collective-permute-done.63
  993.9 14.8 %collective-permute-done.62 = bf16[512,512]{1,0:T(8,128)(2,1)S(1)} collective-permute-done((bf16[512,512]{1,0:T(8,128)(2,1)S(1)}, bf16[512,512]{1,0:T(8,128)(2,1)S(1)}, u32[]{:S(2)}, u32[]{:S(2)}) %collective-permute-start.62) | collective-permute-done | bytes 524320 | tf_op jit(solution)/shard_map/ppermute | solution.py:41
  1008.6 27.1 %collective-permute-start.87 = (bf16[72,6912]{1,0:T(8,128)(2,1)}, bf16[72,6912]{1,0:T(8,128)(2,1)}, u32[]{:S(2)}, u32[]{:S(2)}) collective-permute-start(bf16[72,6912]{1,0:T(8,128)(2,1)} %fusion.64), channel_id=1, source_target_pairs={{0,2},{2,4},{4,6},{6,0},{1,3},{3,5},{5,7},{7,1},{8,10},{10,12},{12... | collective-permute-start | bytes 2985992 | tf_op jit(solution)/shard_map/ppermute | solution.py:41
  1058.9 29.1 %collective-permute-done.84 = bf16[72,6912]{1,0:T(8,128)(2,1)} collective-permute-done((bf16[72,6912]{1,0:T(8,128)(2,1)}, bf16[72,6912]{1,0:T(8,128)(2,1)}, u32[]{:S(2)}, u32[]{:S(2)}) %collective-permute-start.84) | collective-permute-done | bytes 995360 | tf_op jit(solution)/shard_map/ppermute | solution.py:41
  1124.5 8.0 collective-permute-done.73
  (754 shorter events, 535.2 us)
Async XLA Ops:
  11.2 78.1 %collective-permute-start.25 = (bf16[36,6912]{1,0:T(8,128)(2,1)}, bf16[36,6912]{1,0:T(8,128)(2,1)}, u32[]{:S(2)}, u32[]{:S(2)}) collective-permute-start(bf16[36,6912]{1,0:T(8,128)(2,1)} %reshape.602), channel_id=1, source_target_pairs={{0,8},{8,0},{1,9},{9,1},{2,10},{10,2},{3,11},{11,3},{4,12},{12,4},... | collective-permute-start | bytes 1493000 | tf_op jit(solution)/shard_map/ppermute | solution.py:44
  96.9 66.9 %collective-permute-start.33 = (bf16[72,6912]{1,0:T(8,128)(2,1)S(1)}, bf16[72,6912]{1,0:T(8,128)(2,1)}, u32[]{:S(2)}, u32[]{:S(2)}) collective-permute-start(bf16[72,6912]{1,0:T(8,128)(2,1)S(1)} %copy-done.34), channel_id=1, source_target_pairs={{0,4},{2,6},{4,0},{6,2},{1,5},{3,7},{5,1},{7,3},{8,12},{10,14},{12... | collective-permute-start | bytes 2985992 | tf_op jit(solution)/shard_map/ppermute | solution.py:41
  97.2 66.7 %collective-permute-start.37 = (bf16[72,6912]{1,0:T(8,128)(2,1)S(1)}, bf16[72,6912]{1,0:T(8,128)(2,1)S(1)}, u32[]{:S(2)}, u32[]{:S(2)}) collective-permute-start(bf16[72,6912]{1,0:T(8,128)(2,1)S(1)} %copy-done.34), channel_id=1, source_target_pairs={{0,6},{2,0},{4,2},{6,4},{1,7},{3,1},{5,3},{7,5},{8,14},{10,8},{12,... | collective-permute-start | bytes 2985992 | tf_op jit(solution)/shard_map/ppermute | solution.py:41
  100.8 95.9 %collective-permute-start.26 = (bf16[72,6912]{1,0:T(8,128)(2,1)S(1)}, bf16[72,6912]{1,0:T(8,128)(2,1)S(1)}, u32[]{:S(2)}, u32[]{:S(2)}) collective-permute-start(bf16[72,6912]{1,0:T(8,128)(2,1)S(1)} %copy-done.34), channel_id=1, source_target_pairs={{0,1},{1,0},{2,3},{3,2},{4,5},{5,4},{6,7},{7,6},{8,9},{9,8},{10,11... | collective-permute-start | bytes 2985992 | tf_op jit(solution)/shard_map/ppermute | solution.py:34
  101.4 95.3 %collective-permute-start.27 = (bf16[72,6912]{1,0:T(8,128)(2,1)S(1)}, bf16[72,6912]{1,0:T(8,128)(2,1)S(1)}, u32[]{:S(2)}, u32[]{:S(2)}) collective-permute-start(bf16[72,6912]{1,0:T(8,128)(2,1)S(1)} %copy-done.34), channel_id=1, source_target_pairs={{0,16},{16,0},{1,17},{17,1},{2,18},{18,2},{3,19},{19,3},{4,20},{20... | collective-permute-start | bytes 2985992 | tf_op jit(solution)/shard_map/ppermute | solution.py:34
  164.9 55.7 %collective-permute-start.44 = (bf16[216,1152]{1,0:T(8,128)(2,1)S(1)}, bf16[216,1152]{1,0:T(8,128)(2,1)}, u32[]{:S(2)}, u32[]{:S(2)}) collective-permute-start(bf16[216,1152]{1,0:T(8,128)(2,1)S(1)} %copy-done.72), channel_id=1, source_target_pairs={{0,2},{2,4},{4,6},{6,0},{1,3},{3,5},{5,7},{7,1},{8,10},{10,12},{12... | collective-permute-start | bytes 1493000 | tf_op jit(solution)/shard_map/ppermute | solution.py:41
  196.7 48.7 %collective-permute-start.48 = (bf16[216,1152]{1,0:T(8,128)(2,1)S(1)}, bf16[216,1152]{1,0:T(8,128)(2,1)}, u32[]{:S(2)}, u32[]{:S(2)}) collective-permute-start(bf16[216,1152]{1,0:T(8,128)(2,1)S(1)} %copy-done.72), channel_id=1, source_target_pairs={{0,4},{2,6},{4,0},{6,2},{1,5},{3,7},{5,1},{7,3},{8,12},{10,14},{12... | collective-permute-start | bytes 1493000 | tf_op jit(solution)/shard_map/ppermute | solution.py:41
  202.9 65.8 %collective-permute-start.52 = (bf16[216,1152]{1,0:T(8,128)(2,1)S(1)}, bf16[216,1152]{1,0:T(8,128)(2,1)S(1)}, u32[]{:S(2)}, u32[]{:S(2)}) collective-permute-start(bf16[216,1152]{1,0:T(8,128)(2,1)S(1)} %copy-done.72), channel_id=1, source_target_pairs={{0,6},{2,0},{4,2},{6,4},{1,7},{3,1},{5,3},{7,5},{8,14},{10,8},{12,... | collective-permute-start | bytes 1493000 | tf_op jit(solution)/shard_map/ppermute | solution.py:41
  245.5 99.5 %collective-permute-start.35 = (bf16[72,6912]{1,0:T(8,128)(2,1)}, bf16[72,6912]{1,0:T(8,128)(2,1)S(1)}, u32[]{:S(2)}, u32[]{:S(2)}) collective-permute-start(bf16[72,6912]{1,0:T(8,128)(2,1)} %collective-permute-done.33), channel_id=1, source_target_pairs={{0,16},{16,0},{1,17},{17,1},{2,18},{18,2},{3,19},{19,3},{4,20},{20... | collective-permute-start | bytes 2985992 | tf_op jit(solution)/shard_map/ppermute | solution.py:34
  268.7 77.7 %collective-permute-start.39 = (bf16[72,6912]{1,0:T(8,128)(2,1)S(1)}, bf16[72,6912]{1,0:T(8,128)(2,1)}, u32[]{:S(2)}, u32[]{:S(2)}) collective-permute-start(bf16[72,6912]{1,0:T(8,128)(2,1)S(1)} %collective-permute-done.37), channel_id=1, source_target_pairs={{0,1},{1,0},{2,3},{3,2},{4,5},{5,4},{6,7},{7,6},{8,9},{9,8},{10,11... | collective-permute-start | bytes 2985992 | tf_op jit(solution)/shard_map/ppermute | solution.py:34
  321.6 51.9 %collective-permute-start.16 = (bf16[2048,768]{1,0:T(8,128)(2,1)}, bf16[2048,768]{1,0:T(8,128)(2,1)S(1)}, u32[]{:S(2)}, u32[]{:S(2)}) collective-permute-start(bf16[2048,768]{1,0:T(8,128)(2,1)} %constant_dynamic-update-slice_fusion.54), channel_id=1, source_target_pairs={{0,8},{8,0},{1,9},{9,1},{2,10},{10,2},{3,11},{11,3},{4,12},{12,4},... | collective-permute-start | bytes 9437192 | tf_op jit(solution)/shard_map/ppermute | solution.py:44
  348.5 137.4 %collective-permute-start.40 = (bf16[72,6912]{1,0:T(8,128)(2,1)}, bf16[72,6912]{1,0:T(8,128)(2,1)}, u32[]{:S(2)}, u32[]{:S(2)}) collective-permute-start(bf16[72,6912]{1,0:T(8,128)(2,1)} %collective-permute-done.39), channel_id=1, source_target_pairs={{0,16},{16,0},{1,17},{17,1},{2,18},{18,2},{3,19},{19,3},{4,20},{20... | collective-permute-start | bytes 2985992 | tf_op jit(solution)/shard_map/ppermute | solution.py:34
  397.8 49.5 %collective-permute-start.17 = (bf16[512,512]{1,0:T(8,128)(2,1)}, bf16[512,512]{1,0:T(8,128)(2,1)}, u32[]{:S(2)}, u32[]{:S(2)}) collective-permute-start(bf16[512,512]{1,0:T(8,128)(2,1)} %get-tuple-element.161), channel_id=1, source_target_pairs={{0,1},{1,0},{2,3},{3,2},{4,5},{5,4},{6,7},{7,6},{8,9},{9,8},{10,11... | collective-permute-start | bytes 1572872 | tf_op jit(solution)/shard_map/ppermute | solution.py:34
  574.9 90.4 %collective-permute-start.91 = (bf16[2,216,1152]{2,1,0:T(8,128)(2,1)}, bf16[2,216,1152]{2,1,0:T(8,128)(2,1)}, u32[]{:S(2)}, u32[]{:S(2)}) collective-permute-start(bf16[2,216,1152]{2,1,0:T(8,128)(2,1)} %get-tuple-element.103), channel_id=1, source_target_pairs={{0,16},{16,0},{1,17},{17,1},{2,18},{18,2},{3,19},{19,3},{4,20},{20... | collective-permute-start | bytes 2985992 | tf_op jit(solution)/shard_map/ppermute | solution.py:34
  576.0 89.5 %collective-permute-start.97 = (bf16[2,216,1152]{2,1,0:T(8,128)(2,1)}, bf16[2,216,1152]{2,1,0:T(8,128)(2,1)}, u32[]{:S(2)}, u32[]{:S(2)}) collective-permute-start(bf16[2,216,1152]{2,1,0:T(8,128)(2,1)} %get-tuple-element.104), channel_id=1, source_target_pairs={{0,16},{16,0},{1,17},{17,1},{2,18},{18,2},{3,19},{19,3},{4,20},{20... | collective-permute-start | bytes 2985992 | tf_op jit(solution)/shard_map/ppermute | solution.py:34
  578.4 91.9 %collective-permute-start.100 = (bf16[2,216,1152]{2,1,0:T(8,128)(2,1)}, bf16[2,216,1152]{2,1,0:T(8,128)(2,1)}, u32[]{:S(2)}, u32[]{:S(2)}) collective-permute-start(bf16[2,216,1152]{2,1,0:T(8,128)(2,1)} %get-tuple-element.108), channel_id=1, source_target_pairs={{0,1},{1,0},{2,3},{3,2},{4,5},{5,4},{6,7},{7,6},{8,9},{9,8},{10,11... | collective-permute-start | bytes 2985992 | tf_op jit(solution)/shard_map/ppermute | solution.py:34
  584.4 85.9 %collective-permute-start.94 = (bf16[2,216,1152]{2,1,0:T(8,128)(2,1)}, bf16[2,216,1152]{2,1,0:T(8,128)(2,1)}, u32[]{:S(2)}, u32[]{:S(2)}) collective-permute-start(bf16[2,216,1152]{2,1,0:T(8,128)(2,1)} %get-tuple-element.107), channel_id=1, source_target_pairs={{0,1},{1,0},{2,3},{3,2},{4,5},{5,4},{6,7},{7,6},{8,9},{9,8},{10,11... | collective-permute-start | bytes 2985992 | tf_op jit(solution)/shard_map/ppermute | solution.py:34
  661.7 160.9 %collective-permute-start.79 = (bf16[2,72,6912]{2,1,0:T(8,128)(2,1)S(1)}, bf16[2,72,6912]{2,1,0:T(8,128)(2,1)S(1)}, u32[]{:S(2)}, u32[]{:S(2)}) collective-permute-start(bf16[2,72,6912]{2,1,0:T(8,128)(2,1)S(1)} %get-tuple-element.95), channel_id=1, source_target_pairs={{0,16},{16,0},{1,17},{17,1},{2,18},{18,2},{3,19},{19,3},{4,20},{20... | collective-permute-start | bytes 5971976 | tf_op jit(solution)/shard_map/ppermute | solution.py:34
  665.3 157.4 %collective-permute-start.85 = (bf16[2,72,6912]{2,1,0:T(8,128)(2,1)S(1)}, bf16[2,72,6912]{2,1,0:T(8,128)(2,1)S(1)}, u32[]{:S(2)}, u32[]{:S(2)}) collective-permute-start(bf16[2,72,6912]{2,1,0:T(8,128)(2,1)S(1)} %get-tuple-element.96), channel_id=1, source_target_pairs={{0,16},{16,0},{1,17},{17,1},{2,18},{18,2},{3,19},{19,3},{4,20},{20... | collective-permute-start | bytes 5971976 | tf_op jit(solution)/shard_map/ppermute | solution.py:34
  672.9 88.5 %collective-permute-start.95 = (bf16[216,1152]{1,0:T(8,128)(2,1)S(1)}, bf16[216,1152]{1,0:T(8,128)(2,1)S(1)}, u32[]{:S(2)}, u32[]{:S(2)}) collective-permute-start(bf16[216,1152]{1,0:T(8,128)(2,1)S(1)} %dynamic-slice_bitcast_fusion.21), channel_id=1, source_target_pairs={{0,16},{16,0},{1,17},{17,1},{2,18},{18,2},{3,19},{19,3},{4,20},{20... | collective-permute-start | bytes 1493000 | tf_op jit(solution)/shard_map/ppermute | solution.py:34
  674.9 101.2 %collective-permute-start.98 = (bf16[216,1152]{1,0:T(8,128)(2,1)S(1)}, bf16[216,1152]{1,0:T(8,128)(2,1)S(1)}, u32[]{:S(2)}, u32[]{:S(2)}) collective-permute-start(bf16[216,1152]{1,0:T(8,128)(2,1)S(1)} %dynamic-slice_bitcast_fusion.20), channel_id=1, source_target_pairs={{0,1},{1,0},{2,3},{3,2},{4,5},{5,4},{6,7},{7,6},{8,9},{9,8},{10,11... | collective-permute-start | bytes 1493000 | tf_op jit(solution)/shard_map/ppermute | solution.py:34
  682.6 94.2 %collective-permute-start.101 = (bf16[216,1152]{1,0:T(8,128)(2,1)S(1)}, bf16[216,1152]{1,0:T(8,128)(2,1)S(1)}, u32[]{:S(2)}, u32[]{:S(2)}) collective-permute-start(bf16[216,1152]{1,0:T(8,128)(2,1)S(1)} %dynamic-slice_bitcast_fusion.19), channel_id=1, source_target_pairs={{0,16},{16,0},{1,17},{17,1},{2,18},{18,2},{3,19},{19,3},{4,20},{20... | collective-permute-start | bytes 1493000 | tf_op jit(solution)/shard_map/ppermute | solution.py:34
  816.6 60.5 %collective-permute-start.88 = (bf16[2,72,6912]{2,1,0:T(8,128)(2,1)}, bf16[2,72,6912]{2,1,0:T(8,128)(2,1)}, u32[]{:S(2)}, u32[]{:S(2)}) collective-permute-start(bf16[2,72,6912]{2,1,0:T(8,128)(2,1)} %get-tuple-element.100), channel_id=1, source_target_pairs={{0,1},{1,0},{2,3},{3,2},{4,5},{5,4},{6,7},{7,6},{8,9},{9,8},{10,11... | collective-permute-start | bytes 5971976 | tf_op jit(solution)/shard_map/ppermute | solution.py:34
  817.4 70.7 %collective-permute-start.58 = (f32[512,1152]{0,1:T(8,128)}, f32[512,1152]{0,1:T(8,128)S(1)}, u32[]{:S(2)}, u32[]{:S(2)}) collective-permute-start(f32[512,1152]{0,1:T(8,128)} %slice.363), channel_id=1, source_target_pairs={{0,8},{8,0},{1,9},{9,1},{2,10},{10,2},{3,11},{11,3},{4,12},{12,4},... | collective-permute-start | bytes 7077896 | tf_op jit(solution)/shard_map/ppermute | solution.py:44
  830.9 141.6 %collective-permute-start.80 = (bf16[72,6912]{1,0:T(8,128)(2,1)}, bf16[72,6912]{1,0:T(8,128)(2,1)}, u32[]{:S(2)}, u32[]{:S(2)}) collective-permute-start(bf16[72,6912]{1,0:T(8,128)(2,1)} %dynamic-slice_bitcast_fusion.14), channel_id=1, source_target_pairs={{0,1},{1,0},{2,3},{3,2},{4,5},{5,4},{6,7},{7,6},{8,9},{9,8},{10,11... | collective-permute-start | bytes 2985992 | tf_op jit(solution)/shard_map/ppermute | solution.py:34
  884.6 96.2 %collective-permute-start.83 = (bf16[72,6912]{1,0:T(8,128)(2,1)}, bf16[72,6912]{1,0:T(8,128)(2,1)}, u32[]{:S(2)}, u32[]{:S(2)}) collective-permute-start(bf16[72,6912]{1,0:T(8,128)(2,1)} %dynamic-slice_bitcast_fusion.13), channel_id=1, source_target_pairs={{0,16},{16,0},{1,17},{17,1},{2,18},{18,2},{3,19},{19,3},{4,20},{20... | collective-permute-start | bytes 2985992 | tf_op jit(solution)/shard_map/ppermute | solution.py:34
  956.9 102.0 %collective-permute-start.89 = (bf16[72,6912]{1,0:T(8,128)(2,1)}, bf16[72,6912]{1,0:T(8,128)(2,1)}, u32[]{:S(2)}, u32[]{:S(2)}) collective-permute-start(bf16[72,6912]{1,0:T(8,128)(2,1)} %dynamic-slice_bitcast_fusion.11), channel_id=1, source_target_pairs={{0,16},{16,0},{1,17},{17,1},{2,18},{18,2},{3,19},{19,3},{4,20},{20... | collective-permute-start | bytes 2985992 | tf_op jit(solution)/shard_map/ppermute | solution.py:34
  988.3 47.5 %collective-permute-start.64 = (bf16[512,512]{1,0:T(8,128)(2,1)S(1)}, bf16[512,512]{1,0:T(8,128)(2,1)S(1)}, u32[]{:S(2)}, u32[]{:S(2)}) collective-permute-start(bf16[512,512]{1,0:T(8,128)(2,1)S(1)} %get-tuple-element.112), channel_id=1, source_target_pairs={{0,2},{2,4},{4,6},{6,0},{1,3},{3,5},{5,7},{7,1},{8,10},{10,12},{12... | collective-permute-start | bytes 1572872 | tf_op jit(solution)/shard_map/ppermute | solution.py:41
  993.9 65.0 %collective-permute-start.81 = (bf16[72,6912]{1,0:T(8,128)(2,1)}, bf16[72,6912]{1,0:T(8,128)(2,1)}, u32[]{:S(2)}, u32[]{:S(2)}) collective-permute-start(bf16[72,6912]{1,0:T(8,128)(2,1)} %fusion.66), channel_id=1, source_target_pairs={{0,6},{2,0},{4,2},{6,4},{1,7},{3,1},{5,3},{7,5},{8,14},{10,8},{12,... | collective-permute-start | bytes 2985992 | tf_op jit(solution)/shard_map/ppermute | solution.py:41
  993.9 94.2 %collective-permute-start.84 = (bf16[72,6912]{1,0:T(8,128)(2,1)}, bf16[72,6912]{1,0:T(8,128)(2,1)}, u32[]{:S(2)}, u32[]{:S(2)}) collective-permute-start(bf16[72,6912]{1,0:T(8,128)(2,1)} %fusion.65), channel_id=1, source_target_pairs={{0,4},{2,6},{4,0},{6,2},{1,5},{3,7},{5,1},{7,3},{8,12},{10,14},{12... | collective-permute-start | bytes 2985992 | tf_op jit(solution)/shard_map/ppermute | solution.py:41
  1008.6 79.4 %collective-permute-start.87 = (bf16[72,6912]{1,0:T(8,128)(2,1)}, bf16[72,6912]{1,0:T(8,128)(2,1)}, u32[]{:S(2)}, u32[]{:S(2)}) collective-permute-start(bf16[72,6912]{1,0:T(8,128)(2,1)} %fusion.64), channel_id=1, source_target_pairs={{0,2},{2,4},{4,6},{6,0},{1,3},{3,5},{5,7},{7,1},{8,10},{10,12},{12... | collective-permute-start | bytes 2985992 | tf_op jit(solution)/shard_map/ppermute | solution.py:41
  1056.5 52.2 %collective-permute-start.66 = (bf16[2048,768]{1,0:T(8,128)(2,1)}, bf16[2048,768]{1,0:T(8,128)(2,1)}, u32[]{:S(2)}, u32[]{:S(2)}) collective-permute-start(bf16[2048,768]{1,0:T(8,128)(2,1)} %bitcast.52), channel_id=1, source_target_pairs={{0,8},{8,0},{1,9},{9,1},{2,10},{10,2},{3,11},{11,3},{4,12},{12,4},... | collective-permute-start | bytes 9437192 | tf_op jit(solution)/shard_map/ppermute | solution.py:44
  (215 other events, 5083.2 us)

commit v2 on v1

--- a/solution.py
+++ b/solution.py
@@ -46,35 +46,118 @@
     def wz_steps(self):
         return [(kw, kz) for kw in range(self.size["w"]) for kz in range(self.size["z"])]
 
-    def chip(self, spot):
-        size = self.size
-        return ((spot["x"] * size["w"] + spot["w"]) * size["z"] + spot["z"]) * size["y"] + spot["y"]
+    def gather_wz(self, own):
+        return [own if kw == kz == 0 else self.shift_wz(own, kw, kz) for kw, kz in self.wz_steps()]
+
+    def gather_line(self, own):
+        return lax.all_gather(own, ("core", "w", "z"), axis=0, tiled=True)
+
+    def cores_summed(self, full):
+        full = full.reshape(2, -1, full.shape[-1])
+        give = self.swap_core(lax.dynamic_index_in_dim(full, 1 - self.at["core"], 0, keepdims=False))
+        keep = lax.dynamic_index_in_dim(full, self.at["core"], 0, keepdims=False)
+        return (keep.astype(F32) + give.astype(F32)).astype(BF)
+
+    def scatter_line(self, rows):
+        return lax.psum_scatter(rows, ("w", "z"), scatter_dimension=0, tiled=True)
+
+    def plane_steps(self):
+        return [(dx, dy) for dx in range(self.size["x"]) for dy in range(self.size["y"])]
+
+    def gather_near(self, own):
+        blocks = {(0, 0): own}
+        for dx in range(1, self.size["x"]):
+            blocks[dx, 0] = self.shift(own, "x", dx)
+        for dy in range(1, self.size["y"]):
+            blocks[0, dy] = self.shift(own, "y", dy)
+        return blocks
+
+    def gather_far(self, near, *hold):
+        blocks = {step: after(block, *hold) if hold else block for step, block in near.items()}
+        cut = blocks[0, 0].shape[0] // 2
+        for dx, dy in self.plane_steps():
+            if dx and dy:
+                top = self.shift(blocks[dx, 0][:cut], "y", dy)
+                low = self.shift(blocks[0, dy][cut:], "x", dx)
+                blocks[dx, dy] = jnp.concatenate([top, low])
+        return [blocks[step] for step in self.plane_steps()]
+
+    def scatter_plane(self, parts):
+        parts = dict(zip(self.plane_steps(), parts))
+        cut = parts[0, 0].shape[0] // 2
+        tops = {d: parts[d, 0][:cut] for d in range(self.size["x"])}
+        lows = {d: parts[0, d][cut:] for d in range(self.size["y"])}
+        own_top, own_low = parts[0, 0][:cut], parts[0, 0][cut:]
+        for dx in range(1, self.size["x"]):
+            own_low = own_low + self.shift(parts[dx, 0][cut:].astype(BF), "x", -dx).astype(F32)
+        for dy in range(1, self.size["y"]):
+            own_top = own_top + self.shift(parts[0, dy][:cut].astype(BF), "y", -dy).astype(F32)
+        for dx, dy in self.plane_steps():
+            if dx and dy:
+                part = parts[dx, dy].astype(BF)
+                tops[dx] = tops[dx] + self.shift(part[:cut], "y", -dy).astype(F32)
+                lows[dy] = lows[dy] + self.shift(part[cut:], "x", -dx).astype(F32)
+        self.halfway = [tops[self.size["x"] - 1], lows[self.size["y"] - 1]]
+        for dx in range(1, self.size["x"]):
+            own_top = own_top + self.shift(tops[dx].astype(BF), "x", -dx).astype(F32)
+        for dy in range(1, self.size["y"]):
+            own_low = own_low + self.shift(lows[dy].astype(BF), "y", -dy).astype(F32)
+        return jnp.concatenate([own_top, own_low])
+
+    def deal_plane(self, pieces, hold=(), hold_end=()):
+        for dim, axis in ((0, "x"), (1, "y")):
+            n, here = self.size[axis], self.at[axis]
+            dealt = []
+            for d in range(n):
+                piece = lax.dynamic_index_in_dim(pieces, (here + d) % n, dim)
+                dealt.append(piece if d == 0 else self.shift(piece, axis, d))
+            wait_for = hold if axis == "x" else hold_end
+            if wait_for:
+                dealt = [after(piece, *wait_for) for piece in dealt]
+            if n == 2:
+                own, other = dealt
+                low = jnp.where(here == 0, own, other)
+                pieces = jnp.concatenate([low, jnp.where(here == 0, other, own)], axis=dim)
+            else:
+                pieces = jnp.zeros_like(pieces)
+                for d in range(n):
+                    pieces = lax.dynamic_update_slice_in_dim(pieces, dealt[d], (here - d) % n, dim)
+        return pieces
 
     def ctx_chip(self, spot):
         return (spot["w"] * self.size["z"] + spot["z"]) * self.size["y"] + spot["y"]
 
-    def gather(self, own, orders, after=None):
+    def gather_chips(self, own):
         size, at = self.size, self.at
-        rows = own.shape[0]
-        chips = size["x"] * size["w"] * size["z"] * size["y"]
-        full = jnp.zeros((chips * rows, own.shape[1]), own.dtype)
-        came = []
-        if after is not None:
-            own, _ = lax.optimization_barrier((own, after))
-        for number, (kw, kz) in enumerate(self.wz_steps()):
-            block = own if kw == kz == 0 else self.shift_wz(own, kw, kz)
+        rows, width = own.shape
+        line = size["w"] * size["z"] * rows
+        mine = jnp.zeros((line, width), own.dtype)
+        for block, (kw, kz) in zip(self.gather_wz(own), self.wz_steps()):
+            w, z = (at["w"] - kw) % size["w"], (at["z"] - kz) % size["z"]
+            mine = lax.dynamic_update_slice(mine, block, ((w * size["z"] + z) * rows, 0))
+        full = jnp.zeros((size["x"] * size["y"] * line, width), own.dtype)
+        near = self.gather_near(mine)
+        for block, (dx, dy) in zip(self.gather_far(near), self.plane_steps()):
+            x, y = (at["x"] - dx) % size["x"], (at["y"] - dy) % size["y"]
+            full = lax.dynamic_update_slice(full, block, ((x * size["y"] + y) * line, 0))
+        return full, mine, list(near.values())
+
+    def scatter_chips(self, full):
+        size, at = self.size, self.at
+        full = full.reshape((size["x"], size["y"], -1, full.shape[-1]))
+        parts = [
+            full[(at["x"] - dx) % size["x"], (at["y"] - dy) % size["y"]].astype(F32)
+            for dx, dy in self.plane_steps()
+        ]
+        mine = self.scatter_plane(parts)
+        mine = mine.reshape((size["w"], size["z"], -1, mine.shape[-1]))
+        total = None
+        for kw, kz in reversed(self.wz_steps()):
+            part = mine[(at["w"] + kw) % size["w"], (at["z"] + kz) % size["z"]]
             if kw or kz:
-                came.append(block)
-            spot = {"w": (at["w"] - kw) % size["w"], "z": (at["z"] - kz) % size["z"]}
-            first, second = orders[number % len(orders)]
-            for ka in range(size[first]):
-                block_a = block if ka == 0 else self.shift(block, first, ka)
-                spot[first] = (at[first] - ka) % size[first]
-                for kb in range(size[second]):
-                    block_b = block_a if kb == 0 else self.shift(block_a, second, kb)
-                    spot[second] = (at[second] - kb) % size[second]
-                    full = lax.dynamic_update_slice(full, block_b, (self.chip(spot) * rows, 0))
-        return full, came
+                part = self.shift_wz(part.astype(BF), kw, kz).astype(F32)
+            total = part if total is None else total + part
+        return total
 
     def gather_group(self, own):
         size, at = self.size, self.at
@@ -85,40 +168,35 @@
             spot = {"w": (at["w"] - kw) % size["w"], "z": (at["z"] - kz) % size["z"]}
             for ky in range(size["y"]):
                 block_y = block if ky == 0 else self.shift(block, "y", ky)
+                came = block_y if kw == kz == 0 else came
                 spot["y"] = (at["y"] - ky) % size["y"]
                 full = lax.dynamic_update_slice(full, block_y, (self.ctx_chip(spot) * rows, 0))
-        return full
-
-    def scatter(self, full, orders):
+        return full, came
+
+    def scatter_group(self, full, meanwhile):
         size, at = self.size, self.at
-        lead = ("x", "w", "z", "y") if "x" in orders[0] else ("w", "z", "y")
-        grid = tuple(size[a] for a in lead)
-        full = full.reshape(grid + (-1, full.shape[-1]))
-        total = None
-        for number, (kw, kz) in reversed(list(enumerate(self.wz_steps()))):
-            spot = {"w": (at["w"] + kw) % size["w"], "z": (at["z"] + kz) % size["z"]}
-            names = [a for a in lead if a not in spot]
-            part = lax.dynamic_slice(
-                full,
-                tuple(spot.get(a, 0) for a in lead) + (0, 0),
-                tuple(1 if a in spot else size[a] for a in lead) + full.shape[-2:],
-            ).reshape(tuple(size[a] for a in names) + full.shape[-2:])
-            for axis in reversed(orders[number % len(orders)]):
-                dim, n = names.index(axis), size[axis]
-                names.remove(axis)
-
-                def take(k):
-                    return lax.dynamic_index_in_dim(part, (at[axis] + k) % n, dim, keepdims=False)
-
-                acc = take(0).astype(F32)
-                for k in range(1, n):
-                    acc = acc + self.shift(take(k), axis, k).astype(F32)
-                if names:
-                    part = acc.astype(BF)
+        full = full.reshape((size["w"], size["z"], size["y"], -1, full.shape[-1]))
+        steps = sorted(self.wz_steps(), key=lambda k: (k == (0, 0), abs(k[1] - size["z"] // 2)))
+        total, came, gone = None, None, []
+        for kw, kz in steps:
+            part = full[(at["w"] + kw) % size["w"], (at["z"] + kz) % size["z"]]
+            acc = part[at["y"]].astype(F32)
+            for dy in range(1, size["y"]):
+                other = self.shift(part[(at["y"] + dy) % size["y"]], "y", dy)
+                if came is None:
+                    came = other
+                    done = meanwhile(came)
+                acc = acc + after(other, *gone).astype(F32) if gone else acc + other.astype(F32)
             if kw or kz:
-                acc = self.shift_wz(acc.astype(BF), kw, kz).astype(F32)
+                acc = self.shift_wz(acc.astype(BF), kw, kz)
+                gone = gone or [acc, done]
+                acc = acc.astype(F32)
             total = acc if total is None else total + acc
-        return total
+        return total, came
+
+
+def after(value, *others):
+    return lax.optimization_barrier((value,) + others)[0]
 
 
 def rms_factor(values):
@@ -358,12 +436,9 @@
     local, model = tokens.shape
     rows = query_weight.shape[0]
     wide = HQ * HD
-    half = FF // 2
-    stretch = half // nx
     offset = place.ctx_chip(place.at) * local
     query_pos = lax.dynamic_slice_in_dim(positions, offset, local)
     query_seg = lax.dynamic_slice_in_dim(segment_ids, offset, local)
-    both_ways = (("x", "y"), ("y", "x"))
 
     def pick(pair, which):
         return lax.dynamic_index_in_dim(pair, which, 0, keepdims=False)
@@ -371,11 +446,19 @@
     def cores_in_order(own, other):
         return jnp.where(core == 0, jnp.stack([own, other]), jnp.stack([other, own]))
 
-    inside = np.arange(model).reshape(nx, 2, nw, nz, ny, rows).transpose(0, 2, 3, 4, 1, 5).reshape(-1)
-    order = jnp.asarray(inside, jnp.int32)
-    counting = lax.iota(jnp.int32, model)
-    to_inside = (counting[:, None] == order[None, :]).astype(BF)
-    to_outside = (order[:, None] == counting[None, :]).astype(BF)
+    outside = np.arange(model).reshape(nx, 2, nw, nz, ny, rows)
+    inside = outside.transpose(1, 2, 3, 0, 4, 5).reshape(-1)
+    first = outside.transpose(0, 4, 2, 3, 1, 5).reshape(-1)
+
+    def order_change(source, target):
+        at = jnp.asarray(np.argsort(source)[target], jnp.int32)
+        return (lax.iota(jnp.int32, model)[:, None] == at[None, :]).astype(BF)
+
+    outside = np.arange(model)
+    to_inside = order_change(outside, inside)
+    to_outside = order_change(inside, outside)
+    to_first = order_change(outside, first)
+    inside_from_first = order_change(inside, first)
 
     def reorder(values, matrix):
         if values.dtype == F32:
@@ -389,7 +472,7 @@
 
     head_width = wide // 2 + HD
     gains = jnp.concatenate(
-        [attention_gain, mixed_gain, feed_gain, final_gain, query_gain, key_gain]
+        [mixed_gain, feed_gain, final_gain, query_gain, key_gain, attention_gain]
     )
     gain_count = gains.size
     projections = column_halves(query_weight, key_weight, value_weight)
@@ -406,51 +489,63 @@
             small,
         ]
     )
-    first_all, first_came = place.gather(first_own, both_ways)
-    first_all = cores_in_order(first_all, place.swap_core(first_all)).reshape(
-        2, chips, first_own.shape[0], head_width
-    )
-    projection_full = first_all[:, :, : 2 * rows].reshape(2, model, head_width)
-    projection_full = jnp.concatenate([projection_full[0], projection_full[1]], axis=1)
-    gains_all = first_all[:, :, 2 * rows].reshape(2, chips, head_width)[:, :, :gain_count]
+    first_all, first_came, next_came = place.gather_chips(first_own)
+
+    gate_weight, up_weight, down_weight, tokens, cotangent, _ = lax.optimization_barrier(
+        (gate_weight, up_weight, down_weight, tokens, cotangent, first_own)
+    )
+    part = FF // (nx * ny)
+    gate_up = jnp.stack([gate_weight, up_weight]).reshape(2, rows, nx, 2 * nw * nz, ny, -1)
+    gate_up = jnp.transpose(gate_up, (2, 4, 0, 1, 3, 5)).reshape(nx, ny, 2, rows, part)
+    down_own = reorder(down_weight, to_inside)
+    gate_up = place.deal_plane(gate_up, [first_came], next_came)
+    gate_own, up_own = (gate_up[:, :, i].reshape(-1, part) for i in range(2))
+    gate_full = place.gather_line(gate_own)
+    first_other = place.swap_core(first_all)
+
+    def in_order(own, other):
+        return jnp.where(core == 0, own, other), jnp.where(core == 0, other, own)
+
+    first_all, first_other = (
+        block.reshape(chips, first_own.shape[0], head_width) for block in (first_all, first_other)
+    )
+    projections = tuple(
+        block[:, : 2 * rows].reshape(model, head_width) for block in (first_all, first_other)
+    )
+    gains_all = jnp.stack(
+        in_order(*(block[:, 2 * rows, :gain_count] for block in (first_all, first_other)))
+    )
     gains_all = jnp.moveaxis(gains_all.astype(F32), 0, 1)
-    spans = np.cumsum([0, rows, rows, rows, rows, query_gain.size, key_gain.size])
-    gain_one, mixed_scale, feed_scale, final_scale, query_scale, key_scale = (
+    spans = np.cumsum([0, rows, rows, rows, query_gain.size, key_gain.size, rows])
+    mixed_scale, feed_scale, final_scale, query_scale, key_scale, gain_one = (
         gains_all[:, :, a:b] for a, b in zip(spans[:-1], spans[1:])
     )
+    gain_first = gain_one.reshape(model)
+
+    def inside_order(values):
+        values = values.reshape(nx, ny, nw, nz, 2, rows)
+        return jnp.transpose(values, (4, 2, 3, 0, 1, 5)).reshape(-1)
+
     gain_one, mixed_scale, feed_scale, final_scale = (
-        g.reshape(model) for g in (gain_one, mixed_scale, feed_scale, final_scale)
+        inside_order(g) for g in (gain_one, mixed_scale, feed_scale, final_scale)
     )
 
     def true_order(values):
-        values = values.reshape(nx, nw, nz, ny, 2, -1)
-        return jnp.transpose(values, (0, 4, 1, 2, 3, 5)).reshape(-1)
+        values = values.reshape(nx, ny, nw, nz, 2, -1)
+        return jnp.transpose(values, (0, 4, 2, 3, 1, 5)).reshape(-1)
 
     query_scale, key_scale = true_order(query_scale), true_order(key_scale)
-    output_full = first_all[:, :, 2 * rows + gain_rows :].reshape(2, nx, nw * nz * ny, -1, model)
-    output_full = jnp.moveaxis(output_full, 0, 1).reshape(wide, model)
-
-    gate_up = jnp.stack([gate_weight, up_weight], axis=1).reshape(rows, 2, nx, 2, stretch)
-
-    def half_of(which):
-        piece = lax.dynamic_index_in_dim(gate_up, which, 3, keepdims=False)
-        return piece.reshape(rows, FF)
-
-    gate_up_own = cores_in_order(half_of(core), place.swap_core(half_of(1 - core)))
-    gate_up_full, gate_up_came = place.gather(
-        gate_up_own.reshape(2 * rows, FF), both_ways, first_came
-    )
-    down_full, _ = place.gather(reorder(down_weight, to_inside), both_ways, gate_up_came)
 
     tokens_in = reorder(tokens, to_inside).astype(F32)
+    tokens_first = reorder(tokens, to_first).astype(F32)
     out_grad = reorder(cotangent, to_inside).astype(F32)
     factor_one = rms_factor(tokens_in)
-    normed = (tokens_in * factor_one * gain_one).astype(BF)
-    raw = matmul(normed, projection_full)
+    normed = (tokens_first * factor_one * gain_first).astype(BF)
+    raw = in_order(*(matmul(normed, half) for half in projections))
     heads_half = wide // 2
 
     def both_halves(at, width):
-        return [raw[:, at : at + width], raw[:, head_width + at : head_width + at + width]]
+        return [half[:, at : at + width] for half in raw]
 
     query_raw = [
         piece[:, h * HD : (h + 1) * HD]
@@ -462,7 +557,30 @@
     cosine, sine = angles_of(query_pos)
     key_factor = rms_factor(key_raw)
     key_rows = rotate(key_raw * key_factor * key_scale, cosine, sine).astype(BF)
-    key_values = place.gather_group(jnp.concatenate([key_rows, value_rows], axis=1))
+    key_values, came = place.gather_group(jnp.concatenate([key_rows, value_rows], axis=1))
+    query_raw = [after(q, came) for q in query_raw]
+    positions, segment_ids, query_pos, query_seg, first_all, first_other, up_own, projections = (
+        lax.optimization_barrier(
+            (
+                positions,
+                segment_ids,
+                query_pos,
+                query_seg,
+                first_all,
+                first_other,
+                up_own,
+                projections,
+                came,
+            )
+        )[:8]
+    )
+    output_full = jnp.stack(
+        in_order(*(block[:, 2 * rows + gain_rows :] for block in (first_all, first_other)))
+    )
+    output_full = jnp.transpose(
+        output_full.reshape(2, nx, ny, nw * nz, -1, model), (1, 0, 3, 2, 4, 5)
+    ).reshape(wide, model)
+    up_full = place.gather_line(after(up_own, key_values))
     query_factor = [rms_factor(q) for q in query_raw]
     queries = jnp.concatenate(
         [
@@ -472,47 +590,72 @@
         axis=1,
     )
     attention = Attention(positions, segment_ids, query_pos, query_seg)
-    attended, logs = attention.forward(queries, key_values)
+    attended, logs = attention.forward(after(queries, gate_full), key_values)
+    down_full = place.gather_line(after(down_own, attended))
     projected = matmul(attended, output_full)
     factor_three = rms_factor(projected)
     mixed = tokens_in + projected * factor_three * mixed_scale
     factor_two = rms_factor(mixed)
     normed_two = (mixed * factor_two * feed_scale).astype(BF)
-    normed_both = jnp.concatenate([normed_two, place.swap_core(normed_two)])
-    pre = matmul(normed_both, gate_up_full)
-    gate_pre, up_pre = pre[:, :half], pre[:, half:]
-    hidden = (jax.nn.gelu(gate_pre, approximate=True) * up_pre).astype(BF)
-    branch_both = matmul(hidden, down_full)
-    branch = branch_both[:local] + place.swap_core(branch_both[local:])
+    near_blocks = place.gather_near(normed_two)
+    def gelu_parts(value):
+        scale = (2.0 / np.pi) ** 0.5
+        square = value * value
+        bend = jnp.tanh(scale * (value + 0.044715 * (square * value)))
+        rise = 0.5 * (1.0 + bend)
+        slope = 0.5 * value * (1.0 - bend * bend) * (scale * (1.0 + 3 * 0.044715 * square))
+        return value * rise, rise + slope
+
+    kept, hidden_blocks, branch_parts = [], [], []
+    normed_blocks = [normed_two]
+    for number in range(nx * ny):
+        if number == 1:
+            normed_blocks = place.gather_far(near_blocks, branch_parts[0])
+        block = normed_blocks[number]
+        gate_pre, up_pre = matmul(block, gate_full), matmul(block, up_full)
+        gelu, gelu_slope = gelu_parts(gate_pre)
+        kept.append(((gelu_slope * up_pre).astype(BF), gelu.astype(BF)))
+        hidden_blocks.append((gelu * up_pre).astype(BF))
+        branch_parts.append(matmul(hidden_blocks[-1], down_full))
+    branch = place.scatter_plane(branch_parts)
     factor_four = rms_factor(branch)
     layer_out = reorder((mixed + branch * factor_four * final_scale).astype(BF), to_outside)
 
     branch_grad, final_term = norm_back(out_grad, branch, factor_four, final_scale)
     branch_grad = branch_grad.astype(BF)
-    branch_grad_both = jnp.concatenate([branch_grad, place.swap_core(branch_grad)])
-    down_terms = matmul_tn(hidden, branch_grad_both).astype(BF)
-    down_weight_grad = reorder(place.scatter(down_terms, both_ways), to_outside)
-    hidden_grad = matmul_nt(branch_grad_both, down_full)
-    _, geglu_back = jax.vjp(
-        lambda gate_in, up_in: jax.nn.gelu(gate_in, approximate=True) * up_in, gate_pre, up_pre
-    )
-    gate_grad, up_grad = geglu_back(hidden_grad)
-    gate_up_grad = jnp.concatenate([gate_grad.astype(BF), up_grad.astype(BF)], axis=1)
-    gate_up_terms = matmul_tn(normed_both, gate_up_grad).astype(BF)
-    gate_up_rows = place.scatter(gate_up_terms, both_ways).reshape(2, rows, FF)
-    both = cores_in_order(pick(gate_up_rows, core), place.swap_core(pick(gate_up_rows, 1 - core)))
-    both = both.reshape(2, rows, 2, nx, stretch)
-    both = jnp.transpose(both, (2, 1, 3, 0, 4)).reshape(2, rows, FF)
-    gate_weight_grad, up_weight_grad = both[0], both[1]
-
-    normed_two_both = matmul_nt(gate_up_grad, gate_up_full)
-    normed_two_grad = normed_two_both[:local] + place.swap_core(normed_two_both[local:])
+    near_blocks = place.gather_near(branch_grad)
+    branch_grad_blocks = [branch_grad]
+    gate_grads, up_grads, normed_two_parts = [], [], []
+    for number, factors in enumerate(kept):
+        if number == 1:
+            branch_grad_blocks = place.gather_far(near_blocks, normed_two_parts[0])
+        block = branch_grad_blocks[number]
+        hidden_grad = matmul_nt(block, down_full)
+        gate_grad, up_grad = ((hidden_grad * f.astype(F32)).astype(BF) for f in factors)
+        gate_grads.append(gate_grad)
+        up_grads.append(up_grad)
+        normed_two_parts.append(matmul_nt(gate_grad, gate_full) + matmul_nt(up_grad, up_full))
+    normed_two_grad = place.scatter_plane(normed_two_parts)
+    halfway = place.halfway
+    normed_all = jnp.concatenate(normed_blocks)
+    hidden_all = jnp.concatenate(hidden_blocks)
+    down_terms = matmul_tn(
+        after(hidden_all, normed_two_parts[-1]), jnp.concatenate(branch_grad_blocks)
+    ).astype(BF)
+    down_terms = place.cores_summed(down_terms)
+    gate_terms = matmul_tn(
+        normed_all, after(jnp.concatenate(gate_grads), down_terms, *halfway)
+    ).astype(BF)
+    gate_terms = place.cores_summed(gate_terms)
+    down_rows = place.scatter_line(down_terms)
+
     mixed_part, feed_term = norm_back(normed_two_grad, mixed, factor_two, feed_scale)
     mixed_grad = out_grad + mixed_part
     projected_grad, mixed_term = norm_back(mixed_grad, projected, factor_three, mixed_scale)
     projected_grad = projected_grad.astype(BF)
     output_terms = matmul_tn(attended, projected_grad).astype(BF)
     attended_grad = matmul_nt(projected_grad, output_full).astype(BF)
+    attended_grad = after(attended_grad, gate_terms)
     delta = jnp.stack(
         [
             jnp.sum(
@@ -526,7 +669,26 @@
     queries_grad, key_value_terms = attention.backward(
         queries, attended_grad, logs, delta, key_values
     )
-    key_value_grad = place.scatter(key_value_terms, (("y",),))
+    up_terms = []
+
+    def up_terms_after(came):
+        grads = after(jnp.concatenate(up_grads), came)
+        up_terms.append(place.cores_summed(matmul_tn(normed_all, grads).astype(BF)))
+        return up_terms[0]
+
+    key_value_grad, came = place.scatter_group(key_value_terms, up_terms_after)
+    up_terms = up_terms[0]
+    output_terms = after(output_terms, came)
+    gate_rows = place.scatter_line(gate_terms)
+    up_rows = place.scatter_line(after(up_terms, key_value_grad))
+    down_weight_grad = matmul(down_rows, to_outside)
+    gate_up_rows = jnp.stack(
+        [rows_of.reshape(nx, ny, rows, part) for rows_of in (gate_rows, up_rows)], axis=2
+    )
+    gate_up_rows = place.deal_plane(gate_up_rows).reshape(nx, ny, 2, rows, 2 * nw * nz, -1)
+    gate_up_rows = jnp.transpose(gate_up_rows, (2, 3, 0, 4, 1, 5)).reshape(2, rows, FF)
+    gate_weight_grad = gate_up_rows[0].astype(F32)
+    up_weight_grad = gate_up_rows[1].astype(F32)
     key_grad_rows = key_value_grad[:, :HD]
     values_grad = key_value_grad[:, HD:].astype(BF)
     key_back = rotate(key_grad_rows, cosine, -sine)
@@ -551,25 +713,25 @@
                 axis=1,
             )
         )
-    normed_grad = matmul_nt(jnp.concatenate(raw_grad, axis=1), projection_full)
-    tokens_part, gain_one_term = norm_back(normed_grad, tokens_in, factor_one, gain_one)
-    tokens_grad = reorder((mixed_grad + tokens_part).astype(BF), to_outside)
-
     def chip_order(values):
         values = values.reshape(nx, 2, nw, nz, ny, -1)
-        return jnp.transpose(values, (0, 2, 3, 4, 1, 5)).reshape(chips, 2, -1)
+        return jnp.transpose(values, (0, 4, 2, 3, 1, 5)).reshape(chips, 2, -1)
+
+    def chip_order_inside(values):
+        values = values.reshape(2, nw, nz, nx, ny, rows)
+        return jnp.transpose(values, (3, 4, 1, 2, 0, 5)).reshape(chips, 2, rows)
 
     gain_terms = jnp.concatenate(
-        [t.reshape(chips, 2, -1) for t in (gain_one_term, mixed_term, feed_term, final_term)]
+        [chip_order_inside(t) for t in (mixed_term, feed_term, final_term)]
         + [chip_order(query_term), chip_order(key_term)],
         axis=2,
     )
     gain_terms = jnp.moveaxis(gain_terms, 1, 0).astype(BF)
     gain_terms = jnp.pad(
-        gain_terms, ((0, 0), (0, 0), (0, gain_rows * head_width - gain_count))
+        gain_terms, ((0, 0), (0, 0), (0, gain_rows * head_width - gain_terms.shape[2]))
     ).reshape(2, chips, gain_rows, head_width)
-    output_terms = output_terms.reshape(nx, 2, nw * nz * ny, -1, model)
-    output_terms = jnp.moveaxis(output_terms, 1, 0).reshape(2, chips, -1, head_width)
+    output_terms = output_terms.reshape(nx, 2, nw * nz, ny, -1, model)
+    output_terms = jnp.transpose(output_terms, (1, 0, 3, 2, 4, 5)).reshape(2, chips, -1, head_width)
     grads_pair = jnp.stack(raw_grad)
 
     def terms_of(which):
@@ -583,7 +745,15 @@
         ).reshape(-1, head_width)
 
     first_terms = terms_of(core).astype(F32) + place.swap_core(terms_of(1 - core)).astype(F32)
-    first_grad = place.scatter(first_terms.astype(BF), both_ways)
+    first_terms = first_terms.astype(BF)
+    normed_grad = 0.0
+    for half, grad in zip(in_order(*projections), raw_grad):
+        half = matmul(inside_from_first, half).astype(BF)
+        normed_grad = normed_grad + matmul_nt(after(grad, first_terms), half)
+    tokens_part, _ = norm_back(normed_grad, tokens_in, factor_one, gain_one)
+    tokens_grad = reorder((mixed_grad + tokens_part).astype(BF), to_outside)
+
+    first_grad = place.scatter_chips(first_terms)
     projection_rows = first_grad[: 2 * rows].reshape(2, rows, head_width)
     projection_rows = cores_in_order(
         pick(projection_rows, core), place.swap_core(pick(projection_rows, 1 - core))
@@ -597,13 +767,20 @@
     value_weight_grad = whole_columns(heads_half + quarter, head_width)
     gain_grad = first_grad[2 * rows : 2 * rows + gain_rows].reshape(-1)
     (
-        attention_gain_grad,
         mixed_gain_grad,
         feed_gain_grad,
         final_gain_grad,
         query_gain_grad,
         key_gain_grad,
-    ) = (gain_grad[a:b] for a, b in zip(spans[:-1], spans[1:]))
+    ) = (gain_grad[a:b] for a, b in zip(spans[:5], spans[1:6]))
+    attention_gain_grad = sum(
+        jnp.sum(grad * weight.astype(F32), axis=1)
+        for grad, weight in (
+            (query_weight_grad, query_weight),
+            (key_weight_grad, key_weight),
+            (value_weight_grad, value_weight),
+        )
+    ) / attention_gain.astype(F32)
     output_weight_grad = reorder(first_grad[2 * rows + gain_rows :].reshape(-1, model), to_outside)
     return (
         layer_out,

time: 1180 us -> 836 us (0.71)
  waiting for transfers between devices: 436 us -> 275 us
  starting transfers between devices: 225 us -> 66.6 us
  local copies, waits for them, and re-layouts: 186 us -> 122 us
  matrix products: 168 us -> 193 us
  Pallas kernels: 24.2 us -> 45 us
  other arithmetic: 125 us -> 110 us
  between operations: 3.08 us -> 17.5 us
    ppermute x68 -> x42, waiting for transfers between devices: 302 us -> 126 us  [shift(): return lax.ppermute(value, axis, [(i, (i + by) % n) for i in range(n)])]
    ppermute x24 -> x12, starting transfers between devices: 122 us -> 22.7 us  [shift_wz(): return lax.ppermute(value, ('w', 'z'), pairs)]
    ppermute x68 -> x42, starting transfers between devices: 101 us -> 42.3 us  [shift(): return lax.ppermute(value, axis, [(i, (i + by) % n) for i in range(n)])]
    dynamic_update_slice x48 -> x7, local copies, waits for them, and re-layouts: 44.9 us -> 5.96 us  [the longest x3 4.02 us: gather_chips(): lax.dynamic_update_slice(full, block, ((x * size['y'] + y) * line, 0))]
    all_gather x0 -> x3, waiting for transfers between devices: none -> 32 us  [gather_line(): return lax.all_gather(own, ('core', 'w', 'z'), axis=0, tiled=True)]
    convert_element_type x0 -> x8, local copies, waits for them, and re-layouts: none -> 21.7 us  [the longest x1 6.44 us: body(): gate_terms = matmul_tn(normed_all, after(jnp.concatenate(gate_grads), dow...]
    dot_general x10 -> x23, matrix products: 62.7 us -> 83.2 us  [matmul(): return jnp.dot(left, right, preferred_element_type=F32)]
    concatenate x1 -> x8, other arithmetic: 0.86 us -> 18.3 us  [the longest x1 5.37 us: up_terms_after(): grads = after(jnp.concatenate(up_grads), came)]
  transfers between devices with their start and end apart: 102 -> 67, of which waited for: 36 -> 27; matrix products, arithmetic and copies ran while one was open for 32% -> 41% of each run, Pallas kernels for 2% -> 5%
where the time goes in v2:
time: 836 us; the launch traced here: 829 us
  waiting for transfers between devices  275 us (33%)
  matrix products  193 us (23%)
  local copies, waits for them, and re-layouts  122 us (15%)
  other arithmetic  110 us (13%)
  starting transfers between devices  66.6 us (8%)
  Pallas kernels  45 us (5%)
  between operations  17.5 us (2%)
    ppermute x42, waiting for transfers between devices, shift(): return lax.ppermute(value, axis, [(i, (i + by) % n) for i in range(n)])  126 us
    ppermute x12, waiting for transfers between devices, shift_wz(): return lax.ppermute(value, ('w', 'z'), pairs)  116 us
    dot_general x23, matrix products, matmul(): return jnp.dot(left, right, preferred_element_type=F32)  83.2 us
    dot_general x15, matrix products, matmul_nt(): return jnp.einsum('ij,kj->ik', left, right, preferred_element_type=F32)  67.2 us
    ppermute x42, starting transfers between devices, shift(): return lax.ppermute(value, axis, [(i, (i + by) % n) for i in range(n)])  42.3 us
    dot_general x6, matrix products, matmul_tn(): return jnp.einsum('ji,jk->ik', left, right, preferred_element_type=F32)  39.9 us
    all_gather x3, waiting for transfers between devices, gather_line(): return lax.all_gather(own, ('core', 'w', 'z'), axis=0, tiled=True)  32 us
    pallas_call x1, Pallas kernels, backward(): pl.pallas_call(backward_kernel, out_shape=(jax.ShapeDtypeStruct((local, w...  26.6 us
  transfers between devices with their start and end apart: 67, of which 27 were waited for; matrix products, arithmetic and copies ran while one was open for 41% of the time, Pallas kernels for 5%

profile of v2, /device:TPU:0, one launch (start us, length us, event | category | flops | bytes accessed | tf_op | source)
XLA Modules:
  0.0 829.2 jit_solution(9706510820706169277)
XLA Ops:
  33.1 6.7 collective-permute-done.2
  46.0 12.7 %collective-permute-done.5 = bf16[512,768]{1,0:T(8,128)(2,1)} collective-permute-done((bf16[512,768]{1,0:T(8,128)(2,1)S(1)}, bf16[512,768]{1,0:T(8,128)(2,1)}, u32[]{:S(2)}, u32[]{:S(2)}) %collective-permute-start.5) | collective-permute-done | bytes 786464 | tf_op jit(solution)/shard_map/ppermute | solution.py:34
  79.0 5.9 fusion.122
  121.3 21.8 %collective-permute-done.12 = bf16[512,512]{1,0:T(8,128)(2,1)S(1)} collective-permute-done((bf16[512,512]{1,0:T(8,128)(2,1)S(1)}, bf16[512,512]{1,0:T(8,128)(2,1)S(1)}, u32[]{:S(2)}, u32[]{:S(2)}) %collective-permute-start.12) | collective-permute-done | bytes 524320 | tf_op jit(solution)/shard_map/ppermute | solution.py:41
  144.7 23.4 %collective-permute-done.14 = bf16[512,512]{1,0:T(8,128)(2,1)S(1)} collective-permute-done((bf16[512,512]{1,0:T(8,128)(2,1)S(1)}, bf16[512,512]{1,0:T(8,128)(2,1)S(1)}, u32[]{:S(2)}, u32[]{:S(2)}) %collective-permute-start.14) | collective-permute-done | bytes 524320 | tf_op jit(solution)/shard_map/ppermute | solution.py:41
  176.7 6.2 collective-permute-done.15
  184.6 8.7 %collective-permute-done.17 = bf16[512,512]{1,0:T(8,128)(2,1)S(1)} collective-permute-done((bf16[512,512]{1,0:T(8,128)(2,1)S(1)}, bf16[512,512]{1,0:T(8,128)(2,1)S(1)}, u32[]{:S(2)}, u32[]{:S(2)}) %collective-permute-start.17) | collective-permute-done | bytes 524320 | tf_op jit(solution)/shard_map/ppermute | solution.py:34
  220.0 18.4 %shard_map.316 = (bf16[512,1024]{1,0:T(8,128)(2,1)}, f32[1,2048]{1,0:T(1,128)}) custom-call(s32[8]{0:T(128)} %or_select_fusion.live, bf16[512,1024]{1,0:T(8,128)(2,1)} %copy-done.117, bf16[4096,512]{1,0:T(8,128)(2,1)} %constant_dynamic-update-slice_fusion.18.kv_ref, s32[4096,1]{1,0:T(8,128)} %copy.156.key_pos, s32[4096,1]{1,0:T(8,128)} %copy.157.key_seg, ...), custom_call_target="tpu_custom_call" | custom-call | flops 5368709120 | bytes 8388608 | tf_op jit(solution)/shard_map/pallas_call | solution.py:362
  255.2 9.1 %multiply_convert_fusion.11 = (bf16[512,1728]{0,1:T(8,128)(2,1)}, f32[512,1728]{0,1:T(8,128)}) fusion(f32[512,1728]{0,1:T(8,128)} %fusion.257, bf16[512,1152]{1,0:T(8,128)(2,1)S(1)} %multiply_convert_fusion.12, bf16[1152,1728]{1,0:T(8,128)(2,1)} %all-gather.6.cloned.1.call-done), kind=kOutput, calls=%fused_computation.99 | convolution fusion | flops 2047279104 | bytes 14008320 | tf_op jit(solution)/shard_map/dot_general | solution.py:231
  264.3 31.9 %all-gather.8.cloned.1.call-done = bf16[1728,1152]{1,0:T(8,128)(2,1)} async-done(((bf16[216,1152]{1,0:T(8,128)(2,1)}), bf16[1728,1152]{1,0:T(8,128)(2,1)}) %all-gather.8.cloned.1.call-update) | async-done | bytes 3981328 | tf_op jit(solution)/shard_map/all_gather | solution.py:53
  329.3 7.3 multiply_convert_fusion.8
  346.1 9.6 %collective-permute-done.26 = bf16[256,1152]{1,0:T(8,128)(2,1)S(1)} collective-permute-done((bf16[256,1152]{1,0:T(8,128)(2,1)S(1)}, bf16[256,1152]{1,0:T(8,128)(2,1)S(1)}, u32[]{:S(2)}, u32[]{:S(2)}) %collective-permute-start.26) | collective-permute-done | bytes 589856 | tf_op jit(solution)/shard_map/ppermute | solution.py:34
  361.7 6.6 collective-permute-done.25
  368.3 11.0 %collective-permute-done.24 = bf16[256,1152]{1,0:T(8,128)(2,1)S(1)} collective-permute-done((bf16[256,1152]{1,0:T(8,128)(2,1)S(1)}, bf16[256,1152]{1,0:T(8,128)(2,1)S(1)}, u32[]{:S(2)}, u32[]{:S(2)}) %collective-permute-start.24) | collective-permute-done | bytes 589856 | tf_op jit(solution)/shard_map/ppermute | solution.py:34
  399.4 12.0 %collective-permute-done.28 = bf16[512,1152]{1,0:T(8,128)(2,1)S(1)} collective-permute-done((bf16[512,1152]{1,0:T(8,128)(2,1)S(1)}, bf16[512,1152]{1,0:T(8,128)(2,1)S(1)}, u32[]{:S(2)}, u32[]{:S(2)}) %collective-permute-start.28) | collective-permute-done | bytes 1179680 | tf_op jit(solution)/shard_map/ppermute | solution.py:34
  415.6 6.1 multiply_convert_fusion.4
  437.0 8.5 %multiply_convert_fusion = (bf16[512,1728]{0,1:T(8,128)(2,1)S(1)}, bf16[512,1728]{0,1:T(8,128)(2,1)S(1)}) fusion(f32[512,1728]{0,1:T(8,128)} %fusion.263, f32[512,1728]{0,1:T(8,128)} %get-tuple-element.299, bf16[1728,1152]{1,0:T(8,128)(2,1)} %all-gather.8.cloned.1.call-done, bf16[256,1152]{1,0:T(8,128)(2,1)S(1)} %collective-permute-done.32, ...), kind=kOutput, calls=%fused_computation.82 | convolution fusion | flops 2063794176 | bytes 15777792 | tf_op jit(solution)/shard_map/ij,kj->ik/dot_general | solution.py:235
  455.1 9.5 %convolution_convert_fusion.2 = bf16[1728,1152]{1,0:T(8,128)(2,1)S(1)} fusion(bf16[2048,1728]{0,1:T(8,128)(2,1)S(1)} %bitcast.320, bf16[2048,1152]{1,0:T(8,128)(2,1)S(1)} %constant_dynamic-update-slice_fusion.8), kind=kOutput, calls=%fused_computation.2 | convolution fusion | flops 8155717632 | bytes 15777792 | tf_op jit(solution)/shard_map/ji,jk->ik/dot_general | solution.py:239
  473.3 8.1 collective-permute-done.29
  481.4 12.1 %collective-permute-done.37 = bf16[256,1152]{1,0:T(8,128)(2,1)S(1)} collective-permute-done((bf16[256,1152]{1,0:T(8,128)(2,1)S(1)}, bf16[256,1152]{1,0:T(8,128)(2,1)S(1)}, u32[]{:S(2)}, u32[]{:S(2)}) %collective-permute-start.37) | collective-permute-done | bytes 589856 | tf_op jit(solution)/shard_map/ppermute | solution.py:34
  498.7 14.2 %convolution_convert_fusion.1 = bf16[1152,1728]{0,1:T(8,128)(2,1)} fusion(bf16[2048,1728]{0,1:T(8,128)(2,1)} %pad_maximum_fusion, bf16[2048,1152]{1,0:T(8,128)(2,1)} %copy-done.80), kind=kOutput, calls=%fused_computation.1 | convolution fusion | flops 8155717632 | bytes 15777792 | tf_op jit(solution)/shard_map/ji,jk->ik/dot_general | solution.py:239
  512.9 6.4 copy.163
  538.2 26.6 %shard_map.317 = (f32[512,1024]{1,0:T(8,128)}, bf16[4096,512]{1,0:T(8,128)(2,1)}) custom-call(s32[8]{0:T(128)} %or_select_fusion.live, bf16[512,1024]{1,0:T(8,128)(2,1)} %copy-done.117, bf16[512,1024]{1,0:T(8,128)(2,1)} %convolution_convert_fusion.7.grad_ref, f32[1,2048]{1,0:T(1,128)} %get-tuple-element.106.log_ref, f32[1,2048]{1,0:T(1,128)} %bitcast.396, ...), custom_call_target="tpu_custom_call" | custom-call | flops 13421772800 | bytes 16777216 | tf_op jit(solution)/shard_map/pallas_call | solution.py:386
  573.7 8.4 %collective-permute-done.40 = bf16[512,512]{1,0:T(8,128)(2,1)} collective-permute-done((bf16[512,512]{1,0:T(8,128)(2,1)S(1)}, bf16[512,512]{1,0:T(8,128)(2,1)}, u32[]{:S(2)}, u32[]{:S(2)}) %collective-permute-start.40) | collective-permute-done | bytes 524320 | tf_op jit(solution)/shard_map/ppermute | solution.py:34
  582.1 10.7 %convolution_convert_fusion = bf16[1152,1728]{0,1:T(8,128)(2,1)} fusion(bf16[2048,1728]{0,1:T(8,128)(2,1)S(1)} %pad_maximum_fusion.2, bf16[2048,1152]{1,0:T(8,128)(2,1)S(1)} %bitcast.360), kind=kOutput, calls=%fused_computation | convolution fusion | flops 8155717632 | bytes 15777792 | tf_op jit(solution)/shard_map/ji,jk->ik/dot_general | solution.py:239
  592.9 6.4 copy.166
  621.2 47.0 %collective-permute-done.41 = bf16[512,512]{1,0:T(8,128)(2,1)} collective-permute-done((bf16[512,512]{1,0:T(8,128)(2,1)}, bf16[512,512]{1,0:T(8,128)(2,1)}, u32[]{:S(2)}, u32[]{:S(2)}) %collective-permute-start.41) | collective-permute-done | bytes 524320 | tf_op jit(solution)/shard_map/ppermute | solution.py:41
  688.1 8.3 %collective-permute-done.46 = bf16[512,512]{1,0:T(8,128)(2,1)} collective-permute-done((bf16[512,512]{1,0:T(8,128)(2,1)}, bf16[512,512]{1,0:T(8,128)(2,1)}, u32[]{:S(2)}, u32[]{:S(2)}) %collective-permute-start.46) | collective-permute-done | bytes 524320 | tf_op jit(solution)/shard_map/ppermute | solution.py:41
  734.0 7.5 fusion.124
  741.5 8.4 %fusion.95 = (f32[512]{0:T(512)S(1)}, f32[512,1152]{1,0:T(8,128)}) fusion(bf16[512,1152]{1,0:T(8,128)(2,1)} %get-tuple-element.291, f32[1152]{0:T(1024)S(1)} %mul.1396, f32[512,1152]{1,0:T(8,128)} %fusion.124, bf16[512,768]{1,0:T(8,128)(2,1)} %get-tuple-element.114, s32[1152]{0:T(1024)S(1)} %copy-done.152, bf16[1152,768]{1,0:T(8,128)(2,1)S(1)} %bitcast.323, ...), kind=kOutput, calls=%fused_computation.151 | convolution fusion | flops 2950446592 | bytes 10234881 | tf_op jit(solution)/shard_map/ij,kj->ik/dot_general | solution.py:235
  778.8 9.1 %collective-permute-done.56 = bf16[128,768]{1,0:T(8,128)(2,1)S(1)} collective-permute-done((bf16[128,768]{1,0:T(8,128)(2,1)S(1)}, bf16[128,768]{1,0:T(8,128)(2,1)S(1)}, u32[]{:S(2)}, u32[]{:S(2)}) %collective-permute-start.56) | collective-permute-done | bytes 196640 | tf_op jit(solution)/shard_map/ppermute | solution.py:41
  798.2 11.6 %collective-permute-done.60 = bf16[2,1,2,36,1728]{4,2,3,1,0:T(2,128)(2,1)S(1)} collective-permute-done((bf16[2,1,2,36,1728]{4,2,3,1,0:T(2,128)(2,1)S(1)}, bf16[2,1,2,36,1728]{4,2,3,1,0:T(2,128)(2,1)S(1)}, u32[]{:S(2)}, u32[]{:S(2)}) %collective-permute-start.60) | collective-permute-done | bytes 497696 | tf_op jit(solution)/shard_map/ppermute | solution.py:34
  (749 shorter events, 411.1 us)
Async XLA Ops:
  7.3 211.8 %all-gather.4.cloned.1.call-start = ((), (), s32[]{:S(2)}) async-start(), calls=%async_computation.3 | async-start | bytes 4644864 | tf_op jit(solution)/shard_map/all_gather | solution.py:53
  45.5 26.2 %collective-permute-start.10 = (bf16[2,1,2,36,1728]{4,2,3,1,0:T(2,128)(2,1)}, bf16[2,1,2,36,1728]{4,2,3,1,0:T(2,128)(2,1)}, u32[]{:S(2)}, u32[]{:S(2)}) collective-permute-start(bf16[2,1,2,36,1728]{4,2,3,1,0:T(2,128)(2,1)} %get-tuple-element.224), channel_id=1, source_target_pairs={{0,1},{1,0},{2,3},{3,2},{4,5},{5,4},{6,7},{7,6},{8,9},{9,8},{10,11... | collective-permute-start | bytes 1493000 | tf_op jit(solution)/shard_map/ppermute | solution.py:34
  85.9 169.3 %all-gather.6.cloned.1.call-start = ((), (), s32[]{:S(2)}) async-start(), calls=%async_computation.4 | async-start | bytes 4644864 | tf_op jit(solution)/shard_map/all_gather | solution.py:53
  112.6 30.6 %collective-permute-start.12 = (bf16[512,512]{1,0:T(8,128)(2,1)S(1)}, bf16[512,512]{1,0:T(8,128)(2,1)S(1)}, u32[]{:S(2)}, u32[]{:S(2)}) collective-permute-start(bf16[512,512]{1,0:T(8,128)(2,1)S(1)} %get-tuple-element.242), channel_id=1, source_target_pairs={{0,2},{2,4},{4,6},{6,0},{1,3},{3,5},{5,7},{7,1},{8,10},{10,12},{12... | collective-permute-start | bytes 1572872 | tf_op jit(solution)/shard_map/ppermute | solution.py:41
  117.4 50.8 %collective-permute-start.14 = (bf16[512,512]{1,0:T(8,128)(2,1)S(1)}, bf16[512,512]{1,0:T(8,128)(2,1)S(1)}, u32[]{:S(2)}, u32[]{:S(2)}) collective-permute-start(bf16[512,512]{1,0:T(8,128)(2,1)S(1)} %get-tuple-element.242), channel_id=1, source_target_pairs={{0,4},{2,6},{4,0},{6,2},{1,5},{3,7},{5,1},{7,3},{8,12},{10,14},{12... | collective-permute-start | bytes 1572872 | tf_op jit(solution)/shard_map/ppermute | solution.py:41
  119.7 51.0 %collective-permute-start.16 = (bf16[512,512]{1,0:T(8,128)(2,1)S(1)}, bf16[512,512]{1,0:T(8,128)(2,1)S(1)}, u32[]{:S(2)}, u32[]{:S(2)}) collective-permute-start(bf16[512,512]{1,0:T(8,128)(2,1)S(1)} %get-tuple-element.242), channel_id=1, source_target_pairs={{0,6},{2,0},{4,2},{6,4},{1,7},{3,1},{5,3},{7,5},{8,14},{10,8},{12,... | collective-permute-start | bytes 1572872 | tf_op jit(solution)/shard_map/ppermute | solution.py:41
  119.7 51.5 %collective-permute-start.11 = (bf16[512,512]{1,0:T(8,128)(2,1)S(1)}, bf16[512,512]{1,0:T(8,128)(2,1)}, u32[]{:S(2)}, u32[]{:S(2)}) collective-permute-start(bf16[512,512]{1,0:T(8,128)(2,1)S(1)} %get-tuple-element.242), channel_id=1, source_target_pairs={{0,1},{1,0},{2,3},{3,2},{4,5},{5,4},{6,7},{7,6},{8,9},{9,8},{10,11... | collective-permute-start | bytes 1572872 | tf_op jit(solution)/shard_map/ppermute | solution.py:34
  143.2 30.8 %collective-permute-start.13 = (bf16[512,512]{1,0:T(8,128)(2,1)S(1)}, bf16[512,512]{1,0:T(8,128)(2,1)}, u32[]{:S(2)}, u32[]{:S(2)}) collective-permute-start(bf16[512,512]{1,0:T(8,128)(2,1)S(1)} %collective-permute-done.12), channel_id=1, source_target_pairs={{0,1},{1,0},{2,3},{3,2},{4,5},{5,4},{6,7},{7,6},{8,9},{9,8},{10,11... | collective-permute-start | bytes 1572872 | tf_op jit(solution)/shard_map/ppermute | solution.py:34
  170.7 22.6 %collective-permute-start.17 = (bf16[512,512]{1,0:T(8,128)(2,1)S(1)}, bf16[512,512]{1,0:T(8,128)(2,1)S(1)}, u32[]{:S(2)}, u32[]{:S(2)}) collective-permute-start(bf16[512,512]{1,0:T(8,128)(2,1)S(1)} %collective-permute-done.16), channel_id=1, source_target_pairs={{0,1},{1,0},{2,3},{3,2},{4,5},{5,4},{6,7},{7,6},{8,9},{9,8},{10,11... | collective-permute-start | bytes 1572872 | tf_op jit(solution)/shard_map/ppermute | solution.py:34
  194.1 102.1 %all-gather.8.cloned.1.call-start = ((), (), s32[]{:S(2)}) async-start(), calls=%async_computation.5 | async-start | bytes 4478976 | tf_op jit(solution)/shard_map/all_gather | solution.py:53
  238.4 475.3 %reduce-scatter.10.cloned.1.call-start = ((), (), s32[]{:S(2)}) async-start(), calls=%async_computation.8 | async-start | bytes 2488320
  249.7 52.0 %collective-permute-start.18 = (bf16[512,1152]{1,0:T(8,128)(2,1)S(1)}, bf16[512,1152]{1,0:T(8,128)(2,1)S(1)}, u32[]{:S(2)}, u32[]{:S(2)}) collective-permute-start(bf16[512,1152]{1,0:T(8,128)(2,1)S(1)} %multiply_convert_fusion.12), channel_id=1, source_target_pairs={{0,1},{1,0},{2,3},{3,2},{4,5},{5,4},{6,7},{7,6},{8,9},{9,8},{10,11... | collective-permute-start | bytes 3538952 | tf_op jit(solution)/shard_map/ppermute | solution.py:34
  250.9 50.7 %collective-permute-start.20 = (bf16[512,1152]{1,0:T(8,128)(2,1)S(1)}, bf16[512,1152]{1,0:T(8,128)(2,1)S(1)}, u32[]{:S(2)}, u32[]{:S(2)}) collective-permute-start(bf16[512,1152]{1,0:T(8,128)(2,1)S(1)} %multiply_convert_fusion.12), channel_id=1, source_target_pairs={{0,16},{16,0},{1,17},{17,1},{2,18},{18,2},{3,19},{19,3},{4,20},{20... | collective-permute-start | bytes 3538952 | tf_op jit(solution)/shard_map/ppermute | solution.py:34
  301.7 22.9 %collective-permute-start.21 = (bf16[256,1152]{1,0:T(8,128)(2,1)S(1)}, bf16[256,1152]{1,0:T(8,128)(2,1)S(1)}, u32[]{:S(2)}, u32[]{:S(2)}) collective-permute-start(bf16[256,1152]{1,0:T(8,128)(2,1)S(1)} %slice.399), channel_id=1, source_target_pairs={{0,1},{1,0},{2,3},{3,2},{4,5},{5,4},{6,7},{7,6},{8,9},{9,8},{10,11... | collective-permute-start | bytes 1769480 | tf_op jit(solution)/shard_map/ppermute | solution.py:34
  315.6 46.1 %collective-permute-start.19 = (bf16[256,1152]{1,0:T(8,128)(2,1)S(1)}, bf16[256,1152]{1,0:T(8,128)(2,1)S(1)}, u32[]{:S(2)}, u32[]{:S(2)}) collective-permute-start(bf16[256,1152]{1,0:T(8,128)(2,1)S(1)} %slice.673), channel_id=1, source_target_pairs={{0,1},{1,0},{2,3},{3,2},{4,5},{5,4},{6,7},{7,6},{8,9},{9,8},{10,11... | collective-permute-start | bytes 1769480 | tf_op jit(solution)/shard_map/ppermute | solution.py:34
  344.6 23.7 %collective-permute-start.25 = (bf16[256,1152]{1,0:T(8,128)(2,1)S(1)}, bf16[256,1152]{1,0:T(8,128)(2,1)S(1)}, u32[]{:S(2)}, u32[]{:S(2)}) collective-permute-start(bf16[256,1152]{1,0:T(8,128)(2,1)S(1)} %slice.672), channel_id=1, source_target_pairs={{0,16},{16,0},{1,17},{17,1},{2,18},{18,2},{3,19},{19,3},{4,20},{20... | collective-permute-start | bytes 1769480 | tf_op jit(solution)/shard_map/ppermute | solution.py:34
  385.1 26.4 %collective-permute-start.28 = (bf16[512,1152]{1,0:T(8,128)(2,1)S(1)}, bf16[512,1152]{1,0:T(8,128)(2,1)S(1)}, u32[]{:S(2)}, u32[]{:S(2)}) collective-permute-start(bf16[512,1152]{1,0:T(8,128)(2,1)S(1)} %fusion.86), channel_id=1, source_target_pairs={{0,1},{1,0},{2,3},{3,2},{4,5},{5,4},{6,7},{7,6},{8,9},{9,8},{10,11... | collective-permute-start | bytes 3538952 | tf_op jit(solution)/shard_map/ppermute | solution.py:34
  386.6 26.9 %collective-permute-start.30 = (bf16[512,1152]{1,0:T(8,128)(2,1)S(1)}, bf16[512,1152]{1,0:T(8,128)(2,1)S(1)}, u32[]{:S(2)}, u32[]{:S(2)}) collective-permute-start(bf16[512,1152]{1,0:T(8,128)(2,1)S(1)} %fusion.86), channel_id=1, source_target_pairs={{0,16},{16,0},{1,17},{17,1},{2,18},{18,2},{3,19},{19,3},{4,20},{20... | collective-permute-start | bytes 3538952 | tf_op jit(solution)/shard_map/ppermute | solution.py:34
  411.5 25.5 %collective-permute-start.32 = (bf16[256,1152]{1,0:T(8,128)(2,1)S(1)}, bf16[256,1152]{1,0:T(8,128)(2,1)S(1)}, u32[]{:S(2)}, u32[]{:S(2)}) collective-permute-start(bf16[256,1152]{1,0:T(8,128)(2,1)S(1)} %slice.411), channel_id=1, source_target_pairs={{0,16},{16,0},{1,17},{17,1},{2,18},{18,2},{3,19},{19,3},{4,20},{20... | collective-permute-start | bytes 1769480 | tf_op jit(solution)/shard_map/ppermute | solution.py:34
  413.5 23.5 %collective-permute-start.31 = (bf16[256,1152]{1,0:T(8,128)(2,1)S(1)}, bf16[256,1152]{1,0:T(8,128)(2,1)S(1)}, u32[]{:S(2)}, u32[]{:S(2)}) collective-permute-start(bf16[256,1152]{1,0:T(8,128)(2,1)S(1)} %slice.410), channel_id=1, source_target_pairs={{0,1},{1,0},{2,3},{3,2},{4,5},{5,4},{6,7},{7,6},{8,9},{9,8},{10,11... | collective-permute-start | bytes 1769480 | tf_op jit(solution)/shard_map/ppermute | solution.py:34
  464.8 32.0 %collective-permute-start.38 = (bf16[864,1152]{1,0:T(8,128)(2,1)S(1)}, bf16[864,1152]{1,0:T(8,128)(2,1)S(1)}, u32[]{:S(2)}, u32[]{:S(2)}) collective-permute-start(bf16[864,1152]{1,0:T(8,128)(2,1)S(1)} %dynamic-slice_bitcast_fusion.2), channel_id=1, source_target_pairs={{0,8},{8,0},{1,9},{9,1},{2,10},{10,2},{3,11},{11,3},{4,12},{12,4},... | collective-permute-start | bytes 5971976 | tf_op jit(solution)/shard_map/ppermute | solution.py:44
  466.2 27.3 %collective-permute-start.37 = (bf16[256,1152]{1,0:T(8,128)(2,1)S(1)}, bf16[256,1152]{1,0:T(8,128)(2,1)S(1)}, u32[]{:S(2)}, u32[]{:S(2)}) collective-permute-start(bf16[256,1152]{1,0:T(8,128)(2,1)S(1)} %get-tuple-element.191), channel_id=1, source_target_pairs={{0,1},{1,0},{2,3},{3,2},{4,5},{5,4},{6,7},{7,6},{8,9},{9,8},{10,11... | collective-permute-start | bytes 1769480 | tf_op jit(solution)/shard_map/ppermute | solution.py:34
  467.5 26.0 %collective-permute-start.34 = (bf16[256,1152]{1,0:T(8,128)(2,1)S(1)}, bf16[256,1152]{1,0:T(8,128)(2,1)S(1)}, u32[]{:S(2)}, u32[]{:S(2)}) collective-permute-start(bf16[256,1152]{1,0:T(8,128)(2,1)S(1)} %get-tuple-element.192), channel_id=1, source_target_pairs={{0,16},{16,0},{1,17},{17,1},{2,18},{18,2},{3,19},{19,3},{4,20},{20... | collective-permute-start | bytes 1769480 | tf_op jit(solution)/shard_map/ppermute | solution.py:34
  468.6 26.7 %collective-permute-start.35 = (bf16[256,1152]{1,0:T(8,128)(2,1)S(1)}, bf16[256,1152]{1,0:T(8,128)(2,1)S(1)}, u32[]{:S(2)}, u32[]{:S(2)}) collective-permute-start(bf16[256,1152]{1,0:T(8,128)(2,1)S(1)} %get-tuple-element.193), channel_id=1, source_target_pairs={{0,16},{16,0},{1,17},{17,1},{2,18},{18,2},{3,19},{19,3},{4,20},{20... | collective-permute-start | bytes 1769480 | tf_op jit(solution)/shard_map/ppermute | solution.py:34
  531.3 189.1 %reduce-scatter.6.cloned.1.call-start = ((), (), s32[]{:S(2)}) async-start(), calls=%async_computation.6 | async-start | bytes 2580480 | tf_op jit(solution)/shard_map/reduce_scatter | solution.py:62
  606.9 61.3 %collective-permute-start.42 = (bf16[512,512]{1,0:T(8,128)(2,1)}, bf16[512,512]{1,0:T(8,128)(2,1)}, u32[]{:S(2)}, u32[]{:S(2)}) collective-permute-start(bf16[512,512]{1,0:T(8,128)(2,1)} %get-tuple-element.174), channel_id=1, source_target_pairs={{0,1},{1,0},{2,3},{3,2},{4,5},{5,4},{6,7},{7,6},{8,9},{9,8},{10,11... | collective-permute-start | bytes 1572872 | tf_op jit(solution)/shard_map/ppermute | solution.py:34
  608.2 79.9 %collective-permute-start.47 = (bf16[512,512]{1,0:T(8,128)(2,1)}, bf16[512,512]{1,0:T(8,128)(2,1)}, u32[]{:S(2)}, u32[]{:S(2)}) collective-permute-start(bf16[512,512]{1,0:T(8,128)(2,1)} %get-tuple-element.175), channel_id=1, source_target_pairs={{0,1},{1,0},{2,3},{3,2},{4,5},{5,4},{6,7},{7,6},{8,9},{9,8},{10,11... | collective-permute-start | bytes 1572872 | tf_op jit(solution)/shard_map/ppermute | solution.py:34
  609.1 163.3 %reduce-scatter.8.cloned.1.call-start = ((), (), s32[]{:S(2)}) async-start(), calls=%async_computation.7 | async-start | bytes 2580480 | tf_op jit(solution)/shard_map/reduce_scatter | solution.py:62
  616.7 51.5 %collective-permute-start.41 = (bf16[512,512]{1,0:T(8,128)(2,1)}, bf16[512,512]{1,0:T(8,128)(2,1)}, u32[]{:S(2)}, u32[]{:S(2)}) collective-permute-start(bf16[512,512]{1,0:T(8,128)(2,1)} %fusion.121), channel_id=1, source_target_pairs={{0,4},{2,6},{4,0},{6,2},{1,5},{3,7},{5,1},{7,3},{8,12},{10,14},{12... | collective-permute-start | bytes 1572872 | tf_op jit(solution)/shard_map/ppermute | solution.py:41
  671.0 25.5 %collective-permute-start.46 = (bf16[512,512]{1,0:T(8,128)(2,1)}, bf16[512,512]{1,0:T(8,128)(2,1)}, u32[]{:S(2)}, u32[]{:S(2)}) collective-permute-start(bf16[512,512]{1,0:T(8,128)(2,1)} %get-tuple-element.173), channel_id=1, source_target_pairs={{0,6},{2,0},{4,2},{6,4},{1,7},{3,1},{5,3},{7,5},{8,14},{10,8},{12,... | collective-permute-start | bytes 1572872 | tf_op jit(solution)/shard_map/ppermute | solution.py:41
  731.7 27.9 %collective-permute-start.49 = (bf16[256,768]{1,0:T(8,128)(2,1)}, bf16[256,768]{1,0:T(8,128)(2,1)S(1)}, u32[]{:S(2)}, u32[]{:S(2)}) collective-permute-start(bf16[256,768]{1,0:T(8,128)(2,1)} %get-tuple-element.178), channel_id=1, source_target_pairs={{0,1},{1,0},{2,3},{3,2},{4,5},{5,4},{6,7},{7,6},{8,9},{9,8},{10,11... | collective-permute-start | bytes 1179656 | tf_op jit(solution)/shard_map/ppermute | solution.py:34
  732.3 27.2 %collective-permute-start.52 = (bf16[256,768]{1,0:T(8,128)(2,1)}, bf16[256,768]{1,0:T(8,128)(2,1)}, u32[]{:S(2)}, u32[]{:S(2)}) collective-permute-start(bf16[256,768]{1,0:T(8,128)(2,1)} %get-tuple-element.181), channel_id=1, source_target_pairs={{0,16},{16,0},{1,17},{17,1},{2,18},{18,2},{3,19},{19,3},{4,20},{20... | collective-permute-start | bytes 1179656 | tf_op jit(solution)/shard_map/ppermute | solution.py:34
  (202 other events, 1744.1 us)
Sparse Core Ops, SparseCore 0:
  86.0 79.0 all-gather.3
  194.2 56.3 all-gather.5
  252.3 43.8 all-gather.7
  531.4 40.3 reduce-scatter.9
  609.1 59.2 reduce-scatter.5
  717.3 42.2 reduce-scatter.7

commit v3 on v2

--- a/solution.py
+++ b/solution.py
@@ -1,3 +1,5 @@
+import functools
+
 import jax
 import jax.numpy as jnp
 import numpy as np
@@ -142,14 +144,14 @@
             full = lax.dynamic_update_slice(full, block, ((x * size["y"] + y) * line, 0))
         return full, mine, list(near.values())
 
-    def scatter_chips(self, full):
+    def scatter_chips(self, full, hold):
         size, at = self.size, self.at
         full = full.reshape((size["x"], size["y"], -1, full.shape[-1]))
         parts = [
             full[(at["x"] - dx) % size["x"], (at["y"] - dy) % size["y"]].astype(F32)
             for dx, dy in self.plane_steps()
         ]
-        mine = self.scatter_plane(parts)
+        mine = after(self.scatter_plane(parts), hold)
         mine = mine.reshape((size["w"], size["z"], -1, mine.shape[-1]))
         total = None
         for kw, kz in reversed(self.wz_steps()):
@@ -168,31 +170,23 @@
             spot = {"w": (at["w"] - kw) % size["w"], "z": (at["z"] - kz) % size["z"]}
             for ky in range(size["y"]):
                 block_y = block if ky == 0 else self.shift(block, "y", ky)
-                came = block_y if kw == kz == 0 else came
                 spot["y"] = (at["y"] - ky) % size["y"]
                 full = lax.dynamic_update_slice(full, block_y, (self.ctx_chip(spot) * rows, 0))
-        return full, came
-
-    def scatter_group(self, full, meanwhile):
+        return full
+
+    def scatter_group(self, full):
         size, at = self.size, self.at
         full = full.reshape((size["w"], size["z"], size["y"], -1, full.shape[-1]))
-        steps = sorted(self.wz_steps(), key=lambda k: (k == (0, 0), abs(k[1] - size["z"] // 2)))
-        total, came, gone = None, None, []
-        for kw, kz in steps:
+        total = None
+        for kw, kz in reversed(self.wz_steps()):
             part = full[(at["w"] + kw) % size["w"], (at["z"] + kz) % size["z"]]
             acc = part[at["y"]].astype(F32)
             for dy in range(1, size["y"]):
-                other = self.shift(part[(at["y"] + dy) % size["y"]], "y", dy)
-                if came is None:
-                    came = other
-                    done = meanwhile(came)
-                acc = acc + after(other, *gone).astype(F32) if gone else acc + other.astype(F32)
+                acc = acc + self.shift(part[(at["y"] + dy) % size["y"]], "y", dy).astype(F32)
             if kw or kz:
-                acc = self.shift_wz(acc.astype(BF), kw, kz)
-                gone = gone or [acc, done]
-                acc = acc.astype(F32)
+                acc = self.shift_wz(acc.astype(BF), kw, kz).astype(F32)
             total = acc if total is None else total + acc
-        return total, came
+        return total
 
 
 def after(value, *others):
@@ -327,6 +321,322 @@
         for head in range(HQ):
             mine = pl.ds(head * local, local)
             q_grad_ref[:, head * HD : (head + 1) * HD] = acc[:, mine].T
+
+
+class Ring:
+    def __init__(self, sizes):
+        _, _, self.nw, self.nz, self.ny = sizes
+        self.line = self.nw * self.nz
+        self.w, self.z, self.y = (lax.axis_index(a) for a in ("w", "z", "y"))
+
+    def spot(self, k, ky):
+        w = lax.rem(self.w + k // self.nz + self.nw, self.nw)
+        z = lax.rem(self.z + k % self.nz + self.nz, self.nz)
+        return w, z, lax.rem(self.y + ky + self.ny, self.ny)
+
+    def device(self, k, ky):
+        w, z, y = self.spot(k, ky)
+        return {"w": w, "z": z, "y": y}
+
+    def block(self, k, ky):
+        w, z, y = self.spot(k, ky)
+        return (w * self.nz + z) * self.ny + y
+
+    def source(self, k, ky):
+        w = lax.rem(self.w - k // self.nz + self.nw, self.nw)
+        z = lax.rem(self.z - k % self.nz + self.nz, self.nz)
+        return (w * self.nz + z) * self.ny + lax.rem(self.y - ky + self.ny, self.ny)
+
+    def meet(self):
+        barrier = pltpu.get_barrier_semaphore()
+        peers = [(k, 0) for k in range(1, self.line)] + [(0, ky) for ky in range(1, self.ny)]
+        for step in peers:
+            pl.semaphore_signal(
+                barrier, inc=1, device_id=self.device(*step), device_id_type=pl.DeviceIdType.MESH
+            )
+        pl.semaphore_wait(barrier, len(peers))
+
+    def copy(self, source, target, sems, k, ky, to):
+        send, recv = sems
+        return pltpu.make_async_remote_copy(
+            src_ref=source,
+            dst_ref=target,
+            send_sem=send.at[k, ky],
+            recv_sem=recv.at[k, ky],
+            device_id=self.device(*to),
+            device_id_type=pl.DeviceIdType.MESH,
+        )
+
+
+def gather_attend_kernel(
+    sizes,
+    own_ref,
+    raw_ref,
+    gain_ref,
+    cos_ref,
+    sin_ref,
+    key_pos,
+    key_seg,
+    query_pos,
+    query_seg,
+    all_ref,
+    q_ref,
+    out_ref,
+    log_ref,
+    held,
+    acc,
+    total,
+    send_sem,
+    recv_sem,
+    out_sem,
+):
+    ring = Ring(sizes)
+    local = own_ref.shape[0]
+    sems = (send_sem, recv_sem)
+
+    def rows(block):
+        return pl.ds(pl.multiple_of(block * local, local), local)
+
+    mine = held.at[rows(ring.block(0, 0)), :]
+    ring.meet()
+    for ky in range(1, ring.ny):
+        ring.copy(own_ref, mine, sems, 0, ky, (0, ky)).start()
+    for k in range(1, ring.line):
+        ring.copy(own_ref, mine, sems, k, 0, (k, 0)).start()
+    held[rows(ring.block(0, 0)), :] = own_ref[...]
+    acc[...] = jnp.zeros_like(acc)
+    total[...] = jnp.zeros_like(total)
+    for head in range(HQ):
+        raw = raw_ref[:, head * HD : (head + 1) * HD]
+        scaled = raw * rms_factor(raw) * gain_ref[...]
+        q_ref[:, head * HD : (head + 1) * HD] = rotate(scaled, cos_ref[...], sin_ref[...]).astype(BF)
+
+    def attend(block):
+        here = rows(block)
+        keys = held[here, :HD]
+        values_t = held[here, HD:].T
+        allowed = allowed_pairs(key_pos[here, :], key_seg[here, :], query_pos[...], query_seg[...])
+        for head in range(HQ):
+            place = pl.ds(head * local, local)
+            scores = matmul_nt(keys, q_ref[:, head * HD : (head + 1) * HD]) * HD ** (-0.5)
+            weights = jnp.where(allowed, jnp.exp(scores), 0.0)
+            total[:, place] += jnp.sum(weights, axis=0, keepdims=True)
+            acc[:, place] += matmul(values_t, weights.astype(BF))
+
+    def came(k, ky):
+        piece = held.at[rows(ring.source(k, ky)), :]
+        ring.copy(piece, piece, sems, k, ky, (k, ky)).wait_recv()
+
+    @pl.loop(0, ring.ny)
+    def _(ky):
+        @pl.when(ky > 0)
+        def _():
+            came(0, ky)
+
+        attend(ring.source(0, ky))
+
+    @pl.loop(1, ring.line)
+    def _(k):
+        came(k, 0)
+        piece = held.at[rows(ring.source(k, 0)), :]
+        for ky in range(1, ring.ny):
+            ring.copy(piece, piece, sems, k, ky, (0, ky)).start()
+        attend(ring.source(k, 0))
+
+    for ky in range(1, ring.ny):
+
+        @pl.loop(1, ring.line)
+        def _(k, ky=ky):
+            came(k, ky)
+            attend(ring.source(k, ky))
+
+    keep = pltpu.make_async_copy(held, all_ref, out_sem)
+    keep.start()
+    for head in range(HQ):
+        place = pl.ds(head * local, local)
+        out_ref[:, head * HD : (head + 1) * HD] = (acc[:, place] / total[:, place]).T.astype(BF)
+    log_ref[...] = jnp.log(total[...])
+    for ky in range(1, ring.ny):
+        ring.copy(own_ref, mine, sems, 0, ky, (0, ky)).wait_send()
+    for k in range(1, ring.line):
+        ring.copy(own_ref, mine, sems, k, 0, (k, 0)).wait_send()
+        for ky in range(1, ring.ny):
+            ring.copy(own_ref, mine, sems, k, ky, (0, ky)).wait_send()
+    keep.wait()
+
+
+def attend_back_kernel(
+    sizes,
+    q_ref,
+    grad_ref,
+    log_ref,
+    delta_ref,
+    all_ref,
+    key_pos,
+    key_seg,
+    query_pos,
+    query_seg,
+    q_grad_ref,
+    own_grad_ref,
+    acc,
+    term,
+    from_y,
+    on_z,
+    from_z,
+    send_y,
+    recv_y,
+    send_z,
+    recv_z,
+):
+    ring = Ring(sizes)
+    local = q_ref.shape[0]
+    along_y, along_z = (send_y, recv_y), (send_z, recv_z)
+
+    def to_y(k, ky):
+        return ring.copy(term.at[k, ky], from_y.at[k, ky], along_y, k, ky, (0, ky))
+
+    def to_z(k):
+        return ring.copy(on_z.at[k], from_z.at[k], along_z, k, 0, (k, 0))
+
+    def terms(block):
+        here = pl.ds(pl.multiple_of(block * local, local), local)
+        keys = all_ref[here, :HD]
+        keys_t = keys.T
+        values = all_ref[here, HD:]
+        allowed = allowed_pairs(key_pos[here, :], key_seg[here, :], query_pos[...], query_seg[...])
+        key_grad = jnp.zeros(keys.shape, F32)
+        value_grad = jnp.zeros(keys.shape, F32)
+        for head in range(HQ):
+            place = pl.ds(head * local, local)
+            queries = q_ref[:, head * HD : (head + 1) * HD]
+            grads = grad_ref[:, head * HD : (head + 1) * HD]
+            scores = matmul_nt(keys, queries) * HD ** (-0.5)
+            probs = jnp.where(allowed, jnp.exp(scores - log_ref[:, place]), 0.0)
+            prob_grad = matmul_nt(values, grads)
+            score_grad = (probs * (prob_grad - delta_ref[:, place]) * HD ** (-0.5)).astype(BF)
+            value_grad += matmul(probs.astype(BF), grads)
+            key_grad += matmul(score_grad, queries)
+            acc[:, place] += matmul(keys_t, score_grad)
+        return key_grad, value_grad
+
+    def keep(ref, pair):
+        ref[:, :HD] = pair[0].astype(ref.dtype)
+        ref[:, HD:] = pair[1].astype(ref.dtype)
+
+    ring.meet()
+    acc[...] = jnp.zeros_like(acc)
+    for ky in range(1, ring.ny):
+
+        @pl.loop(1, ring.line)
+        def _(k, ky=ky):
+            keep(term.at[k, ky], terms(ring.block(k, ky)))
+            to_y(k, ky).start()
+
+    @pl.loop(1, ring.line)
+    def _(k):
+        keep(own_grad_ref, terms(ring.block(k, 0)))
+        for ky in range(1, ring.ny):
+            to_y(k, ky).wait_recv()
+            own_grad_ref[...] += from_y[k, ky].astype(F32)
+        on_z[k] = own_grad_ref[...].astype(BF)
+        to_z(k).start()
+
+    @pl.loop(0, ring.ny)
+    def _(step):
+        ky = lax.rem(step + 1, ring.ny)
+        pair = terms(ring.block(0, ky))
+
+        @pl.when(ky > 0)
+        def _():
+            keep(term.at[0, ky], pair)
+            to_y(0, ky).start()
+
+        @pl.when(ky == 0)
+        def _():
+            keep(own_grad_ref, pair)
+
+    for head in range(HQ):
+        place = pl.ds(head * local, local)
+        q_grad_ref[:, head * HD : (head + 1) * HD] = acc[:, place].T
+    for ky in range(1, ring.ny):
+        to_y(0, ky).wait_recv()
+        own_grad_ref[...] += from_y[0, ky].astype(F32)
+    for k in range(1, ring.line):
+        to_z(k).wait_recv()
+        own_grad_ref[...] += from_z[k].astype(F32)
+        to_z(k).wait_send()
+    for k in range(ring.line):
+        for ky in range(1, ring.ny):
+            to_y(k, ky).wait_send()
+
+
+IN_VMEM = pl.BlockSpec(memory_space=pltpu.VMEM)
+
+
+def kernel_settings(number):
+    return dict(
+        compiler_params=pltpu.CompilerParams(
+            collective_id=number, has_side_effects=True, vmem_limit_bytes=56 << 20
+        ),
+        cost_estimate=pl.CostEstimate(
+            flops=5 * 10**10, bytes_accessed=16 << 20, transcendentals=0
+        ),
+    )
+
+
+def gather_attend(sizes, own, raw, gain, cosine, sine, marks):
+    local, wide = raw.shape
+    _, _, nw, nz, ny = sizes
+    line = nw * nz
+    full = jax.ShapeDtypeStruct((line * ny * local, own.shape[1]), BF)
+    return pl.pallas_call(
+        functools.partial(gather_attend_kernel, sizes),
+        out_shape=(
+            full,
+            jax.ShapeDtypeStruct((local, wide), BF),
+            jax.ShapeDtypeStruct((local, wide), BF),
+            jax.ShapeDtypeStruct((1, HQ * local), F32),
+        ),
+        in_specs=[IN_VMEM] * 9,
+        out_specs=(pl.BlockSpec(memory_space=pl.ANY), IN_VMEM, IN_VMEM, IN_VMEM),
+        scratch_shapes=[
+            pltpu.VMEM(full.shape, BF),
+            pltpu.VMEM((HD, HQ * local), F32),
+            pltpu.VMEM((1, HQ * local), F32),
+            pltpu.SemaphoreType.DMA((line, ny)),
+            pltpu.SemaphoreType.DMA((line, ny)),
+            pltpu.SemaphoreType.DMA,
+        ],
+        **kernel_settings(0),
+    )(own, raw, gain, cosine, sine, *marks)
+
+
+def attend_back(sizes, queries, grads, logs, delta, key_values, marks):
+    local, wide = queries.shape
+    _, _, nw, nz, ny = sizes
+    line = nw * nz
+    width = key_values.shape[1]
+    return pl.pallas_call(
+        functools.partial(attend_back_kernel, sizes),
+        out_shape=(
+            jax.ShapeDtypeStruct((local, wide), F32),
+            jax.ShapeDtypeStruct((local, width), F32),
+        ),
+        in_specs=[IN_VMEM] * 9,
+        out_specs=(IN_VMEM, IN_VMEM),
+        scratch_shapes=[
+            pltpu.VMEM((HD, HQ * local), F32),
+            pltpu.VMEM((line, ny, local, width), BF),
+            pltpu.VMEM((line, ny, local, width), BF),
+            pltpu.VMEM((line, local, width), BF),
+            pltpu.VMEM((line, local, width), BF),
+            pltpu.SemaphoreType.DMA((line, ny)),
+            pltpu.SemaphoreType.DMA((line, ny)),
+            pltpu.SemaphoreType.DMA((line, 1)),
+            pltpu.SemaphoreType.DMA((line, 1)),
+        ],
+        **kernel_settings(1),
+    )(queries, grads, logs, delta, key_values, *marks)
 
 
 class Attention:
@@ -498,9 +808,7 @@
     gate_up = jnp.stack([gate_weight, up_weight]).reshape(2, rows, nx, 2 * nw * nz, ny, -1)
     gate_up = jnp.transpose(gate_up, (2, 4, 0, 1, 3, 5)).reshape(nx, ny, 2, rows, part)
     down_own = reorder(down_weight, to_inside)
-    gate_up = place.deal_plane(gate_up, [first_came], next_came)
-    gate_own, up_own = (gate_up[:, :, i].reshape(-1, part) for i in range(2))
-    gate_full = place.gather_line(gate_own)
+    down_full = place.gather_line(down_own)
     first_other = place.swap_core(first_all)
 
     def in_order(own, other):
@@ -557,41 +865,43 @@
     cosine, sine = angles_of(query_pos)
     key_factor = rms_factor(key_raw)
     key_rows = rotate(key_raw * key_factor * key_scale, cosine, sine).astype(BF)
-    key_values, came = place.gather_group(jnp.concatenate([key_rows, value_rows], axis=1))
-    query_raw = [after(q, came) for q in query_raw]
-    positions, segment_ids, query_pos, query_seg, first_all, first_other, up_own, projections = (
-        lax.optimization_barrier(
-            (
-                positions,
-                segment_ids,
-                query_pos,
-                query_seg,
-                first_all,
-                first_other,
-                up_own,
-                projections,
-                came,
-            )
-        )[:8]
-    )
+    own_key_values = jnp.concatenate([key_rows, value_rows], axis=1)
+    gate_up = place.deal_plane(gate_up, [first_came], next_came + [own_key_values])
+    gate_own, up_own = (gate_up[:, :, i].reshape(-1, part) for i in range(2))
+    gate_full, up_full = place.gather_line(gate_own), place.gather_line(up_own)
+    own_key_values = after(own_key_values, gate_own, up_own, down_full)
+    attention = Attention(positions, segment_ids, query_pos, query_seg)
+    together = nw * nz * ny <= 8
+    if together:
+        key_values, queries, attended, logs = gather_attend(
+            sizes,
+            own_key_values,
+            jnp.concatenate(query_raw, axis=1),
+            query_scale.reshape(1, -1),
+            cosine,
+            sine,
+            attention.marks,
+        )
+    else:
+        key_values = place.gather_group(own_key_values)
+        queries = jnp.concatenate(
+            [
+                rotate(q * rms_factor(q) * query_scale, cosine, sine).astype(BF)
+                for q in query_raw
+            ],
+            axis=1,
+        )
+        attended, logs = attention.forward(queries, key_values)
+    query_factor = [rms_factor(q) for q in query_raw]
+    first_all, first_other, projections, query_factor = lax.optimization_barrier(
+        (first_all, first_other, projections, query_factor, attended)
+    )[:4]
     output_full = jnp.stack(
         in_order(*(block[:, 2 * rows + gain_rows :] for block in (first_all, first_other)))
     )
     output_full = jnp.transpose(
         output_full.reshape(2, nx, ny, nw * nz, -1, model), (1, 0, 3, 2, 4, 5)
     ).reshape(wide, model)
-    up_full = place.gather_line(after(up_own, key_values))
-    query_factor = [rms_factor(q) for q in query_raw]
-    queries = jnp.concatenate(
-        [
-            rotate(q * f * query_scale, cosine, sine).astype(BF)
-            for q, f in zip(query_raw, query_factor)
-        ],
-        axis=1,
-    )
-    attention = Attention(positions, segment_ids, query_pos, query_seg)
-    attended, logs = attention.forward(after(queries, gate_full), key_values)
-    down_full = place.gather_line(after(down_own, attended))
     projected = matmul(attended, output_full)
     factor_three = rms_factor(projected)
     mixed = tokens_in + projected * factor_three * mixed_scale
@@ -610,7 +920,7 @@
     normed_blocks = [normed_two]
     for number in range(nx * ny):
         if number == 1:
-            normed_blocks = place.gather_far(near_blocks, branch_parts[0])
+            normed_blocks = place.gather_far(near_blocks, hidden_blocks[0])
         block = normed_blocks[number]
         gate_pre, up_pre = matmul(block, gate_full), matmul(block, up_full)
         gelu, gelu_slope = gelu_parts(gate_pre)
@@ -642,12 +952,14 @@
     down_terms = matmul_tn(
         after(hidden_all, normed_two_parts[-1]), jnp.concatenate(branch_grad_blocks)
     ).astype(BF)
+    gate_terms = matmul_tn(normed_all, after(jnp.concatenate(gate_grads), *halfway)).astype(BF)
+    up_terms = matmul_tn(normed_all, after(jnp.concatenate(up_grads), *halfway)).astype(BF)
+    normed_two_grad = after(normed_two_grad, gate_terms, up_terms)
     down_terms = place.cores_summed(down_terms)
-    gate_terms = matmul_tn(
-        normed_all, after(jnp.concatenate(gate_grads), down_terms, *halfway)
-    ).astype(BF)
     gate_terms = place.cores_summed(gate_terms)
+    up_terms = place.cores_summed(up_terms)
     down_rows = place.scatter_line(down_terms)
+    gate_rows = place.scatter_line(gate_terms)
 
     mixed_part, feed_term = norm_back(normed_two_grad, mixed, factor_two, feed_scale)
     mixed_grad = out_grad + mixed_part
@@ -655,7 +967,7 @@
     projected_grad = projected_grad.astype(BF)
     output_terms = matmul_tn(attended, projected_grad).astype(BF)
     attended_grad = matmul_nt(projected_grad, output_full).astype(BF)
-    attended_grad = after(attended_grad, gate_terms)
+    attended_grad = after(attended_grad, gate_terms, up_terms)
     delta = jnp.stack(
         [
             jnp.sum(
@@ -666,29 +978,25 @@
             for h in range(HQ)
         ]
     ).reshape(1, -1)
-    queries_grad, key_value_terms = attention.backward(
-        queries, attended_grad, logs, delta, key_values
-    )
-    up_terms = []
-
-    def up_terms_after(came):
-        grads = after(jnp.concatenate(up_grads), came)
-        up_terms.append(place.cores_summed(matmul_tn(normed_all, grads).astype(BF)))
-        return up_terms[0]
-
-    key_value_grad, came = place.scatter_group(key_value_terms, up_terms_after)
-    up_terms = up_terms[0]
-    output_terms = after(output_terms, came)
-    gate_rows = place.scatter_line(gate_terms)
-    up_rows = place.scatter_line(after(up_terms, key_value_grad))
+    if together:
+        queries_grad, key_value_grad = attend_back(
+            sizes, queries, attended_grad, logs, delta, key_values, attention.marks
+        )
+    else:
+        queries_grad, key_value_terms = attention.backward(
+            queries, attended_grad, logs, delta, key_values
+        )
+        key_value_grad = place.scatter_group(key_value_terms)
+    output_terms = after(output_terms, key_value_grad)
+    up_rows = place.scatter_line(up_terms)
     down_weight_grad = matmul(down_rows, to_outside)
-    gate_up_rows = jnp.stack(
-        [rows_of.reshape(nx, ny, rows, part) for rows_of in (gate_rows, up_rows)], axis=2
-    )
-    gate_up_rows = place.deal_plane(gate_up_rows).reshape(nx, ny, 2, rows, 2 * nw * nz, -1)
-    gate_up_rows = jnp.transpose(gate_up_rows, (2, 3, 0, 4, 1, 5)).reshape(2, rows, FF)
-    gate_weight_grad = gate_up_rows[0].astype(F32)
-    up_weight_grad = gate_up_rows[1].astype(F32)
+
+    def whole_rows(own_part):
+        dealt = place.deal_plane(own_part.reshape(nx, ny, rows, part))
+        dealt = dealt.reshape(nx, ny, rows, 2 * nw * nz, -1)
+        return jnp.transpose(dealt, (2, 0, 3, 1, 4)).reshape(rows, FF).astype(F32)
+
+    gate_weight_grad, up_weight_grad = whole_rows(gate_rows), whole_rows(up_rows)
     key_grad_rows = key_value_grad[:, :HD]
     values_grad = key_value_grad[:, HD:].astype(BF)
     key_back = rotate(key_grad_rows, cosine, -sine)
@@ -745,7 +1053,7 @@
         ).reshape(-1, head_width)
 
     first_terms = terms_of(core).astype(F32) + place.swap_core(terms_of(1 - core)).astype(F32)
-    first_terms = first_terms.astype(BF)
+    first_terms = after(first_terms.astype(BF), gate_rows)
     normed_grad = 0.0
     for half, grad in zip(in_order(*projections), raw_grad):
         half = matmul(inside_from_first, half).astype(BF)
@@ -753,7 +1061,7 @@
     tokens_part, _ = norm_back(normed_grad, tokens_in, factor_one, gain_one)
     tokens_grad = reorder((mixed_grad + tokens_part).astype(BF), to_outside)
 
-    first_grad = place.scatter_chips(first_terms)
+    first_grad = place.scatter_chips(first_terms, up_rows)
     projection_rows = first_grad[: 2 * rows].reshape(2, rows, head_width)
     projection_rows = cores_in_order(
         pick(projection_rows, core), place.swap_core(pick(projection_rows, 1 - core))

time: 836 us -> 779 us (0.932)
  waiting for transfers between devices: 275 us -> 112 us
  Pallas kernels: 45 us -> 173 us
  matrix products: 193 us -> 217 us
  other arithmetic: 110 us -> 91.5 us
  local copies, waits for them, and re-layouts: 122 us -> 105 us
  starting transfers between devices: 66.6 us -> 54.1 us
    pallas_call x2, Pallas kernels: 45 us -> 173 us  [the longest x1 93 us: gather_attend(): pl.pallas_call(functools.partial(gather_attend_kernel, sizes), out_shape=...]
    ppermute x12 -> x6, waiting for transfers between devices: 116 us -> 17.3 us  [shift_wz(): return lax.ppermute(value, ('w', 'z'), pairs)]
    ppermute x42 -> x36, waiting for transfers between devices: 126 us -> 69.1 us  [shift(): return lax.ppermute(value, axis, [(i, (i + by) % n) for i in range(n)])]
    all_gather x3, waiting for transfers between devices: 32 us -> 0.02 us  [gather_line(): return lax.all_gather(own, ('core', 'w', 'z'), axis=0, tiled=True)]
    reduce_scatter x2, waiting for transfers between devices: 0.01 us -> 25.1 us  [scatter_line(): return lax.psum_scatter(rows, ('w', 'z'), scatter_dimension=0, tiled=True)]
    ppermute x12 -> x6, starting transfers between devices: 22.7 us -> 12 us  [shift_wz(): return lax.ppermute(value, ('w', 'z'), pairs)]
    dot_general x23, matrix products: 83.2 us -> 93.3 us  [matmul(): return jnp.dot(left, right, preferred_element_type=F32)]
    dot_general x15, matrix products: 67.2 us -> 76.4 us  [matmul_nt(): return jnp.einsum('ij,kj->ik', left, right, preferred_element_type=F32)]
  transfers between devices with their start and end apart: 67 -> 55, of which waited for: 27 -> 19; matrix products, arithmetic and copies ran while one was open for 41% -> 47% of each run, Pallas kernels for 5% -> 22%
where the time goes in v3:
time: 779 us; the launch traced here: 770 us
  matrix products  217 us (28%)
  Pallas kernels  173 us (22%)
  waiting for transfers between devices  112 us (14%)
  local copies, waits for them, and re-layouts  105 us (13%)
  other arithmetic  91.5 us (12%)
  starting transfers between devices  54.1 us (7%)
  between operations  17.2 us (2%)
    dot_general x23, matrix products, matmul(): return jnp.dot(left, right, preferred_element_type=F32)  93.3 us
    pallas_call x1, Pallas kernels, gather_attend(): pl.pallas_call(functools.partial(gather_attend_kernel, sizes), out_shape=...  93 us
    pallas_call x1, Pallas kernels, attend_back(): pl.pallas_call(functools.partial(attend_back_kernel, sizes), out_shape=(j...  80 us
    dot_general x15, matrix products, matmul_nt(): return jnp.einsum('ij,kj->ik', left, right, preferred_element_type=F32)  76.4 us
    ppermute x36, waiting for transfers between devices, shift(): return lax.ppermute(value, axis, [(i, (i + by) % n) for i in range(n)])  69.1 us
    dot_general x6, matrix products, matmul_tn(): return jnp.einsum('ji,jk->ik', left, right, preferred_element_type=F32)  44.3 us
    ppermute x36, starting transfers between devices, shift(): return lax.ppermute(value, axis, [(i, (i + by) % n) for i in range(n)])  40.8 us
    reduce_scatter x2, waiting for transfers between devices, scatter_line(): return lax.psum_scatter(rows, ('w', 'z'), scatter_dimension=0, tiled=True)  25.1 us
  transfers between devices with their start and end apart: 55, of which 19 were waited for; matrix products, arithmetic and copies ran while one was open for 47% of the time, Pallas kernels for 22%

profile of v3, /device:TPU:0, one launch (start us, length us, event | category | flops | bytes accessed | tf_op | source)
XLA Modules:
  0.0 769.5 jit_solution(6759860635114737612)
XLA Ops:
  23.6 8.2 %collective-permute-done.2 = bf16[128,768]{1,0:T(8,128)(2,1)S(1)} collective-permute-done((bf16[128,768]{1,0:T(8,128)(2,1)S(1)}, bf16[128,768]{1,0:T(8,128)(2,1)S(1)}, u32[]{:S(2)}, u32[]{:S(2)}) %collective-permute-start.2) | collective-permute-done | bytes 196640 | tf_op jit(solution)/shard_map/ppermute | solution.py:43
  34.9 16.4 %collective-permute-done.4 = bf16[512,768]{1,0:T(8,128)(2,1)S(1)} collective-permute-done((bf16[512,768]{1,0:T(8,128)(2,1)S(1)}, bf16[512,768]{1,0:T(8,128)(2,1)S(1)}, u32[]{:S(2)}, u32[]{:S(2)}) %collective-permute-start.4) | collective-permute-done | bytes 786464 | tf_op jit(solution)/shard_map/ppermute | solution.py:36
  78.3 9.5 %collective-permute-done.9 = bf16[1,2,2,36,1728]{4,2,3,1,0:T(2,128)(2,1)S(1)} collective-permute-done((bf16[1,2,2,36,1728]{4,2,3,1,0:T(2,128)(2,1)S(1)}, bf16[1,2,2,36,1728]{4,2,3,1,0:T(2,128)(2,1)S(1)}, u32[]{:S(2)}, u32[]{:S(2)}) %collective-permute-start.9) | collective-permute-done | bytes 497696 | tf_op jit(solution)/shard_map/ppermute | solution.py:36
  110.6 6.4 fusion.118
  134.0 93.0 %shard_map.316 = (bf16[4096,512]{1,0:T(8,128)(2,1)}, bf16[512,1024]{1,0:T(8,128)(2,1)}, bf16[512,1024]{1,0:T(8,128)(2,1)}, f32[1,2048]{1,0:T(1,128)}) custom-call(bf16[512,512]{1,0:T(8,128)(2,1)} %pad_maximum_fusion.15.own_ref, f32[512,1024]{1,0:T(8,128)} %pad_maximum_fusion.8.raw_ref, f32[1,256]{1,0:T(1,128)} %reshape_reshape.3.gain_ref, ...), custom_call_target="tpu_custom_call" | custom-call | flops 49999998976 | bytes 16777216 | tf_op jit(solution)/shard_map/pallas_call | solution.py:592
  241.3 6.4 fusion.205
  247.7 8.4 %multiply_convert_fusion.11 = (bf16[512,1728]{0,1:T(8,128)(2,1)S(1)}, f32[512,1728]{0,1:T(8,128)}) fusion(f32[512,1728]{0,1:T(8,128)} %fusion.205, bf16[512,1152]{1,0:T(8,128)(2,1)S(1)} %multiply_convert_fusion.12, bf16[1152,1728]{1,0:T(8,128)(2,1)} %all-gather.8.cloned.1.call-done), kind=kOutput, calls=%fused_computation.99 | convolution fusion | flops 2047279104 | bytes 14008320 | tf_op jit(solution)/shard_map/dot_general | solution.py:225
  256.1 8.2 %collective-permute-done.13 = bf16[512,1152]{1,0:T(8,128)(2,1)S(1)} collective-permute-done((bf16[512,1152]{1,0:T(8,128)(2,1)S(1)}, bf16[512,1152]{1,0:T(8,128)(2,1)S(1)}, u32[]{:S(2)}, u32[]{:S(2)}) %collective-permute-start.13) | collective-permute-done | bytes 1179680 | tf_op jit(solution)/shard_map/ppermute | solution.py:36
  271.0 7.6 multiply_convert_fusion.10
  287.6 7.1 multiply_convert_fusion.9
  306.0 7.2 multiply_convert_fusion.8
  322.3 8.1 %collective-permute-done.16 = bf16[256,1152]{1,0:T(8,128)(2,1)S(1)} collective-permute-done((bf16[256,1152]{1,0:T(8,128)(2,1)S(1)}, bf16[256,1152]{1,0:T(8,128)(2,1)S(1)}, u32[]{:S(2)}, u32[]{:S(2)}) %collective-permute-start.16) | collective-permute-done | bytes 589856 | tf_op jit(solution)/shard_map/ppermute | solution.py:36
  337.5 6.3 collective-permute-done.17
  351.8 5.6 multiply_convert_fusion.6
  362.2 7.6 convolution_add_fusion.4
  369.9 5.3 collective-permute-done.23
  387.6 6.4 multiply_convert_fusion.4
  402.0 7.0 multiply_convert_fusion
  411.7 6.4 fusion.215
  418.0 5.7 convolution_add_fusion.1
  428.0 11.9 %convolution_convert_fusion.2 = bf16[1728,1152]{1,0:T(8,128)(2,1)S(1)} fusion(bf16[2048,1728]{0,1:T(8,128)(2,1)S(1)} %bitcast.306, bf16[2048,1152]{1,0:T(8,128)(2,1)} %constant_dynamic-update-slice_fusion.13), kind=kOutput, calls=%fused_computation.2 | convolution fusion | flops 8155717632 | bytes 15777792 | tf_op jit(solution)/shard_map/ji,jk->ik/dot_general | solution.py:233
  447.8 13.4 %convolution_convert_fusion.1 = bf16[1152,1728]{0,1:T(8,128)(2,1)} fusion(bf16[2048,1728]{0,1:T(8,128)(2,1)S(1)} %pad_maximum_fusion, bf16[2048,1152]{1,0:T(8,128)(2,1)} %copy-done.71), kind=kOutput, calls=%fused_computation.1 | convolution fusion | flops 8155717632 | bytes 15777792 | tf_op jit(solution)/shard_map/ji,jk->ik/dot_general | solution.py:233
  461.1 10.7 %convolution_convert_fusion = bf16[1152,1728]{0,1:T(8,128)(2,1)} fusion(bf16[2048,1728]{0,1:T(8,128)(2,1)S(1)} %pad_maximum_fusion.1, bf16[2048,1152]{1,0:T(8,128)(2,1)S(1)} %bitcast.337), kind=kOutput, calls=%fused_computation | convolution fusion | flops 8155717632 | bytes 15777792 | tf_op jit(solution)/shard_map/ji,jk->ik/dot_general | solution.py:233
  471.9 6.4 copy.135
  478.3 6.4 copy.136
  519.7 80.0 %shard_map.317 = (f32[512,1024]{1,0:T(8,128)}, f32[512,512]{1,0:T(8,128)}) custom-call(bf16[512,1024]{1,0:T(8,128)(2,1)} %get-tuple-element.89.q_ref, bf16[512,1024]{1,0:T(8,128)(2,1)} %convolution_convert_fusion.7.grad_ref, f32[1,2048]{1,0:T(1,128)} %get-tuple-element.91.log_ref, f32[1,2048]{1,0:T(1,128)} %bitcast.380, ...), custom_call_target="tpu_custom_call" | custom-call | flops 49999998976 | bytes 16777216 | tf_op jit(solution)/shard_map/pallas_call | solution.py:619
  649.5 12.1 %reduce-scatter.6.cloned.1.call-done = bf16[144,1728]{1,0:T(8,128)(2,1)} async-done(((bf16[576,1728]{1,0:T(8,128)(2,1)}), bf16[144,1728]{1,0:T(8,128)(2,1)}) %reduce-scatter.6.cloned.1.call-update) | async-done | bytes 497680 | tf_op jit(solution)/shard_map/reduce_scatter | solution.py:64
  668.6 7.2 fusion.120
  675.8 8.9 %fusion.95 = (f32[512]{0:T(512)S(1)}, f32[512,1152]{1,0:T(8,128)}) fusion(bf16[512,1152]{1,0:T(8,128)(2,1)} %get-tuple-element.261, f32[1152]{0:T(1024)S(1)} %mul.1200, f32[512,1152]{1,0:T(8,128)} %fusion.120, bf16[512,768]{1,0:T(8,128)(2,1)} %get-tuple-element.103, s32[1152]{0:T(1024)S(1)} %copy-done.136, bf16[1152,768]{1,0:T(8,128)(2,1)} %bitcast.326, ...), kind=kOutput, calls=%fused_computation.151 | convolution fusion | flops 2950446592 | bytes 10234881 | tf_op jit(solution)/shard_map/ij,kj->ik/dot_general | solution.py:229
  684.8 5.3 fusion.69
  693.3 13.0 %reduce-scatter.8.cloned.1.call-done = bf16[144,1728]{1,0:T(8,128)(2,1)} async-done(((bf16[576,1728]{1,0:T(8,128)(2,1)}), bf16[144,1728]{1,0:T(8,128)(2,1)}) %reduce-scatter.8.cloned.1.call-update) | async-done | bytes 497680 | tf_op jit(solution)/shard_map/reduce_scatter | solution.py:64
  710.8 5.9 collective-permute-done.46
  (670 shorter events, 334.3 us)
Async XLA Ops:
  7.3 126.7 %all-gather.4.cloned.1.call-start = ((), (), s32[]{:S(2)}) async-start(), calls=%async_computation.3 | async-start | bytes 4478976 | tf_op jit(solution)/shard_map/all_gather | solution.py:55
  31.8 19.5 %collective-permute-start.4 = (bf16[512,768]{1,0:T(8,128)(2,1)S(1)}, bf16[512,768]{1,0:T(8,128)(2,1)S(1)}, u32[]{:S(2)}, u32[]{:S(2)}) collective-permute-start(bf16[512,768]{1,0:T(8,128)(2,1)S(1)} %constant_dynamic-update-slice_fusion.21), channel_id=1, source_target_pairs={{0,1},{1,0},{2,3},{3,2},{4,5},{5,4},{6,7},{7,6},{8,9},{9,8},{10,11... | collective-permute-start | bytes 2359304 | tf_op jit(solution)/shard_map/ppermute | solution.py:36
  33.4 19.5 %collective-permute-start.5 = (bf16[512,768]{1,0:T(8,128)(2,1)S(1)}, bf16[512,768]{1,0:T(8,128)(2,1)S(1)}, u32[]{:S(2)}, u32[]{:S(2)}) collective-permute-start(bf16[512,768]{1,0:T(8,128)(2,1)S(1)} %constant_dynamic-update-slice_fusion.21), channel_id=1, source_target_pairs={{0,16},{16,0},{1,17},{17,1},{2,18},{18,2},{3,19},{19,3},{4,20},{20... | collective-permute-start | bytes 2359304 | tf_op jit(solution)/shard_map/ppermute | solution.py:36
  63.8 30.8 %collective-permute-start.8 = (bf16[2048,768]{1,0:T(8,128)(2,1)}, bf16[2048,768]{1,0:T(8,128)(2,1)}, u32[]{:S(2)}, u32[]{:S(2)}) collective-permute-start(bf16[2048,768]{1,0:T(8,128)(2,1)} %maximum_dynamic-update-slice_fusion), channel_id=1, source_target_pairs={{0,8},{8,0},{1,9},{9,1},{2,10},{10,2},{3,11},{11,3},{4,12},{12,4},... | collective-permute-start | bytes 9437192 | tf_op jit(solution)/shard_map/ppermute | solution.py:46
  65.9 175.3 %all-gather.6.cloned.1.call-start = ((), (), s32[]{:S(2)}) async-start(), calls=%async_computation.4 | async-start | bytes 4644864 | tf_op jit(solution)/shard_map/all_gather | solution.py:55
  90.2 19.2 %collective-permute-start.10 = (bf16[2,1,2,36,1728]{4,2,3,1,0:T(2,128)(2,1)}, bf16[2,1,2,36,1728]{4,2,3,1,0:T(2,128)(2,1)}, u32[]{:S(2)}, u32[]{:S(2)}) collective-permute-start(bf16[2,1,2,36,1728]{4,2,3,1,0:T(2,128)(2,1)} %get-tuple-element.198), channel_id=1, source_target_pairs={{0,1},{1,0},{2,3},{3,2},{4,5},{5,4},{6,7},{7,6},{8,9},{9,8},{10,11... | collective-permute-start | bytes 1493000 | tf_op jit(solution)/shard_map/ppermute | solution.py:36
  118.0 129.8 %all-gather.8.cloned.1.call-start = ((), (), s32[]{:S(2)}) async-start(), calls=%async_computation.5 | async-start | bytes 4644864 | tf_op jit(solution)/shard_map/all_gather | solution.py:55
  133.9 512.3 %reduce-scatter.10.cloned.1.call-start = ((), (), s32[]{:S(2)}) async-start(), calls=%async_computation.8 | async-start | bytes 2488320
  236.8 27.4 %collective-permute-start.13 = (bf16[512,1152]{1,0:T(8,128)(2,1)S(1)}, bf16[512,1152]{1,0:T(8,128)(2,1)S(1)}, u32[]{:S(2)}, u32[]{:S(2)}) collective-permute-start(bf16[512,1152]{1,0:T(8,128)(2,1)S(1)} %multiply_convert_fusion.12), channel_id=1, source_target_pairs={{0,16},{16,0},{1,17},{17,1},{2,18},{18,2},{3,19},{19,3},{4,20},{20... | collective-permute-start | bytes 3538952 | tf_op jit(solution)/shard_map/ppermute | solution.py:36
  238.3 26.8 %collective-permute-start.11 = (bf16[512,1152]{1,0:T(8,128)(2,1)S(1)}, bf16[512,1152]{1,0:T(8,128)(2,1)S(1)}, u32[]{:S(2)}, u32[]{:S(2)}) collective-permute-start(bf16[512,1152]{1,0:T(8,128)(2,1)S(1)} %multiply_convert_fusion.12), channel_id=1, source_target_pairs={{0,1},{1,0},{2,3},{3,2},{4,5},{5,4},{6,7},{7,6},{8,9},{9,8},{10,11... | collective-permute-start | bytes 3538952 | tf_op jit(solution)/shard_map/ppermute | solution.py:36
  265.4 35.9 %collective-permute-start.14 = (bf16[256,1152]{1,0:T(8,128)(2,1)S(1)}, bf16[256,1152]{1,0:T(8,128)(2,1)S(1)}, u32[]{:S(2)}, u32[]{:S(2)}) collective-permute-start(bf16[256,1152]{1,0:T(8,128)(2,1)S(1)} %slice.367), channel_id=1, source_target_pairs={{0,1},{1,0},{2,3},{3,2},{4,5},{5,4},{6,7},{7,6},{8,9},{9,8},{10,11... | collective-permute-start | bytes 1769480 | tf_op jit(solution)/shard_map/ppermute | solution.py:36
  266.3 35.1 %collective-permute-start.15 = (bf16[256,1152]{1,0:T(8,128)(2,1)S(1)}, bf16[256,1152]{1,0:T(8,128)(2,1)S(1)}, u32[]{:S(2)}, u32[]{:S(2)}) collective-permute-start(bf16[256,1152]{1,0:T(8,128)(2,1)S(1)} %slice.368), channel_id=1, source_target_pairs={{0,16},{16,0},{1,17},{17,1},{2,18},{18,2},{3,19},{19,3},{4,20},{20... | collective-permute-start | bytes 1769480 | tf_op jit(solution)/shard_map/ppermute | solution.py:36
  281.3 56.1 %collective-permute-start.12 = (bf16[256,1152]{1,0:T(8,128)(2,1)S(1)}, bf16[256,1152]{1,0:T(8,128)(2,1)S(1)}, u32[]{:S(2)}, u32[]{:S(2)}) collective-permute-start(bf16[256,1152]{1,0:T(8,128)(2,1)S(1)} %slice.595), channel_id=1, source_target_pairs={{0,1},{1,0},{2,3},{3,2},{4,5},{5,4},{6,7},{7,6},{8,9},{9,8},{10,11... | collective-permute-start | bytes 1769480 | tf_op jit(solution)/shard_map/ppermute | solution.py:36
  299.9 37.5 %collective-permute-start.18 = (bf16[256,1152]{1,0:T(8,128)(2,1)S(1)}, bf16[256,1152]{1,0:T(8,128)(2,1)S(1)}, u32[]{:S(2)}, u32[]{:S(2)}) collective-permute-start(bf16[256,1152]{1,0:T(8,128)(2,1)S(1)} %slice.594), channel_id=1, source_target_pairs={{0,16},{16,0},{1,17},{17,1},{2,18},{18,2},{3,19},{19,3},{4,20},{20... | collective-permute-start | bytes 1769480 | tf_op jit(solution)/shard_map/ppermute | solution.py:36
  349.7 25.5 %collective-permute-start.23 = (bf16[512,1152]{1,0:T(8,128)(2,1)S(1)}, bf16[512,1152]{1,0:T(8,128)(2,1)S(1)}, u32[]{:S(2)}, u32[]{:S(2)}) collective-permute-start(bf16[512,1152]{1,0:T(8,128)(2,1)S(1)} %fusion.86), channel_id=1, source_target_pairs={{0,16},{16,0},{1,17},{17,1},{2,18},{18,2},{3,19},{19,3},{4,20},{20... | collective-permute-start | bytes 3538952 | tf_op jit(solution)/shard_map/ppermute | solution.py:36
  350.8 25.2 %collective-permute-start.21 = (bf16[512,1152]{1,0:T(8,128)(2,1)S(1)}, bf16[512,1152]{1,0:T(8,128)(2,1)S(1)}, u32[]{:S(2)}, u32[]{:S(2)}) collective-permute-start(bf16[512,1152]{1,0:T(8,128)(2,1)S(1)} %fusion.86), channel_id=1, source_target_pairs={{0,1},{1,0},{2,3},{3,2},{4,5},{5,4},{6,7},{7,6},{8,9},{9,8},{10,11... | collective-permute-start | bytes 3538952 | tf_op jit(solution)/shard_map/ppermute | solution.py:36
  376.0 25.9 %collective-permute-start.25 = (bf16[256,1152]{1,0:T(8,128)(2,1)S(1)}, bf16[256,1152]{1,0:T(8,128)(2,1)S(1)}, u32[]{:S(2)}, u32[]{:S(2)}) collective-permute-start(bf16[256,1152]{1,0:T(8,128)(2,1)S(1)} %slice.379), channel_id=1, source_target_pairs={{0,16},{16,0},{1,17},{17,1},{2,18},{18,2},{3,19},{19,3},{4,20},{20... | collective-permute-start | bytes 1769480 | tf_op jit(solution)/shard_map/ppermute | solution.py:36
  377.0 25.0 %collective-permute-start.24 = (bf16[256,1152]{1,0:T(8,128)(2,1)S(1)}, bf16[256,1152]{1,0:T(8,128)(2,1)S(1)}, u32[]{:S(2)}, u32[]{:S(2)}) collective-permute-start(bf16[256,1152]{1,0:T(8,128)(2,1)S(1)} %slice.378), channel_id=1, source_target_pairs={{0,1},{1,0},{2,3},{3,2},{4,5},{5,4},{6,7},{7,6},{8,9},{9,8},{10,11... | collective-permute-start | bytes 1769480 | tf_op jit(solution)/shard_map/ppermute | solution.py:36
  441.5 64.4 %collective-permute-start.48 = (bf16[864,1152]{1,0:T(8,128)(2,1)}, bf16[864,1152]{1,0:T(8,128)(2,1)}, u32[]{:S(2)}, u32[]{:S(2)}) collective-permute-start(bf16[864,1152]{1,0:T(8,128)(2,1)} %dynamic-slice_bitcast_fusion.2), channel_id=1, source_target_pairs={{0,8},{8,0},{1,9},{9,1},{2,10},{10,2},{3,11},{11,3},{4,12},{12,4},... | collective-permute-start | bytes 5971976 | tf_op jit(solution)/shard_map/ppermute | solution.py:46
  442.7 46.7 %collective-permute-start.27 = (bf16[256,1152]{1,0:T(8,128)(2,1)}, bf16[256,1152]{1,0:T(8,128)(2,1)S(1)}, u32[]{:S(2)}, u32[]{:S(2)}) collective-permute-start(bf16[256,1152]{1,0:T(8,128)(2,1)} %get-tuple-element.168), channel_id=1, source_target_pairs={{0,16},{16,0},{1,17},{17,1},{2,18},{18,2},{3,19},{19,3},{4,20},{20... | collective-permute-start | bytes 1769480 | tf_op jit(solution)/shard_map/ppermute | solution.py:36
  444.6 44.8 %collective-permute-start.22 = (bf16[256,1152]{1,0:T(8,128)(2,1)}, bf16[256,1152]{1,0:T(8,128)(2,1)S(1)}, u32[]{:S(2)}, u32[]{:S(2)}) collective-permute-start(bf16[256,1152]{1,0:T(8,128)(2,1)} %get-tuple-element.166), channel_id=1, source_target_pairs={{0,1},{1,0},{2,3},{3,2},{4,5},{5,4},{6,7},{7,6},{8,9},{9,8},{10,11... | collective-permute-start | bytes 1769480 | tf_op jit(solution)/shard_map/ppermute | solution.py:36
  445.4 44.5 %collective-permute-start.30 = (bf16[256,1152]{1,0:T(8,128)(2,1)S(1)}, bf16[256,1152]{1,0:T(8,128)(2,1)S(1)}, u32[]{:S(2)}, u32[]{:S(2)}) collective-permute-start(bf16[256,1152]{1,0:T(8,128)(2,1)S(1)} %get-tuple-element.167), channel_id=1, source_target_pairs={{0,1},{1,0},{2,3},{3,2},{4,5},{5,4},{6,7},{7,6},{8,9},{9,8},{10,11... | collective-permute-start | bytes 1769480 | tf_op jit(solution)/shard_map/ppermute | solution.py:36
  446.6 43.3 %collective-permute-start.28 = (bf16[256,1152]{1,0:T(8,128)(2,1)S(1)}, bf16[256,1152]{1,0:T(8,128)(2,1)S(1)}, u32[]{:S(2)}, u32[]{:S(2)}) collective-permute-start(bf16[256,1152]{1,0:T(8,128)(2,1)S(1)} %get-tuple-element.169), channel_id=1, source_target_pairs={{0,16},{16,0},{1,17},{17,1},{2,18},{18,2},{3,19},{19,3},{4,20},{20... | collective-permute-start | bytes 1769480 | tf_op jit(solution)/shard_map/ppermute | solution.py:36
  489.4 20.0 %collective-permute-start.31 = (bf16[576,1728]{1,0:T(8,128)(2,1)}, bf16[576,1728]{1,0:T(8,128)(2,1)}, u32[]{:S(2)}, u32[]{:S(2)}) collective-permute-start(bf16[576,1728]{1,0:T(8,128)(2,1)} %dynamic-slice_bitcast_fusion.1), channel_id=1, source_target_pairs={{0,8},{8,0},{1,9},{9,1},{2,10},{10,2},{3,11},{11,3},{4,12},{12,4},... | collective-permute-start | bytes 5971976 | tf_op jit(solution)/shard_map/ppermute | solution.py:46
  489.4 23.9 %collective-permute-start.32 = (bf16[576,1728]{1,0:T(8,128)(2,1)}, bf16[576,1728]{1,0:T(8,128)(2,1)}, u32[]{:S(2)}, u32[]{:S(2)}) collective-permute-start(bf16[576,1728]{1,0:T(8,128)(2,1)} %dynamic-slice_bitcast_fusion), channel_id=1, source_target_pairs={{0,8},{8,0},{1,9},{9,1},{2,10},{10,2},{3,11},{11,3},{4,12},{12,4},... | collective-permute-start | bytes 5971976 | tf_op jit(solution)/shard_map/ppermute | solution.py:46
  509.3 152.3 %reduce-scatter.6.cloned.1.call-start = ((), (), s32[]{:S(2)}) async-start(), calls=%async_computation.6 | async-start | bytes 2580480 | tf_op jit(solution)/shard_map/reduce_scatter | solution.py:64
  612.8 93.5 %reduce-scatter.8.cloned.1.call-start = ((), (), s32[]{:S(2)}) async-start(), calls=%async_computation.7 | async-start | bytes 2580480 | tf_op jit(solution)/shard_map/reduce_scatter | solution.py:64
  664.3 56.3 %collective-permute-start.38 = (bf16[256,768]{1,0:T(8,128)(2,1)}, bf16[256,768]{1,0:T(8,128)(2,1)}, u32[]{:S(2)}, u32[]{:S(2)}) collective-permute-start(bf16[256,768]{1,0:T(8,128)(2,1)} %get-tuple-element.156), channel_id=1, source_target_pairs={{0,16},{16,0},{1,17},{17,1},{2,18},{18,2},{3,19},{19,3},{4,20},{20... | collective-permute-start | bytes 1179656 | tf_op jit(solution)/shard_map/ppermute | solution.py:36
  665.7 72.2 %collective-permute-start.34 = (bf16[256,768]{1,0:T(8,128)(2,1)}, bf16[256,768]{1,0:T(8,128)(2,1)}, u32[]{:S(2)}, u32[]{:S(2)}) collective-permute-start(bf16[256,768]{1,0:T(8,128)(2,1)} %get-tuple-element.154), channel_id=1, source_target_pairs={{0,1},{1,0},{2,3},{3,2},{4,5},{5,4},{6,7},{7,6},{8,9},{9,8},{10,11... | collective-permute-start | bytes 1179656 | tf_op jit(solution)/shard_map/ppermute | solution.py:36
  668.1 39.5 %collective-permute-start.44 = (bf16[1,2,36,1728]{3,2,1,0:T(8,128)(2,1)}, bf16[1,2,36,1728]{3,2,1,0:T(8,128)(2,1)}, u32[]{:S(2)}, u32[]{:S(2)}) collective-permute-start(bf16[1,2,36,1728]{3,2,1,0:T(8,128)(2,1)} %constant_dynamic-slice_fusion.1), channel_id=1, source_target_pairs={{0,16},{16,0},{1,17},{17,1},{2,18},{18,2},{3,19},{19,3},{4,20},{20... | collective-permute-start | bytes 746504 | tf_op jit(solution)/shard_map/ppermute | solution.py:36
  691.3 28.7 %collective-permute-start.35 = (bf16[256,768]{1,0:T(8,128)(2,1)}, bf16[256,768]{1,0:T(8,128)(2,1)}, u32[]{:S(2)}, u32[]{:S(2)}) collective-permute-start(bf16[256,768]{1,0:T(8,128)(2,1)} %get-tuple-element.155), channel_id=1, source_target_pairs={{0,1},{1,0},{2,3},{3,2},{4,5},{5,4},{6,7},{7,6},{8,9},{9,8},{10,11... | collective-permute-start | bytes 1179656 | tf_op jit(solution)/shard_map/ppermute | solution.py:36
  691.9 46.1 %collective-permute-start.37 = (bf16[256,768]{1,0:T(8,128)(2,1)}, bf16[256,768]{1,0:T(8,128)(2,1)}, u32[]{:S(2)}, u32[]{:S(2)}) collective-permute-start(bf16[256,768]{1,0:T(8,128)(2,1)} %get-tuple-element.157), channel_id=1, source_target_pairs={{0,16},{16,0},{1,17},{17,1},{2,18},{18,2},{3,19},{19,3},{4,20},{20... | collective-permute-start | bytes 1179656 | tf_op jit(solution)/shard_map/ppermute | solution.py:36
  (172 other events, 1399.7 us)
Sparse Core Ops, SparseCore 0:
  66.1 47.1 all-gather.3
  118.1 80.6 all-gather.5
  201.0 45.2 all-gather.7
  509.4 54.6 reduce-scatter.9
  613.0 48.5 reduce-scatter.5
  663.8 42.4 reduce-scatter.7

commit v4 on v3

--- a/solution.py
+++ b/solution.py
@@ -144,14 +144,14 @@
             full = lax.dynamic_update_slice(full, block, ((x * size["y"] + y) * line, 0))
         return full, mine, list(near.values())
 
-    def scatter_chips(self, full, hold):
+    def scatter_chips(self, full):
         size, at = self.size, self.at
         full = full.reshape((size["x"], size["y"], -1, full.shape[-1]))
         parts = [
             full[(at["x"] - dx) % size["x"], (at["y"] - dy) % size["y"]].astype(F32)
             for dx, dy in self.plane_steps()
         ]
-        mine = after(self.scatter_plane(parts), hold)
+        mine = self.scatter_plane(parts)
         mine = mine.reshape((size["w"], size["z"], -1, mine.shape[-1]))
         total = None
         for kw, kz in reversed(self.wz_steps()):
@@ -959,7 +959,6 @@
     gate_terms = place.cores_summed(gate_terms)
     up_terms = place.cores_summed(up_terms)
     down_rows = place.scatter_line(down_terms)
-    gate_rows = place.scatter_line(gate_terms)
 
     mixed_part, feed_term = norm_back(normed_two_grad, mixed, factor_two, feed_scale)
     mixed_grad = out_grad + mixed_part
@@ -967,7 +966,7 @@
     projected_grad = projected_grad.astype(BF)
     output_terms = matmul_tn(attended, projected_grad).astype(BF)
     attended_grad = matmul_nt(projected_grad, output_full).astype(BF)
-    attended_grad = after(attended_grad, gate_terms, up_terms)
+    attended_grad = after(attended_grad, down_terms)
     delta = jnp.stack(
         [
             jnp.sum(
@@ -988,7 +987,13 @@
         )
         key_value_grad = place.scatter_group(key_value_terms)
     output_terms = after(output_terms, key_value_grad)
-    up_rows = place.scatter_line(up_terms)
+    share = gate_terms.shape[0] // (nw * nz)
+    gate_up_terms = jnp.stack(
+        [t.reshape(nw * nz, share, part) for t in (gate_terms, up_terms)], axis=1
+    )
+    gate_up_rows = place.scatter_line(after(gate_up_terms.reshape(-1, part), key_value_grad))
+    key_value_grad = after(key_value_grad, down_rows)
+    gate_rows, up_rows = gate_up_rows[:share], gate_up_rows[share:]
     down_weight_grad = matmul(down_rows, to_outside)
 
     def whole_rows(own_part):
@@ -1053,7 +1058,7 @@
         ).reshape(-1, head_width)
 
     first_terms = terms_of(core).astype(F32) + place.swap_core(terms_of(1 - core)).astype(F32)
-    first_terms = after(first_terms.astype(BF), gate_rows)
+    first_terms = first_terms.astype(BF)
     normed_grad = 0.0
     for half, grad in zip(in_order(*projections), raw_grad):
         half = matmul(inside_from_first, half).astype(BF)
@@ -1061,7 +1066,7 @@
     tokens_part, _ = norm_back(normed_grad, tokens_in, factor_one, gain_one)
     tokens_grad = reorder((mixed_grad + tokens_part).astype(BF), to_outside)
 
-    first_grad = place.scatter_chips(first_terms, up_rows)
+    first_grad = place.scatter_chips(first_terms)
     projection_rows = first_grad[: 2 * rows].reshape(2, rows, head_width)
     projection_rows = cores_in_order(
         pick(projection_rows, core), place.swap_core(pick(projection_rows, 1 - core))

time: 779 us -> 789 us (1.013)
  waiting for transfers between devices: 112 us -> 130 us
  matrix products: 217 us -> 201 us
  starting transfers between devices: 54.1 us -> 62.8 us
    ppermute x6, waiting for transfers between devices: 17.3 us -> 48 us  [shift_wz(): return lax.ppermute(value, ('w', 'z'), pairs)]
    reduce_scatter x2 -> x1, waiting for transfers between devices: 25.1 us -> 0.01 us  [scatter_line(): return lax.psum_scatter(rows, ('w', 'z'), scatter_dimension=0, tiled=True)]
    ppermute x36, waiting for transfers between devices: 69.1 us -> 81.5 us  [shift(): return lax.ppermute(value, axis, [(i, (i + by) % n) for i in range(n)])]
    dot_general x23, matrix products: 93.3 us -> 84.6 us  [matmul(): return jnp.dot(left, right, preferred_element_type=F32)]
    ppermute x6, starting transfers between devices: 12 us -> 20.3 us  [shift_wz(): return lax.ppermute(value, ('w', 'z'), pairs)]
    unnamed x321 -> x339, local copies, waits for them, and re-layouts: 18.7 us -> 19.5 us
  transfers between devices with their start and end apart: 55 -> 54, of which waited for: 19 -> 21; matrix products, arithmetic and copies ran while one was open for 47% -> 44% of each run, Pallas kernels for 22% -> 23%
where the time goes in v4:
time: 789 us; the launch traced here: 781 us
  matrix products  201 us (25%)
  Pallas kernels  176 us (22%)
  waiting for transfers between devices  130 us (16%)
  local copies, waits for them, and re-layouts  111 us (14%)
  other arithmetic  83.8 us (11%)
  starting transfers between devices  62.8 us (8%)
  between operations  17 us (2%)
    pallas_call x1, Pallas kernels, gather_attend(): pl.pallas_call(functools.partial(gather_attend_kernel, sizes), out_shape=...  93.1 us
    dot_general x23, matrix products, matmul(): return jnp.dot(left, right, preferred_element_type=F32)  84.6 us
    pallas_call x1, Pallas kernels, attend_back(): pl.pallas_call(functools.partial(attend_back_kernel, sizes), out_shape=(j...  82.9 us
    ppermute x36, waiting for transfers between devices, shift(): return lax.ppermute(value, axis, [(i, (i + by) % n) for i in range(n)])  81.5 us
    dot_general x15, matrix products, matmul_nt(): return jnp.einsum('ij,kj->ik', left, right, preferred_element_type=F32)  71.9 us
    ppermute x6, waiting for transfers between devices, shift_wz(): return lax.ppermute(value, ('w', 'z'), pairs)  48 us
    dot_general x6, matrix products, matmul_tn(): return jnp.einsum('ji,jk->ik', left, right, preferred_element_type=F32)  41.5 us
    ppermute x36, starting transfers between devices, shift(): return lax.ppermute(value, axis, [(i, (i + by) % n) for i in range(n)])  41.2 us
  transfers between devices with their start and end apart: 54, of which 21 were waited for; matrix products, arithmetic and copies ran while one was open for 44% of the time, Pallas kernels for 23%

profile of v4, /device:TPU:0, one launch (start us, length us, event | category | flops | bytes accessed | tf_op | source)
XLA Modules:
  0.0 780.9 jit_solution(16024342987201215038)
XLA Ops:
  23.6 8.2 %collective-permute-done.2 = bf16[128,768]{1,0:T(8,128)(2,1)S(1)} collective-permute-done((bf16[128,768]{1,0:T(8,128)(2,1)S(1)}, bf16[128,768]{1,0:T(8,128)(2,1)S(1)}, u32[]{:S(2)}, u32[]{:S(2)}) %collective-permute-start.2) | collective-permute-done | bytes 196640 | tf_op jit(solution)/shard_map/ppermute | solution.py:43
  34.9 16.4 %collective-permute-done.5 = bf16[512,768]{1,0:T(8,128)(2,1)S(1)} collective-permute-done((bf16[512,768]{1,0:T(8,128)(2,1)S(1)}, bf16[512,768]{1,0:T(8,128)(2,1)S(1)}, u32[]{:S(2)}, u32[]{:S(2)}) %collective-permute-start.5) | collective-permute-done | bytes 786464 | tf_op jit(solution)/shard_map/ppermute | solution.py:36
  79.9 9.2 %collective-permute-done.9 = bf16[1,2,2,36,1728]{4,2,3,1,0:T(2,128)(2,1)S(1)} collective-permute-done((bf16[1,2,2,36,1728]{4,2,3,1,0:T(2,128)(2,1)S(1)}, bf16[1,2,2,36,1728]{4,2,3,1,0:T(2,128)(2,1)S(1)}, u32[]{:S(2)}, u32[]{:S(2)}) %collective-permute-start.9) | collective-permute-done | bytes 497696 | tf_op jit(solution)/shard_map/ppermute | solution.py:36
  115.6 7.3 fusion.118
  141.9 93.1 %shard_map.316 = (bf16[4096,512]{1,0:T(8,128)(2,1)}, bf16[512,1024]{1,0:T(8,128)(2,1)}, bf16[512,1024]{1,0:T(8,128)(2,1)}, f32[1,2048]{1,0:T(1,128)}) custom-call(bf16[512,512]{1,0:T(8,128)(2,1)} %pad_maximum_fusion.16.own_ref, f32[512,1024]{1,0:T(8,128)} %pad_maximum_fusion.9.raw_ref, f32[1,256]{1,0:T(1,128)} %reshape_reshape.3.gain_ref, ...), custom_call_target="tpu_custom_call" | custom-call | flops 49999998976 | bytes 16777216 | tf_op jit(solution)/shard_map/pallas_call | solution.py:592
  249.3 6.5 fusion.206
  255.8 8.4 %multiply_convert_fusion.11 = (bf16[512,1728]{0,1:T(8,128)(2,1)S(1)}, f32[512,1728]{0,1:T(8,128)}) fusion(f32[512,1728]{0,1:T(8,128)} %fusion.206, bf16[512,1152]{1,0:T(8,128)(2,1)S(1)} %multiply_convert_fusion.12, bf16[1152,1728]{1,0:T(8,128)(2,1)} %all-gather.8.cloned.1.call-done), kind=kOutput, calls=%fused_computation.100 | convolution fusion | flops 2047279104 | bytes 14008320 | tf_op jit(solution)/shard_map/dot_general | solution.py:225
  264.1 8.2 %collective-permute-done.11 = bf16[512,1152]{1,0:T(8,128)(2,1)S(1)} collective-permute-done((bf16[512,1152]{1,0:T(8,128)(2,1)S(1)}, bf16[512,1152]{1,0:T(8,128)(2,1)S(1)}, u32[]{:S(2)}, u32[]{:S(2)}) %collective-permute-start.11) | collective-permute-done | bytes 1179680 | tf_op jit(solution)/shard_map/ppermute | solution.py:36
  278.3 5.4 multiply_convert_fusion.10
  293.5 7.1 multiply_convert_fusion.9
  300.7 5.2 fusion.211
  309.6 5.2 multiply_convert_fusion.8
  325.5 7.3 collective-permute-done.19
  339.4 7.0 collective-permute-done.20
  366.4 10.6 %collective-permute-done.21 = bf16[512,1152]{1,0:T(8,128)(2,1)} collective-permute-done((bf16[512,1152]{1,0:T(8,128)(2,1)S(1)}, bf16[512,1152]{1,0:T(8,128)(2,1)}, u32[]{:S(2)}, u32[]{:S(2)}) %collective-permute-start.21) | collective-permute-done | bytes 1179680 | tf_op jit(solution)/shard_map/ppermute | solution.py:36
  384.4 6.6 multiply_convert_fusion.4
  391.1 4.9 multiply_convert_fusion.2
  406.6 7.3 multiply_convert_fusion
  416.4 6.3 fusion.216
  422.7 5.7 convolution_add_fusion.1
  432.3 12.1 %convolution_convert_fusion.2 = bf16[1728,1152]{1,0:T(8,128)(2,1)S(1)} fusion(bf16[2048,1728]{0,1:T(8,128)(2,1)S(1)} %bitcast.312, bf16[2048,1152]{1,0:T(8,128)(2,1)} %constant_dynamic-update-slice_fusion.13), kind=kOutput, calls=%fused_computation.2 | convolution fusion | flops 8155717632 | bytes 15777792 | tf_op jit(solution)/shard_map/ji,jk->ik/dot_general | solution.py:233
  452.5 13.2 %convolution_convert_fusion.1 = bf16[1152,1728]{0,1:T(8,128)(2,1)} fusion(bf16[2048,1728]{0,1:T(8,128)(2,1)S(1)} %pad_maximum_fusion, bf16[2048,1152]{1,0:T(8,128)(2,1)} %copy-done.76), kind=kOutput, calls=%fused_computation.1 | convolution fusion | flops 8155717632 | bytes 15777792 | tf_op jit(solution)/shard_map/ji,jk->ik/dot_general | solution.py:233
  465.7 10.8 %convolution_convert_fusion = bf16[1152,1728]{0,1:T(8,128)(2,1)} fusion(bf16[2048,1728]{0,1:T(8,128)(2,1)S(1)} %pad_maximum_fusion.1, bf16[2048,1152]{1,0:T(8,128)(2,1)S(1)} %bitcast.343), kind=kOutput, calls=%fused_computation | convolution fusion | flops 8155717632 | bytes 15777792 | tf_op jit(solution)/shard_map/ji,jk->ik/dot_general | solution.py:233
  476.5 6.5 copy.151
  483.0 6.4 copy.152
  517.9 82.9 %shard_map.317 = (f32[512,1024]{1,0:T(8,128)}, f32[512,512]{1,0:T(8,128)}) custom-call(bf16[512,1024]{1,0:T(8,128)(2,1)} %get-tuple-element.89.q_ref, bf16[512,1024]{1,0:T(8,128)(2,1)} %convolution_convert_fusion.7.grad_ref, f32[1,2048]{1,0:T(1,128)} %get-tuple-element.93.log_ref, f32[1,2048]{1,0:T(1,128)} %bitcast.386, ...), custom_call_target="tpu_custom_call" | custom-call | flops 49999998976 | bytes 16777216 | tf_op jit(solution)/shard_map/pallas_call | solution.py:619
  658.6 7.7 fusion.120
  672.4 8.9 %fusion.95 = (f32[512]{0:T(512)S(1)}, f32[512,1152]{1,0:T(8,128)}) fusion(bf16[512,1152]{1,0:T(8,128)(2,1)} %get-tuple-element.263, f32[1152]{0:T(1024)S(1)} %mul.1200, f32[512,1152]{1,0:T(8,128)} %fusion.120, bf16[512,768]{1,0:T(8,128)(2,1)} %get-tuple-element.102, s32[1152]{0:T(1024)} %constant.342.clone, bf16[1152,768]{1,0:T(8,128)(2,1)} %bitcast.314, ...), kind=kOutput, calls=%fused_computation.152 | convolution fusion | flops 2950446592 | bytes 10234881 | tf_op jit(solution)/shard_map/ij,kj->ik/dot_general | solution.py:229
  685.4 12.3 %collective-permute-start.39 = (bf16[128,768]{1,0:T(8,128)(2,1)S(1)}, bf16[128,768]{1,0:T(8,128)(2,1)S(1)}, u32[]{:S(2)}, u32[]{:S(2)}) collective-permute-start(bf16[128,768]{1,0:T(8,128)(2,1)S(1)} %get-tuple-element.184), channel_id=1, source_target_pairs={{0,6},{2,0},{4,2},{6,4},{1,7},{3,1},{5,3},{7,5},{8,14},{10,8},{12,... | collective-permute-start | bytes 589832 | tf_op jit(solution)/shard_map/ppermute | solution.py:43
  702.6 7.2 collective-permute-done.39
  709.8 28.7 %collective-permute-done.40 = bf16[128,768]{1,0:T(8,128)(2,1)S(1)} collective-permute-done((bf16[128,768]{1,0:T(8,128)(2,1)S(1)}, bf16[128,768]{1,0:T(8,128)(2,1)S(1)}, u32[]{:S(2)}, u32[]{:S(2)}) %collective-permute-start.40) | collective-permute-done | bytes 196640 | tf_op jit(solution)/shard_map/ppermute | solution.py:43
  748.3 6.9 collective-permute-done.47
  (688 shorter events, 324.3 us)
Async XLA Ops:
  7.3 134.6 %all-gather.4.cloned.1.call-start = ((), (), s32[]{:S(2)}) async-start(), calls=%async_computation.2 | async-start | bytes 4478976 | tf_op jit(solution)/shard_map/all_gather | solution.py:55
  31.8 19.5 %collective-permute-start.5 = (bf16[512,768]{1,0:T(8,128)(2,1)S(1)}, bf16[512,768]{1,0:T(8,128)(2,1)S(1)}, u32[]{:S(2)}, u32[]{:S(2)}) collective-permute-start(bf16[512,768]{1,0:T(8,128)(2,1)S(1)} %constant_dynamic-update-slice_fusion.21), channel_id=1, source_target_pairs={{0,16},{16,0},{1,17},{17,1},{2,18},{18,2},{3,19},{19,3},{4,20},{20... | collective-permute-start | bytes 2359304 | tf_op jit(solution)/shard_map/ppermute | solution.py:36
  33.4 19.6 %collective-permute-start.4 = (bf16[512,768]{1,0:T(8,128)(2,1)S(1)}, bf16[512,768]{1,0:T(8,128)(2,1)S(1)}, u32[]{:S(2)}, u32[]{:S(2)}) collective-permute-start(bf16[512,768]{1,0:T(8,128)(2,1)S(1)} %constant_dynamic-update-slice_fusion.21), channel_id=1, source_target_pairs={{0,1},{1,0},{2,3},{3,2},{4,5},{5,4},{6,7},{7,6},{8,9},{9,8},{10,11... | collective-permute-start | bytes 2359304 | tf_op jit(solution)/shard_map/ppermute | solution.py:36
  63.9 31.6 %collective-permute-start.8 = (bf16[2048,768]{1,0:T(8,128)(2,1)}, bf16[2048,768]{1,0:T(8,128)(2,1)}, u32[]{:S(2)}, u32[]{:S(2)}) collective-permute-start(bf16[2048,768]{1,0:T(8,128)(2,1)} %maximum_dynamic-update-slice_fusion), channel_id=1, source_target_pairs={{0,8},{8,0},{1,9},{9,1},{2,10},{10,2},{3,11},{11,3},{4,12},{12,4},... | collective-permute-start | bytes 9437192 | tf_op jit(solution)/shard_map/ppermute | solution.py:46
  66.0 183.3 %all-gather.6.cloned.1.call-start = ((), (), s32[]{:S(2)}) async-start(), calls=%async_computation.3 | async-start | bytes 4644864 | tf_op jit(solution)/shard_map/all_gather | solution.py:55
  91.6 22.8 %collective-permute-start.10 = (bf16[2,1,2,36,1728]{4,2,3,1,0:T(2,128)(2,1)}, bf16[2,1,2,36,1728]{4,2,3,1,0:T(2,128)(2,1)}, u32[]{:S(2)}, u32[]{:S(2)}) collective-permute-start(bf16[2,1,2,36,1728]{4,2,3,1,0:T(2,128)(2,1)} %get-tuple-element.200), channel_id=1, source_target_pairs={{0,1},{1,0},{2,3},{3,2},{4,5},{5,4},{6,7},{7,6},{8,9},{9,8},{10,11... | collective-permute-start | bytes 1493000 | tf_op jit(solution)/shard_map/ppermute | solution.py:36
  125.0 130.7 %all-gather.8.cloned.1.call-start = ((), (), s32[]{:S(2)}) async-start(), calls=%async_computation.4 | async-start | bytes 4644864 | tf_op jit(solution)/shard_map/all_gather | solution.py:55
  141.8 477.5 %reduce-scatter.7.cloned.1.call-start = ((), (), s32[]{:S(2)}) async-start(), calls=%async_computation.6 | async-start | bytes 2488320
  244.9 27.5 %collective-permute-start.11 = (bf16[512,1152]{1,0:T(8,128)(2,1)S(1)}, bf16[512,1152]{1,0:T(8,128)(2,1)S(1)}, u32[]{:S(2)}, u32[]{:S(2)}) collective-permute-start(bf16[512,1152]{1,0:T(8,128)(2,1)S(1)} %multiply_convert_fusion.12), channel_id=1, source_target_pairs={{0,1},{1,0},{2,3},{3,2},{4,5},{5,4},{6,7},{7,6},{8,9},{9,8},{10,11... | collective-permute-start | bytes 3538952 | tf_op jit(solution)/shard_map/ppermute | solution.py:36
  245.4 27.4 %collective-permute-start.13 = (bf16[512,1152]{1,0:T(8,128)(2,1)S(1)}, bf16[512,1152]{1,0:T(8,128)(2,1)S(1)}, u32[]{:S(2)}, u32[]{:S(2)}) collective-permute-start(bf16[512,1152]{1,0:T(8,128)(2,1)S(1)} %multiply_convert_fusion.12), channel_id=1, source_target_pairs={{0,16},{16,0},{1,17},{17,1},{2,18},{18,2},{3,19},{19,3},{4,20},{20... | collective-permute-start | bytes 3538952 | tf_op jit(solution)/shard_map/ppermute | solution.py:36
  272.8 33.9 %collective-permute-start.14 = (bf16[256,1152]{1,0:T(8,128)(2,1)S(1)}, bf16[256,1152]{1,0:T(8,128)(2,1)S(1)}, u32[]{:S(2)}, u32[]{:S(2)}) collective-permute-start(bf16[256,1152]{1,0:T(8,128)(2,1)S(1)} %slice.373), channel_id=1, source_target_pairs={{0,1},{1,0},{2,3},{3,2},{4,5},{5,4},{6,7},{7,6},{8,9},{9,8},{10,11... | collective-permute-start | bytes 1769480 | tf_op jit(solution)/shard_map/ppermute | solution.py:36
  274.2 32.6 %collective-permute-start.15 = (bf16[256,1152]{1,0:T(8,128)(2,1)S(1)}, bf16[256,1152]{1,0:T(8,128)(2,1)S(1)}, u32[]{:S(2)}, u32[]{:S(2)}) collective-permute-start(bf16[256,1152]{1,0:T(8,128)(2,1)S(1)} %slice.374), channel_id=1, source_target_pairs={{0,16},{16,0},{1,17},{17,1},{2,18},{18,2},{3,19},{19,3},{4,20},{20... | collective-permute-start | bytes 1769480 | tf_op jit(solution)/shard_map/ppermute | solution.py:36
  288.5 50.9 %collective-permute-start.12 = (bf16[256,1152]{1,0:T(8,128)(2,1)S(1)}, bf16[256,1152]{1,0:T(8,128)(2,1)S(1)}, u32[]{:S(2)}, u32[]{:S(2)}) collective-permute-start(bf16[256,1152]{1,0:T(8,128)(2,1)S(1)} %slice.605), channel_id=1, source_target_pairs={{0,1},{1,0},{2,3},{3,2},{4,5},{5,4},{6,7},{7,6},{8,9},{9,8},{10,11... | collective-permute-start | bytes 1769480 | tf_op jit(solution)/shard_map/ppermute | solution.py:36
  305.9 33.5 %collective-permute-start.18 = (bf16[256,1152]{1,0:T(8,128)(2,1)S(1)}, bf16[256,1152]{1,0:T(8,128)(2,1)S(1)}, u32[]{:S(2)}, u32[]{:S(2)}) collective-permute-start(bf16[256,1152]{1,0:T(8,128)(2,1)S(1)} %slice.604), channel_id=1, source_target_pairs={{0,16},{16,0},{1,17},{17,1},{2,18},{18,2},{3,19},{19,3},{4,20},{20... | collective-permute-start | bytes 1769480 | tf_op jit(solution)/shard_map/ppermute | solution.py:36
  352.0 25.0 %collective-permute-start.21 = (bf16[512,1152]{1,0:T(8,128)(2,1)S(1)}, bf16[512,1152]{1,0:T(8,128)(2,1)}, u32[]{:S(2)}, u32[]{:S(2)}) collective-permute-start(bf16[512,1152]{1,0:T(8,128)(2,1)S(1)} %fusion.86), channel_id=1, source_target_pairs={{0,1},{1,0},{2,3},{3,2},{4,5},{5,4},{6,7},{7,6},{8,9},{9,8},{10,11... | collective-permute-start | bytes 3538952 | tf_op jit(solution)/shard_map/ppermute | solution.py:36
  352.9 25.8 %collective-permute-start.23 = (bf16[512,1152]{1,0:T(8,128)(2,1)S(1)}, bf16[512,1152]{1,0:T(8,128)(2,1)S(1)}, u32[]{:S(2)}, u32[]{:S(2)}) collective-permute-start(bf16[512,1152]{1,0:T(8,128)(2,1)S(1)} %fusion.86), channel_id=1, source_target_pairs={{0,16},{16,0},{1,17},{17,1},{2,18},{18,2},{3,19},{19,3},{4,20},{20... | collective-permute-start | bytes 3538952 | tf_op jit(solution)/shard_map/ppermute | solution.py:36
  378.2 28.3 %collective-permute-start.25 = (bf16[256,1152]{1,0:T(8,128)(2,1)S(1)}, bf16[256,1152]{1,0:T(8,128)(2,1)S(1)}, u32[]{:S(2)}, u32[]{:S(2)}) collective-permute-start(bf16[256,1152]{1,0:T(8,128)(2,1)S(1)} %slice.385), channel_id=1, source_target_pairs={{0,16},{16,0},{1,17},{17,1},{2,18},{18,2},{3,19},{19,3},{4,20},{20... | collective-permute-start | bytes 1769480 | tf_op jit(solution)/shard_map/ppermute | solution.py:36
  378.8 27.7 %collective-permute-start.24 = (bf16[256,1152]{1,0:T(8,128)(2,1)S(1)}, bf16[256,1152]{1,0:T(8,128)(2,1)S(1)}, u32[]{:S(2)}, u32[]{:S(2)}) collective-permute-start(bf16[256,1152]{1,0:T(8,128)(2,1)S(1)} %slice.384), channel_id=1, source_target_pairs={{0,1},{1,0},{2,3},{3,2},{4,5},{5,4},{6,7},{7,6},{8,9},{9,8},{10,11... | collective-permute-start | bytes 1769480 | tf_op jit(solution)/shard_map/ppermute | solution.py:36
  446.0 66.3 %collective-permute-start.31 = (bf16[864,1152]{1,0:T(8,128)(2,1)}, bf16[864,1152]{1,0:T(8,128)(2,1)}, u32[]{:S(2)}, u32[]{:S(2)}) collective-permute-start(bf16[864,1152]{1,0:T(8,128)(2,1)} %dynamic-slice_bitcast_fusion.2), channel_id=1, source_target_pairs={{0,8},{8,0},{1,9},{9,1},{2,10},{10,2},{3,11},{11,3},{4,12},{12,4},... | collective-permute-start | bytes 5971976 | tf_op jit(solution)/shard_map/ppermute | solution.py:46
  447.3 46.7 %collective-permute-start.30 = (bf16[256,1152]{1,0:T(8,128)(2,1)}, bf16[256,1152]{1,0:T(8,128)(2,1)S(1)}, u32[]{:S(2)}, u32[]{:S(2)}) collective-permute-start(bf16[256,1152]{1,0:T(8,128)(2,1)} %get-tuple-element.167), channel_id=1, source_target_pairs={{0,1},{1,0},{2,3},{3,2},{4,5},{5,4},{6,7},{7,6},{8,9},{9,8},{10,11... | collective-permute-start | bytes 1769480 | tf_op jit(solution)/shard_map/ppermute | solution.py:36
  449.3 45.2 %collective-permute-start.27 = (bf16[256,1152]{1,0:T(8,128)(2,1)}, bf16[256,1152]{1,0:T(8,128)(2,1)S(1)}, u32[]{:S(2)}, u32[]{:S(2)}) collective-permute-start(bf16[256,1152]{1,0:T(8,128)(2,1)} %get-tuple-element.168), channel_id=1, source_target_pairs={{0,16},{16,0},{1,17},{17,1},{2,18},{18,2},{3,19},{19,3},{4,20},{20... | collective-permute-start | bytes 1769480 | tf_op jit(solution)/shard_map/ppermute | solution.py:36
  450.6 43.4 %collective-permute-start.22 = (bf16[256,1152]{1,0:T(8,128)(2,1)}, bf16[256,1152]{1,0:T(8,128)(2,1)S(1)}, u32[]{:S(2)}, u32[]{:S(2)}) collective-permute-start(bf16[256,1152]{1,0:T(8,128)(2,1)} %get-tuple-element.166), channel_id=1, source_target_pairs={{0,1},{1,0},{2,3},{3,2},{4,5},{5,4},{6,7},{7,6},{8,9},{9,8},{10,11... | collective-permute-start | bytes 1769480 | tf_op jit(solution)/shard_map/ppermute | solution.py:36
  451.1 43.5 %collective-permute-start.28 = (bf16[256,1152]{1,0:T(8,128)(2,1)}, bf16[256,1152]{1,0:T(8,128)(2,1)S(1)}, u32[]{:S(2)}, u32[]{:S(2)}) collective-permute-start(bf16[256,1152]{1,0:T(8,128)(2,1)} %get-tuple-element.169), channel_id=1, source_target_pairs={{0,16},{16,0},{1,17},{17,1},{2,18},{18,2},{3,19},{19,3},{4,20},{20... | collective-permute-start | bytes 1769480 | tf_op jit(solution)/shard_map/ppermute | solution.py:36
  494.0 137.0 %collective-permute-start.43 = (bf16[576,1728]{1,0:T(8,128)(2,1)}, bf16[576,1728]{1,0:T(8,128)(2,1)}, u32[]{:S(2)}, u32[]{:S(2)}) collective-permute-start(bf16[576,1728]{1,0:T(8,128)(2,1)} %dynamic-slice_bitcast_fusion.1), channel_id=1, source_target_pairs={{0,8},{8,0},{1,9},{9,1},{2,10},{10,2},{3,11},{11,3},{4,12},{12,4},... | collective-permute-start | bytes 5971976 | tf_op jit(solution)/shard_map/ppermute | solution.py:46
  494.0 140.7 %collective-permute-start.44 = (bf16[576,1728]{1,0:T(8,128)(2,1)}, bf16[576,1728]{1,0:T(8,128)(2,1)}, u32[]{:S(2)}, u32[]{:S(2)}) collective-permute-start(bf16[576,1728]{1,0:T(8,128)(2,1)} %dynamic-slice_bitcast_fusion), channel_id=1, source_target_pairs={{0,8},{8,0},{1,9},{9,1},{2,10},{10,2},{3,11},{11,3},{4,12},{12,4},... | collective-permute-start | bytes 5971976 | tf_op jit(solution)/shard_map/ppermute | solution.py:46
  515.6 228.4 %reduce-scatter.5.cloned.1.call-start = ((), (), s32[]{:S(2)}) async-start(), calls=%async_computation.5 | async-start | bytes 5160960 | tf_op jit(solution)/shard_map/reduce_scatter | solution.py:64
  631.0 19.6 %collective-permute-start.32 = (bf16[2048,768]{1,0:T(8,128)(2,1)}, bf16[2048,768]{1,0:T(8,128)(2,1)}, u32[]{:S(2)}, u32[]{:S(2)}) collective-permute-start(bf16[2048,768]{1,0:T(8,128)(2,1)} %bitcast.69), channel_id=1, source_target_pairs={{0,8},{8,0},{1,9},{9,1},{2,10},{10,2},{3,11},{11,3},{4,12},{12,4},... | collective-permute-start | bytes 9437192 | tf_op jit(solution)/shard_map/ppermute | solution.py:46
  657.2 24.3 %collective-permute-start.33 = (bf16[256,768]{1,0:T(8,128)(2,1)}, bf16[256,768]{1,0:T(8,128)(2,1)S(1)}, u32[]{:S(2)}, u32[]{:S(2)}) collective-permute-start(bf16[256,768]{1,0:T(8,128)(2,1)} %get-tuple-element.154), channel_id=1, source_target_pairs={{0,1},{1,0},{2,3},{3,2},{4,5},{5,4},{6,7},{7,6},{8,9},{9,8},{10,11... | collective-permute-start | bytes 1179656 | tf_op jit(solution)/shard_map/ppermute | solution.py:36
  657.9 23.6 %collective-permute-start.36 = (bf16[256,768]{1,0:T(8,128)(2,1)}, bf16[256,768]{1,0:T(8,128)(2,1)}, u32[]{:S(2)}, u32[]{:S(2)}) collective-permute-start(bf16[256,768]{1,0:T(8,128)(2,1)} %get-tuple-element.157), channel_id=1, source_target_pairs={{0,16},{16,0},{1,17},{17,1},{2,18},{18,2},{3,19},{19,3},{4,20},{20... | collective-permute-start | bytes 1179656 | tf_op jit(solution)/shard_map/ppermute | solution.py:36
  685.4 24.3 %collective-permute-start.39 = (bf16[128,768]{1,0:T(8,128)(2,1)S(1)}, bf16[128,768]{1,0:T(8,128)(2,1)S(1)}, u32[]{:S(2)}, u32[]{:S(2)}) collective-permute-start(bf16[128,768]{1,0:T(8,128)(2,1)S(1)} %get-tuple-element.184), channel_id=1, source_target_pairs={{0,6},{2,0},{4,2},{6,4},{1,7},{3,1},{5,3},{7,5},{8,14},{10,8},{12,... | collective-permute-start | bytes 589832 | tf_op jit(solution)/shard_map/ppermute | solution.py:43
  697.7 40.8 %collective-permute-start.40 = (bf16[128,768]{1,0:T(8,128)(2,1)S(1)}, bf16[128,768]{1,0:T(8,128)(2,1)S(1)}, u32[]{:S(2)}, u32[]{:S(2)}) collective-permute-start(bf16[128,768]{1,0:T(8,128)(2,1)S(1)} %get-tuple-element.186), channel_id=1, source_target_pairs={{0,4},{2,6},{4,0},{6,2},{1,5},{3,7},{5,1},{7,3},{8,12},{10,14},{12... | collective-permute-start | bytes 589832 | tf_op jit(solution)/shard_map/ppermute | solution.py:43
  699.0 39.6 %collective-permute-start.41 = (bf16[128,768]{1,0:T(8,128)(2,1)S(1)}, bf16[128,768]{1,0:T(8,128)(2,1)S(1)}, u32[]{:S(2)}, u32[]{:S(2)}) collective-permute-start(bf16[128,768]{1,0:T(8,128)(2,1)S(1)} %get-tuple-element.185), channel_id=1, source_target_pairs={{0,2},{2,4},{4,6},{6,0},{1,3},{3,5},{5,7},{7,1},{8,10},{10,12},{12... | collective-permute-start | bytes 589832 | tf_op jit(solution)/shard_map/ppermute | solution.py:43
  (180 other events, 1432.9 us)
Sparse Core Ops, SparseCore 0:
  66.1 47.0 all-gather.3
  125.1 81.6 all-gather.5
  208.4 44.7 all-gather.7
  515.7 63.6 reduce-scatter.6
  639.6 97.9 reduce-scatter.4

commit v5 on v4

--- a/solution.py
+++ b/solution.py
@@ -959,6 +959,7 @@
     gate_terms = place.cores_summed(gate_terms)
     up_terms = place.cores_summed(up_terms)
     down_rows = place.scatter_line(down_terms)
+    gate_rows = place.scatter_line(gate_terms)
 
     mixed_part, feed_term = norm_back(normed_two_grad, mixed, factor_two, feed_scale)
     mixed_grad = out_grad + mixed_part
@@ -987,13 +988,7 @@
         )
         key_value_grad = place.scatter_group(key_value_terms)
     output_terms = after(output_terms, key_value_grad)
-    share = gate_terms.shape[0] // (nw * nz)
-    gate_up_terms = jnp.stack(
-        [t.reshape(nw * nz, share, part) for t in (gate_terms, up_terms)], axis=1
-    )
-    gate_up_rows = place.scatter_line(after(gate_up_terms.reshape(-1, part), key_value_grad))
-    key_value_grad = after(key_value_grad, down_rows)
-    gate_rows, up_rows = gate_up_rows[:share], gate_up_rows[share:]
+    up_rows = place.scatter_line(up_terms)
     down_weight_grad = matmul(down_rows, to_outside)
 
     def whole_rows(own_part):

time: 789 us -> 775 us (0.982)
  waiting for transfers between devices: 130 us -> 109 us
    ppermute x6, waiting for transfers between devices: 48 us -> 31.2 us  [shift_wz(): return lax.ppermute(value, ('w', 'z'), pairs)]
    unnamed x339 -> x345, local copies, waits for them, and re-layouts: 19.5 us -> 23.4 us
  transfers between devices with their start and end apart: 54 -> 55, of which waited for: 21 -> 20; matrix products, arithmetic and copies ran while one was open for 44% -> 45% of each run, Pallas kernels for 23% -> 23%
where the time goes in v5:
time: 775 us; the launch traced here: 767 us
  matrix products  203 us (26%)
  Pallas kernels  176 us (23%)
  local copies, waits for them, and re-layouts  115 us (15%)
  waiting for transfers between devices  109 us (14%)
  other arithmetic  81.9 us (11%)
  starting transfers between devices  64 us (8%)
  between operations  17.4 us (2%)
    pallas_call x1, Pallas kernels, gather_attend(): pl.pallas_call(functools.partial(gather_attend_kernel, sizes), out_shape=...  93.2 us
    dot_general x23, matrix products, matmul(): return jnp.dot(left, right, preferred_element_type=F32)  87.5 us
    pallas_call x1, Pallas kernels, attend_back(): pl.pallas_call(functools.partial(attend_back_kernel, sizes), out_shape=(j...  82.8 us
    ppermute x36, waiting for transfers between devices, shift(): return lax.ppermute(value, axis, [(i, (i + by) % n) for i in range(n)])  77.9 us
    dot_general x15, matrix products, matmul_nt(): return jnp.einsum('ij,kj->ik', left, right, preferred_element_type=F32)  71.7 us
    ppermute x36, starting transfers between devices, shift(): return lax.ppermute(value, axis, [(i, (i + by) % n) for i in range(n)])  42.8 us
    dot_general x6, matrix products, matmul_tn(): return jnp.einsum('ji,jk->ik', left, right, preferred_element_type=F32)  41.4 us
    ppermute x6, waiting for transfers between devices, shift_wz(): return lax.ppermute(value, ('w', 'z'), pairs)  31.2 us
  transfers between devices with their start and end apart: 55, of which 20 were waited for; matrix products, arithmetic and copies ran while one was open for 45% of the time, Pallas kernels for 23%

profile of v5, /device:TPU:0, one launch (start us, length us, event | category | flops | bytes accessed | tf_op | source)
XLA Modules:
  0.0 767.0 jit_solution(15549299821999719326)
XLA Ops:
  23.6 8.2 %collective-permute-done.2 = bf16[128,768]{1,0:T(8,128)(2,1)S(1)} collective-permute-done((bf16[128,768]{1,0:T(8,128)(2,1)S(1)}, bf16[128,768]{1,0:T(8,128)(2,1)S(1)}, u32[]{:S(2)}, u32[]{:S(2)}) %collective-permute-start.2) | collective-permute-done | bytes 196640 | tf_op jit(solution)/shard_map/ppermute | solution.py:43
  34.9 16.4 %collective-permute-done.5 = bf16[512,768]{1,0:T(8,128)(2,1)S(1)} collective-permute-done((bf16[512,768]{1,0:T(8,128)(2,1)S(1)}, bf16[512,768]{1,0:T(8,128)(2,1)S(1)}, u32[]{:S(2)}, u32[]{:S(2)}) %collective-permute-start.5) | collective-permute-done | bytes 786464 | tf_op jit(solution)/shard_map/ppermute | solution.py:36
  79.9 9.1 %collective-permute-done.9 = bf16[1,2,2,36,1728]{4,2,3,1,0:T(2,128)(2,1)S(1)} collective-permute-done((bf16[1,2,2,36,1728]{4,2,3,1,0:T(2,128)(2,1)S(1)}, bf16[1,2,2,36,1728]{4,2,3,1,0:T(2,128)(2,1)S(1)}, u32[]{:S(2)}, u32[]{:S(2)}) %collective-permute-start.9) | collective-permute-done | bytes 497696 | tf_op jit(solution)/shard_map/ppermute | solution.py:36
  115.5 7.3 fusion.118
  141.7 93.2 %shard_map.316 = (bf16[4096,512]{1,0:T(8,128)(2,1)}, bf16[512,1024]{1,0:T(8,128)(2,1)}, bf16[512,1024]{1,0:T(8,128)(2,1)}, f32[1,2048]{1,0:T(1,128)}) custom-call(bf16[512,512]{1,0:T(8,128)(2,1)} %pad_maximum_fusion.15.own_ref, f32[512,1024]{1,0:T(8,128)} %pad_maximum_fusion.8.raw_ref, f32[1,256]{1,0:T(1,128)} %reshape_reshape.3.gain_ref, ...), custom_call_target="tpu_custom_call" | custom-call | flops 49999998976 | bytes 16777216 | tf_op jit(solution)/shard_map/pallas_call | solution.py:592
  249.2 6.5 fusion.205
  255.7 8.3 %multiply_convert_fusion.11 = (bf16[512,1728]{0,1:T(8,128)(2,1)S(1)}, f32[512,1728]{0,1:T(8,128)}) fusion(f32[512,1728]{0,1:T(8,128)} %fusion.205, bf16[512,1152]{1,0:T(8,128)(2,1)S(1)} %multiply_convert_fusion.12, bf16[1152,1728]{1,0:T(8,128)(2,1)} %all-gather.8.cloned.1.call-done), kind=kOutput, calls=%fused_computation.99 | convolution fusion | flops 2047279104 | bytes 14008320 | tf_op jit(solution)/shard_map/dot_general | solution.py:225
  264.0 8.3 %collective-permute-done.11 = bf16[512,1152]{1,0:T(8,128)(2,1)S(1)} collective-permute-done((bf16[512,1152]{1,0:T(8,128)(2,1)S(1)}, bf16[512,1152]{1,0:T(8,128)(2,1)S(1)}, u32[]{:S(2)}, u32[]{:S(2)}) %collective-permute-start.11) | collective-permute-done | bytes 1179680 | tf_op jit(solution)/shard_map/ppermute | solution.py:36
  278.2 5.6 multiply_convert_fusion.10
  293.6 7.2 multiply_convert_fusion.9
  300.8 5.2 fusion.210
  309.7 5.3 multiply_convert_fusion.8
  325.7 7.3 collective-permute-done.19
  339.3 7.3 collective-permute-done.20
  366.6 10.8 %collective-permute-done.21 = bf16[512,1152]{1,0:T(8,128)(2,1)} collective-permute-done((bf16[512,1152]{1,0:T(8,128)(2,1)S(1)}, bf16[512,1152]{1,0:T(8,128)(2,1)}, u32[]{:S(2)}, u32[]{:S(2)}) %collective-permute-start.21) | collective-permute-done | bytes 1179680 | tf_op jit(solution)/shard_map/ppermute | solution.py:36
  384.6 6.6 multiply_convert_fusion.4
  406.7 7.3 multiply_convert_fusion
  416.5 6.3 fusion.215
  422.9 5.7 convolution_add_fusion.1
  432.4 12.1 %convolution_convert_fusion.2 = bf16[1728,1152]{1,0:T(8,128)(2,1)S(1)} fusion(bf16[2048,1728]{0,1:T(8,128)(2,1)S(1)} %bitcast.306, bf16[2048,1152]{1,0:T(8,128)(2,1)} %constant_dynamic-update-slice_fusion.13), kind=kOutput, calls=%fused_computation.2 | convolution fusion | flops 8155717632 | bytes 15777792 | tf_op jit(solution)/shard_map/ji,jk->ik/dot_general | solution.py:233
  452.7 13.2 %convolution_convert_fusion = bf16[1152,1728]{0,1:T(8,128)(2,1)} fusion(bf16[2048,1728]{0,1:T(8,128)(2,1)S(1)} %pad_maximum_fusion.1, bf16[2048,1152]{1,0:T(8,128)(2,1)} %copy-done.82), kind=kOutput, calls=%fused_computation | convolution fusion | flops 8155717632 | bytes 15777792 | tf_op jit(solution)/shard_map/ji,jk->ik/dot_general | solution.py:233
  465.9 10.7 %convolution_convert_fusion.1 = bf16[1152,1728]{0,1:T(8,128)(2,1)} fusion(bf16[2048,1728]{0,1:T(8,128)(2,1)S(1)} %pad_maximum_fusion, bf16[2048,1152]{1,0:T(8,128)(2,1)S(1)} %bitcast.337), kind=kOutput, calls=%fused_computation.1 | convolution fusion | flops 8155717632 | bytes 15777792 | tf_op jit(solution)/shard_map/ji,jk->ik/dot_general | solution.py:233
  476.6 6.4 copy.151
  509.0 82.8 %shard_map.317 = (f32[512,1024]{1,0:T(8,128)}, f32[512,512]{1,0:T(8,128)}) custom-call(bf16[512,1024]{1,0:T(8,128)(2,1)} %get-tuple-element.87.q_ref, bf16[512,1024]{1,0:T(8,128)(2,1)} %convolution_convert_fusion.7.grad_ref, f32[1,2048]{1,0:T(1,128)} %get-tuple-element.91.log_ref, f32[1,2048]{1,0:T(1,128)} %bitcast.380, ...), custom_call_target="tpu_custom_call" | custom-call | flops 49999998976 | bytes 16777216 | tf_op jit(solution)/shard_map/pallas_call | solution.py:619
  626.8 6.6 copy.148
  659.7 7.2 fusion.120
  666.8 9.2 %fusion.95 = (f32[512]{0:T(512)S(1)}, f32[512,1152]{1,0:T(8,128)}) fusion(bf16[512,1152]{1,0:T(8,128)(2,1)} %get-tuple-element.257, f32[1152]{0:T(1024)S(1)} %mul.1200, f32[512,1152]{1,0:T(8,128)} %fusion.120, bf16[512,768]{1,0:T(8,128)(2,1)} %get-tuple-element.99, s32[1152]{0:T(1024)} %constant.342.clone, bf16[1152,768]{1,0:T(8,128)(2,1)} %bitcast.307, ...), kind=kOutput, calls=%fused_computation.151 | convolution fusion | flops 2950446592 | bytes 10234881 | tf_op jit(solution)/shard_map/ij,kj->ik/dot_general | solution.py:229
  680.7 4.9 fusion.69
  688.9 12.6 %collective-permute-start.39 = (bf16[128,768]{1,0:T(8,128)(2,1)S(1)}, bf16[128,768]{1,0:T(8,128)(2,1)S(1)}, u32[]{:S(2)}, u32[]{:S(2)}) collective-permute-start(bf16[128,768]{1,0:T(8,128)(2,1)S(1)} %get-tuple-element.180), channel_id=1, source_target_pairs={{0,6},{2,0},{4,2},{6,4},{1,7},{3,1},{5,3},{7,5},{8,14},{10,8},{12,... | collective-permute-start | bytes 589832 | tf_op jit(solution)/shard_map/ppermute | solution.py:43
  705.4 5.3 collective-permute-done.39
  710.7 13.8 %collective-permute-done.40 = bf16[128,768]{1,0:T(8,128)(2,1)S(1)} collective-permute-done((bf16[128,768]{1,0:T(8,128)(2,1)S(1)}, bf16[128,768]{1,0:T(8,128)(2,1)S(1)}, u32[]{:S(2)}, u32[]{:S(2)}) %collective-permute-start.40) | collective-permute-done | bytes 196640 | tf_op jit(solution)/shard_map/ppermute | solution.py:43
  735.0 5.8 collective-permute-done.47
  (694 shorter events, 326.9 us)
Async XLA Ops:
  7.3 134.5 %all-gather.4.cloned.1.call-start = ((), (), s32[]{:S(2)}) async-start(), calls=%async_computation.3 | async-start | bytes 4478976 | tf_op jit(solution)/shard_map/all_gather | solution.py:55
  33.4 19.6 %collective-permute-start.4 = (bf16[512,768]{1,0:T(8,128)(2,1)S(1)}, bf16[512,768]{1,0:T(8,128)(2,1)S(1)}, u32[]{:S(2)}, u32[]{:S(2)}) collective-permute-start(bf16[512,768]{1,0:T(8,128)(2,1)S(1)} %constant_dynamic-update-slice_fusion.21), channel_id=1, source_target_pairs={{0,1},{1,0},{2,3},{3,2},{4,5},{5,4},{6,7},{7,6},{8,9},{9,8},{10,11... | collective-permute-start | bytes 2359304 | tf_op jit(solution)/shard_map/ppermute | solution.py:36
  63.8 31.6 %collective-permute-start.8 = (bf16[2048,768]{1,0:T(8,128)(2,1)}, bf16[2048,768]{1,0:T(8,128)(2,1)}, u32[]{:S(2)}, u32[]{:S(2)}) collective-permute-start(bf16[2048,768]{1,0:T(8,128)(2,1)} %maximum_dynamic-update-slice_fusion), channel_id=1, source_target_pairs={{0,8},{8,0},{1,9},{9,1},{2,10},{10,2},{3,11},{11,3},{4,12},{12,4},... | collective-permute-start | bytes 9437192 | tf_op jit(solution)/shard_map/ppermute | solution.py:46
  65.9 183.3 %all-gather.6.cloned.1.call-start = ((), (), s32[]{:S(2)}) async-start(), calls=%async_computation.4 | async-start | bytes 4644864 | tf_op jit(solution)/shard_map/all_gather | solution.py:55
  91.5 22.8 %collective-permute-start.10 = (bf16[2,1,2,36,1728]{4,2,3,1,0:T(2,128)(2,1)}, bf16[2,1,2,36,1728]{4,2,3,1,0:T(2,128)(2,1)}, u32[]{:S(2)}, u32[]{:S(2)}) collective-permute-start(bf16[2,1,2,36,1728]{4,2,3,1,0:T(2,128)(2,1)} %get-tuple-element.194), channel_id=1, source_target_pairs={{0,1},{1,0},{2,3},{3,2},{4,5},{5,4},{6,7},{7,6},{8,9},{9,8},{10,11... | collective-permute-start | bytes 1493000 | tf_op jit(solution)/shard_map/ppermute | solution.py:36
  124.9 130.8 %all-gather.8.cloned.1.call-start = ((), (), s32[]{:S(2)}) async-start(), calls=%async_computation.5 | async-start | bytes 4644864 | tf_op jit(solution)/shard_map/all_gather | solution.py:55
  141.7 560.5 %reduce-scatter.10.cloned.1.call-start = ((), (), s32[]{:S(2)}) async-start(), calls=%async_computation.8 | async-start | bytes 2488320
  244.7 27.6 %collective-permute-start.11 = (bf16[512,1152]{1,0:T(8,128)(2,1)S(1)}, bf16[512,1152]{1,0:T(8,128)(2,1)S(1)}, u32[]{:S(2)}, u32[]{:S(2)}) collective-permute-start(bf16[512,1152]{1,0:T(8,128)(2,1)S(1)} %multiply_convert_fusion.12), channel_id=1, source_target_pairs={{0,1},{1,0},{2,3},{3,2},{4,5},{5,4},{6,7},{7,6},{8,9},{9,8},{10,11... | collective-permute-start | bytes 3538952 | tf_op jit(solution)/shard_map/ppermute | solution.py:36
  245.2 27.4 %collective-permute-start.13 = (bf16[512,1152]{1,0:T(8,128)(2,1)S(1)}, bf16[512,1152]{1,0:T(8,128)(2,1)S(1)}, u32[]{:S(2)}, u32[]{:S(2)}) collective-permute-start(bf16[512,1152]{1,0:T(8,128)(2,1)S(1)} %multiply_convert_fusion.12), channel_id=1, source_target_pairs={{0,16},{16,0},{1,17},{17,1},{2,18},{18,2},{3,19},{19,3},{4,20},{20... | collective-permute-start | bytes 3538952 | tf_op jit(solution)/shard_map/ppermute | solution.py:36
  272.7 34.1 %collective-permute-start.14 = (bf16[256,1152]{1,0:T(8,128)(2,1)S(1)}, bf16[256,1152]{1,0:T(8,128)(2,1)S(1)}, u32[]{:S(2)}, u32[]{:S(2)}) collective-permute-start(bf16[256,1152]{1,0:T(8,128)(2,1)S(1)} %slice.367), channel_id=1, source_target_pairs={{0,1},{1,0},{2,3},{3,2},{4,5},{5,4},{6,7},{7,6},{8,9},{9,8},{10,11... | collective-permute-start | bytes 1769480 | tf_op jit(solution)/shard_map/ppermute | solution.py:36
  274.2 32.8 %collective-permute-start.15 = (bf16[256,1152]{1,0:T(8,128)(2,1)S(1)}, bf16[256,1152]{1,0:T(8,128)(2,1)S(1)}, u32[]{:S(2)}, u32[]{:S(2)}) collective-permute-start(bf16[256,1152]{1,0:T(8,128)(2,1)S(1)} %slice.368), channel_id=1, source_target_pairs={{0,16},{16,0},{1,17},{17,1},{2,18},{18,2},{3,19},{19,3},{4,20},{20... | collective-permute-start | bytes 1769480 | tf_op jit(solution)/shard_map/ppermute | solution.py:36
  288.6 50.7 %collective-permute-start.12 = (bf16[256,1152]{1,0:T(8,128)(2,1)S(1)}, bf16[256,1152]{1,0:T(8,128)(2,1)S(1)}, u32[]{:S(2)}, u32[]{:S(2)}) collective-permute-start(bf16[256,1152]{1,0:T(8,128)(2,1)S(1)} %slice.595), channel_id=1, source_target_pairs={{0,1},{1,0},{2,3},{3,2},{4,5},{5,4},{6,7},{7,6},{8,9},{9,8},{10,11... | collective-permute-start | bytes 1769480 | tf_op jit(solution)/shard_map/ppermute | solution.py:36
  306.0 33.3 %collective-permute-start.18 = (bf16[256,1152]{1,0:T(8,128)(2,1)S(1)}, bf16[256,1152]{1,0:T(8,128)(2,1)S(1)}, u32[]{:S(2)}, u32[]{:S(2)}) collective-permute-start(bf16[256,1152]{1,0:T(8,128)(2,1)S(1)} %slice.594), channel_id=1, source_target_pairs={{0,16},{16,0},{1,17},{17,1},{2,18},{18,2},{3,19},{19,3},{4,20},{20... | collective-permute-start | bytes 1769480 | tf_op jit(solution)/shard_map/ppermute | solution.py:36
  352.2 25.1 %collective-permute-start.21 = (bf16[512,1152]{1,0:T(8,128)(2,1)S(1)}, bf16[512,1152]{1,0:T(8,128)(2,1)}, u32[]{:S(2)}, u32[]{:S(2)}) collective-permute-start(bf16[512,1152]{1,0:T(8,128)(2,1)S(1)} %fusion.86), channel_id=1, source_target_pairs={{0,1},{1,0},{2,3},{3,2},{4,5},{5,4},{6,7},{7,6},{8,9},{9,8},{10,11... | collective-permute-start | bytes 3538952 | tf_op jit(solution)/shard_map/ppermute | solution.py:36
  353.2 25.8 %collective-permute-start.23 = (bf16[512,1152]{1,0:T(8,128)(2,1)S(1)}, bf16[512,1152]{1,0:T(8,128)(2,1)S(1)}, u32[]{:S(2)}, u32[]{:S(2)}) collective-permute-start(bf16[512,1152]{1,0:T(8,128)(2,1)S(1)} %fusion.86), channel_id=1, source_target_pairs={{0,16},{16,0},{1,17},{17,1},{2,18},{18,2},{3,19},{19,3},{4,20},{20... | collective-permute-start | bytes 3538952 | tf_op jit(solution)/shard_map/ppermute | solution.py:36
  378.5 28.2 %collective-permute-start.25 = (bf16[256,1152]{1,0:T(8,128)(2,1)S(1)}, bf16[256,1152]{1,0:T(8,128)(2,1)S(1)}, u32[]{:S(2)}, u32[]{:S(2)}) collective-permute-start(bf16[256,1152]{1,0:T(8,128)(2,1)S(1)} %slice.379), channel_id=1, source_target_pairs={{0,16},{16,0},{1,17},{17,1},{2,18},{18,2},{3,19},{19,3},{4,20},{20... | collective-permute-start | bytes 1769480 | tf_op jit(solution)/shard_map/ppermute | solution.py:36
  379.0 27.7 %collective-permute-start.24 = (bf16[256,1152]{1,0:T(8,128)(2,1)S(1)}, bf16[256,1152]{1,0:T(8,128)(2,1)S(1)}, u32[]{:S(2)}, u32[]{:S(2)}) collective-permute-start(bf16[256,1152]{1,0:T(8,128)(2,1)S(1)} %slice.378), channel_id=1, source_target_pairs={{0,1},{1,0},{2,3},{3,2},{4,5},{5,4},{6,7},{7,6},{8,9},{9,8},{10,11... | collective-permute-start | bytes 1769480 | tf_op jit(solution)/shard_map/ppermute | solution.py:36
  446.1 57.4 %collective-permute-start.31 = (bf16[864,1152]{1,0:T(8,128)(2,1)}, bf16[864,1152]{1,0:T(8,128)(2,1)}, u32[]{:S(2)}, u32[]{:S(2)}) collective-permute-start(bf16[864,1152]{1,0:T(8,128)(2,1)} %dynamic-slice_bitcast_fusion.2), channel_id=1, source_target_pairs={{0,8},{8,0},{1,9},{9,1},{2,10},{10,2},{3,11},{11,3},{4,12},{12,4},... | collective-permute-start | bytes 5971976 | tf_op jit(solution)/shard_map/ppermute | solution.py:46
  447.5 38.8 %collective-permute-start.30 = (bf16[256,1152]{1,0:T(8,128)(2,1)}, bf16[256,1152]{1,0:T(8,128)(2,1)S(1)}, u32[]{:S(2)}, u32[]{:S(2)}) collective-permute-start(bf16[256,1152]{1,0:T(8,128)(2,1)} %get-tuple-element.163), channel_id=1, source_target_pairs={{0,1},{1,0},{2,3},{3,2},{4,5},{5,4},{6,7},{7,6},{8,9},{9,8},{10,11... | collective-permute-start | bytes 1769480 | tf_op jit(solution)/shard_map/ppermute | solution.py:36
  449.5 36.8 %collective-permute-start.27 = (bf16[256,1152]{1,0:T(8,128)(2,1)}, bf16[256,1152]{1,0:T(8,128)(2,1)S(1)}, u32[]{:S(2)}, u32[]{:S(2)}) collective-permute-start(bf16[256,1152]{1,0:T(8,128)(2,1)} %get-tuple-element.164), channel_id=1, source_target_pairs={{0,16},{16,0},{1,17},{17,1},{2,18},{18,2},{3,19},{19,3},{4,20},{20... | collective-permute-start | bytes 1769480 | tf_op jit(solution)/shard_map/ppermute | solution.py:36
  450.8 35.5 %collective-permute-start.22 = (bf16[256,1152]{1,0:T(8,128)(2,1)}, bf16[256,1152]{1,0:T(8,128)(2,1)S(1)}, u32[]{:S(2)}, u32[]{:S(2)}) collective-permute-start(bf16[256,1152]{1,0:T(8,128)(2,1)} %get-tuple-element.162), channel_id=1, source_target_pairs={{0,1},{1,0},{2,3},{3,2},{4,5},{5,4},{6,7},{7,6},{8,9},{9,8},{10,11... | collective-permute-start | bytes 1769480 | tf_op jit(solution)/shard_map/ppermute | solution.py:36
  451.3 35.0 %collective-permute-start.28 = (bf16[256,1152]{1,0:T(8,128)(2,1)}, bf16[256,1152]{1,0:T(8,128)(2,1)S(1)}, u32[]{:S(2)}, u32[]{:S(2)}) collective-permute-start(bf16[256,1152]{1,0:T(8,128)(2,1)} %get-tuple-element.165), channel_id=1, source_target_pairs={{0,16},{16,0},{1,17},{17,1},{2,18},{18,2},{3,19},{19,3},{4,20},{20... | collective-permute-start | bytes 1769480 | tf_op jit(solution)/shard_map/ppermute | solution.py:36
  486.3 119.4 %collective-permute-start.46 = (bf16[576,1728]{1,0:T(8,128)(2,1)}, bf16[576,1728]{1,0:T(8,128)(2,1)}, u32[]{:S(2)}, u32[]{:S(2)}) collective-permute-start(bf16[576,1728]{1,0:T(8,128)(2,1)} %dynamic-slice_bitcast_fusion), channel_id=1, source_target_pairs={{0,8},{8,0},{1,9},{9,1},{2,10},{10,2},{3,11},{11,3},{4,12},{12,4},... | collective-permute-start | bytes 5971976 | tf_op jit(solution)/shard_map/ppermute | solution.py:46
  506.8 223.1 %reduce-scatter.8.cloned.1.call-start = ((), (), s32[]{:S(2)}) async-start(), calls=%async_computation.7 | async-start | bytes 2580480 | tf_op jit(solution)/shard_map/reduce_scatter | solution.py:64
  610.5 122.7 %reduce-scatter.6.cloned.1.call-start = ((), (), s32[]{:S(2)}) async-start(), calls=%async_computation.6 | async-start | bytes 2580480 | tf_op jit(solution)/shard_map/reduce_scatter | solution.py:64
  626.8 23.3 %collective-permute-start.32 = (bf16[2048,768]{1,0:T(8,128)(2,1)}, bf16[2048,768]{1,0:T(8,128)(2,1)}, u32[]{:S(2)}, u32[]{:S(2)}) collective-permute-start(bf16[2048,768]{1,0:T(8,128)(2,1)} %bitcast.69), channel_id=1, source_target_pairs={{0,8},{8,0},{1,9},{9,1},{2,10},{10,2},{3,11},{11,3},{4,12},{12,4},... | collective-permute-start | bytes 9437192 | tf_op jit(solution)/shard_map/ppermute | solution.py:46
  655.6 20.7 %collective-permute-start.34 = (bf16[256,768]{1,0:T(8,128)(2,1)}, bf16[256,768]{1,0:T(8,128)(2,1)}, u32[]{:S(2)}, u32[]{:S(2)}) collective-permute-start(bf16[256,768]{1,0:T(8,128)(2,1)} %get-tuple-element.151), channel_id=1, source_target_pairs={{0,1},{1,0},{2,3},{3,2},{4,5},{5,4},{6,7},{7,6},{8,9},{9,8},{10,11... | collective-permute-start | bytes 1179656 | tf_op jit(solution)/shard_map/ppermute | solution.py:36
  658.5 27.2 %collective-permute-start.33 = (bf16[256,768]{1,0:T(8,128)(2,1)}, bf16[256,768]{1,0:T(8,128)(2,1)S(1)}, u32[]{:S(2)}, u32[]{:S(2)}) collective-permute-start(bf16[256,768]{1,0:T(8,128)(2,1)} %get-tuple-element.150), channel_id=1, source_target_pairs={{0,1},{1,0},{2,3},{3,2},{4,5},{5,4},{6,7},{7,6},{8,9},{9,8},{10,11... | collective-permute-start | bytes 1179656 | tf_op jit(solution)/shard_map/ppermute | solution.py:36
  659.1 26.6 %collective-permute-start.36 = (bf16[256,768]{1,0:T(8,128)(2,1)}, bf16[256,768]{1,0:T(8,128)(2,1)}, u32[]{:S(2)}, u32[]{:S(2)}) collective-permute-start(bf16[256,768]{1,0:T(8,128)(2,1)} %get-tuple-element.153), channel_id=1, source_target_pairs={{0,16},{16,0},{1,17},{17,1},{2,18},{18,2},{3,19},{19,3},{4,20},{20... | collective-permute-start | bytes 1179656 | tf_op jit(solution)/shard_map/ppermute | solution.py:36
  688.9 21.9 %collective-permute-start.39 = (bf16[128,768]{1,0:T(8,128)(2,1)S(1)}, bf16[128,768]{1,0:T(8,128)(2,1)S(1)}, u32[]{:S(2)}, u32[]{:S(2)}) collective-permute-start(bf16[128,768]{1,0:T(8,128)(2,1)S(1)} %get-tuple-element.180), channel_id=1, source_target_pairs={{0,6},{2,0},{4,2},{6,4},{1,7},{3,1},{5,3},{7,5},{8,14},{10,8},{12,... | collective-permute-start | bytes 589832 | tf_op jit(solution)/shard_map/ppermute | solution.py:43
  701.5 23.0 %collective-permute-start.40 = (bf16[128,768]{1,0:T(8,128)(2,1)S(1)}, bf16[128,768]{1,0:T(8,128)(2,1)S(1)}, u32[]{:S(2)}, u32[]{:S(2)}) collective-permute-start(bf16[128,768]{1,0:T(8,128)(2,1)S(1)} %get-tuple-element.182), channel_id=1, source_target_pairs={{0,4},{2,6},{4,0},{6,2},{1,5},{3,7},{5,1},{7,3},{8,12},{10,14},{12... | collective-permute-start | bytes 589832 | tf_op jit(solution)/shard_map/ppermute | solution.py:43
  702.1 22.4 %collective-permute-start.41 = (bf16[128,768]{1,0:T(8,128)(2,1)S(1)}, bf16[128,768]{1,0:T(8,128)(2,1)S(1)}, u32[]{:S(2)}, u32[]{:S(2)}) collective-permute-start(bf16[128,768]{1,0:T(8,128)(2,1)S(1)} %get-tuple-element.181), channel_id=1, source_target_pairs={{0,2},{2,4},{4,6},{6,0},{1,3},{3,5},{5,7},{7,1},{8,10},{10,12},{12... | collective-permute-start | bytes 589832 | tf_op jit(solution)/shard_map/ppermute | solution.py:43
  (184 other events, 1426.9 us)
Sparse Core Ops, SparseCore 0:
  66.0 47.1 all-gather.3
  125.0 81.7 all-gather.5
  208.4 44.7 all-gather.7
  506.9 63.0 reduce-scatter.9
  610.6 53.2 reduce-scatter.7
  666.2 49.6 reduce-scatter.5
